TPU v7x, 32 devices: a whole 2x2x4 slice. The times are simulated.
32 devices in a mesh: gx: 8 (over y, x, core), gy: 4 (over z).
Axes of the slice: x: 2, y: 2, z: 4, core: 2. Of those that a mesh axis runs over, the one named last changes fastest.
Arguments:
- tracers: float32 [2, 24, 64, 1024], P(None, None, 'gy', 'gx'), may hold values from -6 to 6
- uvel: float32 [24, 64, 1024], P(None, 'gy', 'gx'), may hold values from -6 to 6
- vvel: float32 [24, 64, 1024], P(None, 'gy', 'gx'), may hold values from -6 to 6
- sea_mask: int32 [64, 1024], P('gy', 'gx'), may hold values from 0 to 1, as said below
- levels: int32 [64, 1024], P('gy', 'gx'), may hold values from 1 to 24
- tracer_bar: float32 [2, 24, 64, 1024], P(None, None, 'gy', 'gx'), may hold values from -6 to 6
- eta_bar: float32 [64, 1024], P('gy', 'gx'), may hold values from -12 to 12
Outputs:
- tracer_adj: float32 [2, 24, 64, 1024], P(None, None, 'gy', 'gx')
- eta_adj: float32 [64, 1024], P('gy', 'gx')
Inputs may be any that keep to these rules, and one draw needn't show every extreme that they name: `sea_mask`: the first and the last latitude row are land.
All inputs are finite; a program needn't handle non-finite values.
Results may differ from a plain program's by a relative error of at most 0.0001.
Values sent between devices are 32-bit elements; how exact they have to be, the bound alone decides.
No kernel may reach another device: no remote copies, remote signals or barrier semaphores. Data moves between devices by JAX's collectives and lax.ppermute only.
A program may use at most 64 MiB of HBM per device.

v0:
```python
import jax
import jax.numpy as jnp
from jax import lax
from jax.sharding import PartitionSpec as P

ITERS = 3


advect_rate = 0.25
mix_floor = 0.2
mix_boost = 2.0
mix_slope = 2.0
mix_rate = 1.0
surface_stiffness = 2.0
thermal_steric = 0.5
haline_steric = 0.5


def with_halo(cells, sides, width):
    for axis, dim in sides:
        count = lax.axis_size(axis)
        head = lax.slice_in_dim(cells, 0, width, axis=dim)
        tail = lax.slice_in_dim(cells, cells.shape[dim] - width, cells.shape[dim], axis=dim)
        cells = jnp.concatenate(
            [
                lax.ppermute(tail, axis, [(i, (i + 1) % count) for i in range(count)]),
                cells,
                lax.ppermute(head, axis, [((i + 1) % count, i) for i in range(count)]),
            ],
            axis=dim,
        )
    return cells


def wet_cells(sea_mask, levels, count):
    layer = lax.broadcasted_iota(jnp.int32, (count,) + sea_mask.shape, 0)
    return jnp.where(layer < levels[None], sea_mask[None], 0).astype(jnp.float32)


def thomas_solve(kappa, right_side):
    count = right_side.shape[1]
    nothing = jnp.zeros_like(kappa[0])
    primes = []
    partial_values = []
    for layer_index in range(count):
        below = kappa[layer_index] if layer_index < count - 1 else nothing
        above = kappa[layer_index - 1] if layer_index > 0 else nothing
        diagonal_term = 1.0 + mix_rate * (above + below)
        if layer_index == 0:
            divisor = diagonal_term
            current = right_side[:, 0] / divisor
        else:
            divisor = diagonal_term + mix_rate * above * primes[-1]
            current = (right_side[:, layer_index] + mix_rate * above * partial_values[-1]) / divisor
        primes.append(-mix_rate * below / divisor)
        partial_values.append(current)
    results = [partial_values[-1]]
    for layer_index in range(count - 2, -1, -1):
        results.append(partial_values[layer_index] - primes[layer_index] * results[-1])
    return jnp.stack(results[::-1], axis=1)


def vertical_mix(advanced, wet):
    density = advanced[1] - advanced[0]
    kappa = (
        mix_floor + mix_boost * jax.nn.sigmoid(mix_slope * (density[:-1] - density[1:]))
    ) * wet[1:]
    return thomas_solve(kappa, advanced)


def column_adjoint(advanced, wet, mixed_bar):

    def forward(values):
        return vertical_mix(values, wet)

    unused, pull = jax.vjp(forward, advanced)
    return pull(mixed_bar)[0]


def face_flows(u_pad, v_pad, wet_pad):
    east_flow = u_pad[:, 1:-1, :-1] * wet_pad[:, 1:-1, :-1] * wet_pad[:, 1:-1, 1:]
    north_flow = v_pad[:, :-1, 1:-1] * wet_pad[:, :-1, 1:-1] * wet_pad[:, 1:, 1:-1]
    return (east_flow, north_flow)


def advance(tracer_pad, wet_pad, east_flow, north_flow):
    east_flux = east_flow[None] * 0.5 * (tracer_pad[:, :, 1:-1, :-1] + tracer_pad[:, :, 1:-1, 1:])
    north_flux = north_flow[None] * 0.5 * (tracer_pad[:, :, :-1, 1:-1] + tracer_pad[:, :, 1:, 1:-1])
    divergence = (
        east_flux[..., 1:] - east_flux[..., :-1] + north_flux[:, :, 1:] - north_flux[:, :, :-1]
    )
    return tracer_pad[:, :, 1:-1, 1:-1] - advect_rate * wet_pad[None, :, 1:-1, 1:-1] * divergence


def retreat(cotan_pad, east_flow, north_flow):
    east_part = east_flow[None] * (cotan_pad[:, :, 1:-1, :-1] - cotan_pad[:, :, 1:-1, 1:])
    north_part = north_flow[None] * (cotan_pad[:, :, :-1, 1:-1] - cotan_pad[:, :, 1:, 1:-1])
    return 0.5 * (
        east_part[..., 1:] + east_part[..., :-1] + north_part[:, :, 1:] + north_part[:, :, :-1]
    )


def surface_weights(depth_pad):
    east_weight = surface_stiffness * jnp.minimum(depth_pad[1:-1, :-1], depth_pad[1:-1, 1:])
    north_weight = surface_stiffness * jnp.minimum(depth_pad[:-1, 1:-1], depth_pad[1:, 1:-1])
    return (east_weight, north_weight)


def surface_apply(field, weights):
    padded = with_halo(field, (("gx", 1), ("gy", 0)), 1)
    east_flux = weights[0] * (padded[1:-1, :-1] - padded[1:-1, 1:])
    north_flux = weights[1] * (padded[:-1, 1:-1] - padded[1:, 1:-1])
    return field + east_flux[:, 1:] - east_flux[:, :-1] + north_flux[1:] - north_flux[:-1]


def paired_sums(residual, image):
    return lax.psum((jnp.sum(residual * residual), jnp.sum(residual * image)), ("gx", "gy"))


def surface_solve(target, weights):
    iterate = jnp.zeros_like(target)
    residual = target
    image = surface_apply(residual, weights)
    norm_now, product = paired_sums(residual, image)
    alpha = norm_now / product
    direction = residual
    carried = image
    for iteration in range(ITERS):
        iterate = iterate + alpha * direction
        residual = residual - alpha * carried
        if iteration < ITERS - 1:
            image = surface_apply(residual, weights)
            norm_next, product = paired_sums(residual, image)
            ratio = norm_next / norm_now
            alpha = norm_next / (product - ratio * norm_next / alpha)
            direction = residual + ratio * direction
            carried = image + ratio * carried
            norm_now = norm_next
    return iterate


def per_device(tracers, uvel, vvel, sea_mask, levels, tracer_bar, eta_bar):
    count = tracers.shape[1]
    wet = wet_cells(sea_mask, levels, count)
    steric = jnp.array([thermal_steric, -haline_steric], jnp.float32)[:, None, None, None]
    stacked = jnp.concatenate([tracers, uvel[None], vvel[None], wet[None]], axis=0)
    padded = with_halo(stacked, (("gx", 3), ("gy", 2)), 1)
    east_flow, north_flow = face_flows(padded[2], padded[3], padded[4])
    advanced = advance(padded[0:2], padded[4], east_flow, north_flow)
    depth_pad = jnp.sum(padded[4], axis=0) / count
    eta_adj = surface_solve(eta_bar, surface_weights(depth_pad))
    mixed_bar = tracer_bar + steric * wet[None] * eta_adj[None, None]
    advanced_bar = column_adjoint(advanced, wet, mixed_bar)
    cotangent = -advect_rate * wet[None] * advanced_bar
    cotan_pad = with_halo(cotangent, (("gx", 3), ("gy", 2)), 1)
    tracer_adj = advanced_bar + retreat(cotan_pad, east_flow, north_flow)
    return (tracer_adj, eta_adj)


def solution(mesh):
    return jax.shard_map(
        per_device,
        mesh=mesh,
        in_specs=(
            P(None, None, "gy", "gx"),
            P(None, "gy", "gx"),
            P(None, "gy", "gx"),
            P("gy", "gx"),
            P("gy", "gx"),
            P(None, None, "gy", "gx"),
            P("gy", "gx"),
        ),
        out_specs=(P(None, None, "gy", "gx"), P("gy", "gx")),
        check_vma=False,
    )
```

profile of v0, /device:TPU:0, one launch (start us, length us, event | category | flops | bytes accessed | tf_op | source)
XLA Modules:
  0.0 209.8 jit_solution(7855816345737204124)
XLA Ops:
  0.6 0.7 select_convert_fusion
  1.4 1.3 pad_maximum_fusion.1
  3.0 0.6 copy.79
  3.6 0.5 collective-permute-start
  4.1 0.6 copy.80
  4.7 2.9 %collective-permute-start.1 = (f32[5,24,16,1]{1,2,3,0:T(8,128)S(1)}, f32[5,24,16,1]{1,2,3,0:T(8,128)S(1)}, u32[]{:S(2)}, u32[]{:S(2)}) collective-permute-start(f32[5,24,16,1]{1,2,3,0:T(8,128)S(1)} %copy.80), channel_id=1, source_target_pairs={{4,0},{8,4},{12,8},{16,12},{20,16},{24,20},{28,24},{0,28},{5,1},{9... | collective-permute-start | bytes 23048 | tf_op jit(solution)/shard_map/ppermute | solution.py:28
  7.7 2.6 %collective-permute-start.5 = (f32[16,1]{1,0:T(8,128)S(1)}, f32[16,1]{1,0:T(8,128)S(1)}, u32[]{:S(2)}, u32[]{:S(2)}) collective-permute-start(f32[16,1]{1,0:T(8,128)S(1)} %get-tuple-element.407), channel_id=1, source_target_pairs={{4,0},{8,4},{12,8},{16,12},{20,16},{24,20},{28,24},{0,28},{5,1},{9... | collective-permute-start | bytes 200 | tf_op jit(solution)/shard_map/ppermute | solution.py:28
  10.3 0.7 select_convert_fusion.1
  11.0 0.7 broadcast_multiply_fusion.3
  11.7 0.6 copy.81
  12.3 0.6 copy.82
  12.9 0.8 pad_maximum_fusion.33
  13.7 2.4 %collective-permute-start.2 = (f32[5,24,1,130]{3,2,1,0:T(1,128)S(1)}, f32[5,24,1,130]{3,2,1,0:T(1,128)S(1)}, u32[]{:S(2)}, u32[]{:S(2)}) collective-permute-start(f32[5,24,1,130]{3,2,1,0:T(1,128)S(1)} %get-tuple-element.292), channel_id=1, source_target_pairs={{0,1},{1,2},{2,3},{3,0},{4,5},{5,6},{6,7},{7,4},{8,9},{9,10},{10,1... | collective-permute-start | bytes 187208 | tf_op jit(solution)/shard_map/ppermute | solution.py:26
  16.1 2.1 collective-permute-start.3
  18.3 3.8 %collective-permute-start.7 = (f32[1,130]{1,0:T(1,128)S(1)}, f32[1,130]{1,0:T(1,128)S(1)}, u32[]{:S(2)}, u32[]{:S(2)}) collective-permute-start(f32[1,130]{1,0:T(1,128)S(1)} %get-tuple-element.392), channel_id=1, source_target_pairs={{1,0},{2,1},{3,2},{0,3},{5,4},{6,5},{7,6},{4,7},{9,8},{10,9},{11,1... | collective-permute-start | bytes 1568 | tf_op jit(solution)/shard_map/ppermute | solution.py:28
  22.3 0.4 copy-done.11
  22.8 0.6 copy-done.13
  23.4 2.4 %pad_maximum_fusion = f32[5,24,18,130]{3,2,1,0:T(8,128)S(1)} fusion(f32[5,24,1,130]{3,2,1,0:T(1,128)S(1)} %collective-permute-done.3, f32[5,24,16,1]{3,2,1,0:T(8,128)S(1)} %copy.82, f32[1,24,16,128]{3,2,1,0:T(8,128)S(1)} %select_convert_fusion, f32[1,24,16,128]{3,2,1,0:T(8,128)S(1)} %bitcast.897, f32[1,24,16,128]{3,2,1,0:T(8,128)S(1)} %bitcast.902, ...), kind=kLoop, calls=%fused_computation | loop fusion | flops 1965600 | bytes 2246400 | tf_op jit(solution)/shard_map/concatenate | solution.py:24
  25.8 1.1 slice_reduce_fusion
  27.1 0.5 copy-done.5
  27.7 1.3 multiply_reduce_fusion.72
  29.0 39.0 %all-reduce.76 = (f32[]{:T(128)}, f32[]{:T(128)}) all-reduce(f32[]{:T(128)} %get-tuple-element.81, f32[]{:T(128)} %get-tuple-element.80), channel_id=1, replica_groups=mesh['gx'=8,'gy'=4] {'gx','gy'}, use_global_device_ids=true, to_apply=%region_1.2 | all-reduce | flops 2 | bytes 16 | tf_op jit(solution)/shard_map/psum | solution.py:117
  69.3 0.7 multiply_subtract_fusion.22
  70.2 2.1 broadcast_multiply_fusion.2
  72.3 2.0 broadcast_multiply_fusion.1
  76.1 2.7 %collective-permute-start.9 = (f32[16,1]{1,0:T(8,128)S(1)}, f32[16,1]{1,0:T(8,128)S(1)}, u32[]{:S(2)}, u32[]{:S(2)}) collective-permute-start(f32[16,1]{1,0:T(8,128)S(1)} %get-tuple-element.405), channel_id=1, source_target_pairs={{4,0},{8,4},{12,8},{16,12},{20,16},{24,20},{28,24},{0,28},{5,1},{9... | collective-permute-start | bytes 200 | tf_op jit(solution)/shard_map/ppermute | solution.py:28
  78.8 1.4 collective-permute-done.9
  80.2 1.5 collective-permute-start.10
  81.7 2.4 %collective-permute-start.11 = (f32[1,130]{1,0:T(1,128)S(1)}, f32[1,130]{1,0:T(1,128)S(1)}, u32[]{:S(2)}, u32[]{:S(2)}) collective-permute-start(f32[1,130]{1,0:T(1,128)S(1)} %get-tuple-element.390), channel_id=1, source_target_pairs={{1,0},{2,1},{3,2},{0,3},{5,4},{6,5},{7,6},{4,7},{9,8},{10,9},{11,1... | collective-permute-start | bytes 1568 | tf_op jit(solution)/shard_map/ppermute | solution.py:28
  84.2 1.5 collective-permute-done.10
  85.7 0.7 multiply_reduce_fusion.70
  86.5 40.4 %all-reduce.75 = (f32[]{:T(128)}, f32[]{:T(128)}) all-reduce(f32[]{:T(128)} %get-tuple-element.79, f32[]{:T(128)} %get-tuple-element.78), channel_id=1, replica_groups=mesh['gx'=8,'gy'=4] {'gx','gy'}, use_global_device_ids=true, to_apply=%region_6.7 | all-reduce | flops 2 | bytes 16 | tf_op jit(solution)/shard_map/psum | solution.py:117
  131.6 2.6 %collective-permute-start.13 = (f32[16,1]{1,0:T(8,128)S(1)}, f32[16,1]{1,0:T(8,128)S(1)}, u32[]{:S(2)}, u32[]{:S(2)}) collective-permute-start(f32[16,1]{1,0:T(8,128)S(1)} %get-tuple-element.403), channel_id=1, source_target_pairs={{4,0},{8,4},{12,8},{16,12},{20,16},{24,20},{28,24},{0,28},{5,1},{9... | collective-permute-start | bytes 200 | tf_op jit(solution)/shard_map/ppermute | solution.py:28
  134.3 1.3 collective-permute-done.12
  135.7 2.1 %collective-permute-start.14 = (f32[1,130]{1,0:T(1,128)S(1)}, f32[1,130]{1,0:T(1,128)S(1)}, u32[]{:S(2)}, u32[]{:S(2)}) collective-permute-start(f32[1,130]{1,0:T(1,128)S(1)} %get-tuple-element.387), channel_id=1, source_target_pairs={{0,1},{1,2},{2,3},{3,0},{4,5},{5,6},{6,7},{7,4},{8,9},{9,10},{10,1... | collective-permute-start | bytes 1568 | tf_op jit(solution)/shard_map/ppermute | solution.py:26
  137.8 1.7 collective-permute-start.15
  139.6 1.5 collective-permute-done.14
  141.5 0.7 fusion.60
  142.2 40.5 %all-reduce.74 = (f32[]{:T(128)}, f32[]{:T(128)}) all-reduce(f32[]{:T(128)} %get-tuple-element.77, f32[]{:T(128)} %get-tuple-element.76), channel_id=1, replica_groups=mesh['gx'=8,'gy'=4] {'gx','gy'}, use_global_device_ids=true, to_apply=%region_10.11 | all-reduce | flops 2 | bytes 16 | tf_op jit(solution)/shard_map/psum | solution.py:117
  189.6 2.6 %collective-permute-start.17 = (f32[2,24,16,1]{3,2,0,1:T(8,128)S(1)}, f32[2,24,16,1]{3,2,0,1:T(8,128)S(1)}, u32[]{:S(2)}, u32[]{:S(2)}) collective-permute-start(f32[2,24,16,1]{3,2,0,1:T(8,128)S(1)} %get-tuple-element.299), channel_id=1, source_target_pairs={{4,0},{8,4},{12,8},{16,12},{20,16},{24,20},{28,24},{0,28},{5,1},{9... | collective-permute-start | bytes 9224 | tf_op jit(solution)/shard_map/ppermute | solution.py:28
  192.3 6.8 %collective-permute-done.16 = f32[2,24,16,1]{3,2,0,1:T(8,128)S(1)} collective-permute-done((f32[2,24,16,1]{3,2,0,1:T(8,128)S(1)}, f32[2,24,16,1]{3,2,0,1:T(8,128)S(1)}, u32[]{:S(2)}, u32[]{:S(2)}) %collective-permute-start.16) | collective-permute-done | bytes 3104 | tf_op jit(solution)/shard_map/ppermute | solution.py:26
  199.1 1.8 collective-permute-done.17
  201.2 1.9 collective-permute-start.18
  203.1 2.0 collective-permute-start.19
  205.4 1.8 collective-permute-done.18
  207.2 1.2 collective-permute-done.19
  208.4 0.4 fusion.4
  209.1 0.8 copy.87
  (153 shorter events, 6.9 us)
Async XLA Ops:
  2.6 5.0 %copy-start.10 = (f32[16,128]{1,0:T(8,128)S(1)}, f32[16,128]{1,0:T(8,128)}, u32[]{:S(2)}) copy-start(f32[16,128]{1,0:T(8,128)} %param.14) | copy-start | bytes 24580
  2.6 7.7 %copy-start.19 = (s32[16,128]{1,0:T(8,128)S(1)}, s32[16,128]{1,0:T(8,128)}, u32[]{:S(2)}) copy-start(s32[16,128]{1,0:T(8,128)} %param.11) | copy-start | bytes 24580
  2.7 7.7 %copy-start.20 = (s32[16,128]{1,0:T(8,128)S(1)}, s32[16,128]{1,0:T(8,128)}, u32[]{:S(2)}) copy-start(s32[16,128]{1,0:T(8,128)} %param.12) | copy-start | bytes 24580
  3.0 9.9 %copy-start = (f32[2,24,16,128]{3,2,1,0:T(8,128)S(1)}, f32[2,24,16,128]{3,2,1,0:T(8,128)}, u32[]{:S(2)}) copy-start(f32[2,24,16,128]{3,2,1,0:T(8,128)} %param.8) | copy-start | bytes 1179652
  3.0 9.9 %copy-start.1 = (f32[24,16,128]{2,1,0:T(8,128)S(1)}, f32[24,16,128]{2,1,0:T(8,128)}, u32[]{:S(2)}) copy-start(f32[24,16,128]{2,1,0:T(8,128)} %param.10) | copy-start | bytes 589828
  3.0 9.9 %copy-start.2 = (f32[24,16,128]{2,1,0:T(8,128)S(1)}, f32[24,16,128]{2,1,0:T(8,128)}, u32[]{:S(2)}) copy-start(f32[24,16,128]{2,1,0:T(8,128)} %param.9) | copy-start | bytes 589828
  3.6 8.1 %collective-permute-start = (f32[5,24,16,1]{1,2,3,0:T(8,128)S(1)}, f32[5,24,16,1]{1,2,3,0:T(8,128)S(1)}, u32[]{:S(2)}, u32[]{:S(2)}) collective-permute-start(f32[5,24,16,1]{1,2,3,0:T(8,128)S(1)} %copy.79), channel_id=1, source_target_pairs={{0,4},{4,8},{8,12},{12,16},{16,20},{20,24},{24,28},{28,0},{1,5},{5... | collective-permute-start | bytes 23048 | tf_op jit(solution)/shard_map/ppermute | solution.py:26
  4.7 7.6 %collective-permute-start.1 = (f32[5,24,16,1]{1,2,3,0:T(8,128)S(1)}, f32[5,24,16,1]{1,2,3,0:T(8,128)S(1)}, u32[]{:S(2)}, u32[]{:S(2)}) collective-permute-start(f32[5,24,16,1]{1,2,3,0:T(8,128)S(1)} %copy.80), channel_id=1, source_target_pairs={{4,0},{8,4},{12,8},{16,12},{20,16},{24,20},{28,24},{0,28},{5,1},{9... | collective-permute-start | bytes 23048 | tf_op jit(solution)/shard_map/ppermute | solution.py:28
  7.7 10.5 %collective-permute-start.4 = (f32[16,1]{1,0:T(8,128)S(1)}, f32[16,1]{1,0:T(8,128)S(1)}, u32[]{:S(2)}, u32[]{:S(2)}) collective-permute-start(f32[16,1]{1,0:T(8,128)S(1)} %get-tuple-element.406), channel_id=1, source_target_pairs={{0,4},{4,8},{8,12},{12,16},{16,20},{20,24},{24,28},{28,0},{1,5},{5... | collective-permute-start | bytes 200 | tf_op jit(solution)/shard_map/ppermute | solution.py:26
  7.7 10.5 %collective-permute-start.5 = (f32[16,1]{1,0:T(8,128)S(1)}, f32[16,1]{1,0:T(8,128)S(1)}, u32[]{:S(2)}, u32[]{:S(2)}) collective-permute-start(f32[16,1]{1,0:T(8,128)S(1)} %get-tuple-element.407), channel_id=1, source_target_pairs={{4,0},{8,4},{12,8},{16,12},{20,16},{24,20},{28,24},{0,28},{5,1},{9... | collective-permute-start | bytes 200 | tf_op jit(solution)/shard_map/ppermute | solution.py:28
  13.7 8.4 %collective-permute-start.2 = (f32[5,24,1,130]{3,2,1,0:T(1,128)S(1)}, f32[5,24,1,130]{3,2,1,0:T(1,128)S(1)}, u32[]{:S(2)}, u32[]{:S(2)}) collective-permute-start(f32[5,24,1,130]{3,2,1,0:T(1,128)S(1)} %get-tuple-element.292), channel_id=1, source_target_pairs={{0,1},{1,2},{2,3},{3,0},{4,5},{5,6},{6,7},{7,4},{8,9},{9,10},{10,1... | collective-permute-start | bytes 187208 | tf_op jit(solution)/shard_map/ppermute | solution.py:26
  16.1 6.2 %collective-permute-start.3 = (f32[5,24,1,130]{3,2,1,0:T(1,128)S(1)}, f32[5,24,1,130]{3,2,1,0:T(1,128)S(1)}, u32[]{:S(2)}, u32[]{:S(2)}) collective-permute-start(f32[5,24,1,130]{3,2,1,0:T(1,128)S(1)} %get-tuple-element.293), channel_id=1, source_target_pairs={{1,0},{2,1},{3,2},{0,3},{5,4},{6,5},{7,6},{4,7},{9,8},{10,9},{11,1... | collective-permute-start | bytes 187208 | tf_op jit(solution)/shard_map/ppermute | solution.py:28
  18.2 4.1 %copy-start.17 = (f32[16,1]{1,0:T(8,128)}, f32[16,1]{1,0:T(8,128)S(1)}, u32[]{:S(2)}) copy-start(f32[16,1]{1,0:T(8,128)S(1)} %collective-permute-done.5) | copy-start | bytes 196
  18.3 8.8 %collective-permute-start.6 = (f32[1,130]{1,0:T(1,128)S(1)}, f32[1,130]{1,0:T(1,128)S(1)}, u32[]{:S(2)}, u32[]{:S(2)}) collective-permute-start(f32[1,130]{1,0:T(1,128)S(1)} %get-tuple-element.391), channel_id=1, source_target_pairs={{0,1},{1,2},{2,3},{3,0},{4,5},{5,6},{6,7},{7,4},{8,9},{9,10},{10,1... | collective-permute-start | bytes 1568 | tf_op jit(solution)/shard_map/ppermute | solution.py:26
  18.3 8.8 %collective-permute-start.7 = (f32[1,130]{1,0:T(1,128)S(1)}, f32[1,130]{1,0:T(1,128)S(1)}, u32[]{:S(2)}, u32[]{:S(2)}) collective-permute-start(f32[1,130]{1,0:T(1,128)S(1)} %get-tuple-element.392), channel_id=1, source_target_pairs={{1,0},{2,1},{3,2},{0,3},{5,4},{6,5},{7,6},{4,7},{9,8},{10,9},{11,1... | collective-permute-start | bytes 1568 | tf_op jit(solution)/shard_map/ppermute | solution.py:28
  22.1 0.6 copy-start.11
  22.8 0.6 copy-start.13
  25.8 1.1 copy-start.18
  27.0 0.6 copy-start.5
  70.1 8.7 %collective-permute-start.8 = (f32[16,1]{1,0:T(8,128)S(1)}, f32[16,1]{1,0:T(8,128)S(1)}, u32[]{:S(2)}, u32[]{:S(2)}) collective-permute-start(f32[16,1]{1,0:T(8,128)S(1)} %get-tuple-element.404), channel_id=1, source_target_pairs={{0,4},{4,8},{8,12},{12,16},{16,20},{20,24},{24,28},{28,0},{1,5},{5... | collective-permute-start | bytes 200 | tf_op jit(solution)/shard_map/ppermute | solution.py:26
  72.3 2.3 %copy-start.12 = (f32[5,24,1,130]{3,2,1,0:T(1,128)S(1)}, f32[5,24,1,130]{3,2,1,0:T(1,128)}, u32[]{:S(2)}) copy-start(f32[5,24,1,130]{3,2,1,0:T(1,128)} %copy-done.11) | copy-start | bytes 187204
  72.3 2.3 %copy-start.14 = (f32[5,24,1,130]{3,2,1,0:T(1,128)S(1)}, f32[5,24,1,130]{3,2,1,0:T(1,128)}, u32[]{:S(2)}) copy-start(f32[5,24,1,130]{3,2,1,0:T(1,128)} %copy-done.13) | copy-start | bytes 187204
  74.6 0.9 copy-start.3
  75.1 9.0 %copy-start.6 = (f32[18,130]{1,0:T(8,128)S(1)}, f32[18,130]{1,0:T(8,128)}, u32[]{:S(2)}) copy-start(f32[18,130]{1,0:T(8,128)} %copy-done.5) | copy-start | bytes 28084
  75.1 56.4 %copy-start.16 = (f32[16,128]{1,0:T(8,128)S(1)}, f32[16,128]{1,0:T(8,128)}, u32[]{:S(2)}) copy-start(f32[16,128]{1,0:T(8,128)} %get-tuple-element.283) | copy-start | bytes 24580
  75.1 111.8 %copy-start.4 = (f32[24,16,128]{2,1,0:T(8,128)S(1)}, f32[24,16,128]{2,1,0:T(8,128)}, u32[]{:S(2)}) copy-start(f32[24,16,128]{2,1,0:T(8,128)} %select_convert_fusion.1) | copy-start | bytes 589828
  75.1 111.8 %copy-start.15 = (f32[2,24,16,128]{3,2,1,0:T(8,128)S(1)}, f32[2,24,16,128]{3,2,1,0:T(8,128)}, u32[]{:S(2)}) copy-start(f32[2,24,16,128]{3,2,1,0:T(8,128)} %param.13) | copy-start | bytes 1179652
  75.1 111.8 %copy-start.22 = (f32[2]{0:T(128)S(1)}, f32[2]{0:T(128)}, u32[]{:S(2)}) copy-start(f32[2]{0:T(128)} %constant.6.clone) | copy-start | bytes 28
  76.1 4.1 %collective-permute-start.9 = (f32[16,1]{1,0:T(8,128)S(1)}, f32[16,1]{1,0:T(8,128)S(1)}, u32[]{:S(2)}, u32[]{:S(2)}) collective-permute-start(f32[16,1]{1,0:T(8,128)S(1)} %get-tuple-element.405), channel_id=1, source_target_pairs={{4,0},{8,4},{12,8},{16,12},{20,16},{24,20},{28,24},{0,28},{5,1},{9... | collective-permute-start | bytes 200 | tf_op jit(solution)/shard_map/ppermute | solution.py:28
  80.2 5.4 %collective-permute-start.10 = (f32[1,130]{1,0:T(1,128)S(1)}, f32[1,130]{1,0:T(1,128)S(1)}, u32[]{:S(2)}, u32[]{:S(2)}) collective-permute-start(f32[1,130]{1,0:T(1,128)S(1)} %get-tuple-element.389), channel_id=1, source_target_pairs={{0,1},{1,2},{2,3},{3,0},{4,5},{5,6},{6,7},{7,4},{8,9},{9,10},{10,1... | collective-permute-start | bytes 1568 | tf_op jit(solution)/shard_map/ppermute | solution.py:26
  81.7 3.9 %collective-permute-start.11 = (f32[1,130]{1,0:T(1,128)S(1)}, f32[1,130]{1,0:T(1,128)S(1)}, u32[]{:S(2)}, u32[]{:S(2)}) collective-permute-start(f32[1,130]{1,0:T(1,128)S(1)} %get-tuple-element.390), channel_id=1, source_target_pairs={{1,0},{2,1},{3,2},{0,3},{5,4},{6,5},{7,6},{4,7},{9,8},{10,9},{11,1... | collective-permute-start | bytes 1568 | tf_op jit(solution)/shard_map/ppermute | solution.py:28
  131.6 4.0 %collective-permute-start.12 = (f32[16,1]{1,0:T(8,128)S(1)}, f32[16,1]{1,0:T(8,128)S(1)}, u32[]{:S(2)}, u32[]{:S(2)}) collective-permute-start(f32[16,1]{1,0:T(8,128)S(1)} %get-tuple-element.402), channel_id=1, source_target_pairs={{0,4},{4,8},{8,12},{12,16},{16,20},{20,24},{24,28},{28,0},{1,5},{5... | collective-permute-start | bytes 200 | tf_op jit(solution)/shard_map/ppermute | solution.py:26
  131.6 4.0 %collective-permute-start.13 = (f32[16,1]{1,0:T(8,128)S(1)}, f32[16,1]{1,0:T(8,128)S(1)}, u32[]{:S(2)}, u32[]{:S(2)}) collective-permute-start(f32[16,1]{1,0:T(8,128)S(1)} %get-tuple-element.403), channel_id=1, source_target_pairs={{4,0},{8,4},{12,8},{16,12},{20,16},{24,20},{28,24},{0,28},{5,1},{9... | collective-permute-start | bytes 200 | tf_op jit(solution)/shard_map/ppermute | solution.py:28
  135.7 5.4 %collective-permute-start.14 = (f32[1,130]{1,0:T(1,128)S(1)}, f32[1,130]{1,0:T(1,128)S(1)}, u32[]{:S(2)}, u32[]{:S(2)}) collective-permute-start(f32[1,130]{1,0:T(1,128)S(1)} %get-tuple-element.387), channel_id=1, source_target_pairs={{0,1},{1,2},{2,3},{3,0},{4,5},{5,6},{6,7},{7,4},{8,9},{9,10},{10,1... | collective-permute-start | bytes 1568 | tf_op jit(solution)/shard_map/ppermute | solution.py:26
  137.8 3.6 %collective-permute-start.15 = (f32[1,130]{1,0:T(1,128)S(1)}, f32[1,130]{1,0:T(1,128)S(1)}, u32[]{:S(2)}, u32[]{:S(2)}) collective-permute-start(f32[1,130]{1,0:T(1,128)S(1)} %get-tuple-element.388), channel_id=1, source_target_pairs={{1,0},{2,1},{3,2},{0,3},{5,4},{6,5},{7,6},{4,7},{9,8},{10,9},{11,1... | collective-permute-start | bytes 1568 | tf_op jit(solution)/shard_map/ppermute | solution.py:28
  186.9 0.7 copy-start.21
  188.2 1.1 copy-start.9
  189.1 16.0 %copy-start.7 = (f32[24,16,129]{2,1,0:T(8,128)S(1)}, f32[24,16,129]{2,1,0:T(8,128)}, u32[]{:S(2)}) copy-start(f32[24,16,129]{2,1,0:T(8,128)} %get-tuple-element.285) | copy-start | bytes 594436
  189.4 19.1 %copy-start.8 = (f32[24,17,128]{2,1,0:T(8,128)S(1)}, f32[24,17,128]{2,1,0:T(8,128)}, u32[]{:S(2)}) copy-start(f32[24,17,128]{2,1,0:T(8,128)} %get-tuple-element.287) | copy-start | bytes 626692
  189.6 9.5 %collective-permute-start.16 = (f32[2,24,16,1]{3,2,0,1:T(8,128)S(1)}, f32[2,24,16,1]{3,2,0,1:T(8,128)S(1)}, u32[]{:S(2)}, u32[]{:S(2)}) collective-permute-start(f32[2,24,16,1]{3,2,0,1:T(8,128)S(1)} %get-tuple-element.298), channel_id=1, source_target_pairs={{0,4},{4,8},{8,12},{12,16},{16,20},{20,24},{24,28},{28,0},{1,5},{5... | collective-permute-start | bytes 9224 | tf_op jit(solution)/shard_map/ppermute | solution.py:26
  189.6 11.2 %collective-permute-start.17 = (f32[2,24,16,1]{3,2,0,1:T(8,128)S(1)}, f32[2,24,16,1]{3,2,0,1:T(8,128)S(1)}, u32[]{:S(2)}, u32[]{:S(2)}) collective-permute-start(f32[2,24,16,1]{3,2,0,1:T(8,128)S(1)} %get-tuple-element.299), channel_id=1, source_target_pairs={{4,0},{8,4},{12,8},{16,12},{20,16},{24,20},{28,24},{0,28},{5,1},{9... | collective-permute-start | bytes 9224 | tf_op jit(solution)/shard_map/ppermute | solution.py:28
  201.2 6.0 %collective-permute-start.18 = (f32[2,24,1,130]{3,2,0,1:T(1,128)S(1)}, f32[2,24,1,130]{3,2,0,1:T(1,128)S(1)}, u32[]{:S(2)}, u32[]{:S(2)}) collective-permute-start(f32[2,24,1,130]{3,2,0,1:T(1,128)S(1)} %get-tuple-element.294), channel_id=1, source_target_pairs={{0,1},{1,2},{2,3},{3,0},{4,5},{5,6},{6,7},{7,4},{8,9},{9,10},{10,1... | collective-permute-start | bytes 74888 | tf_op jit(solution)/shard_map/ppermute | solution.py:26
  203.1 5.3 %collective-permute-start.19 = (f32[2,24,1,130]{3,2,0,1:T(1,128)S(1)}, f32[2,24,1,130]{3,2,0,1:T(1,128)S(1)}, u32[]{:S(2)}, u32[]{:S(2)}) collective-permute-start(f32[2,24,1,130]{3,2,0,1:T(1,128)S(1)} %get-tuple-element.295), channel_id=1, source_target_pairs={{1,0},{2,1},{3,2},{0,3},{5,4},{6,5},{7,6},{4,7},{9,8},{10,9},{11,1... | collective-permute-start | bytes 74888 | tf_op jit(solution)/shard_map/ppermute | solution.py:28
where the time goes:
time: 211 us; the launch traced here: 210 us
  blocking collectives  120 us (57%)
  starting transfers between devices  33.9 us (16%)
  other arithmetic  21 us (10%)
  waiting for transfers between devices  17.8 us (8%)
  between operations  11.5 us (5%)
  local copies, waits for them, and re-layouts  5.63 us (3%)
    psum x3, blocking collectives, paired_sums(): lax.psum((jnp.sum(residual * residual), jnp.sum(residual * image)), ('gx'...  120 us
    ppermute x10, starting transfers between devices, with_halo(): lax.ppermute(head, axis, [((i + 1) % count, i) for i in range(count)])  25.4 us
    ppermute x10, waiting for transfers between devices, with_halo(): lax.ppermute(tail, axis, [(i, (i + 1) % count) for i in range(count)])  12.9 us
    ppermute x10, starting transfers between devices, with_halo(): lax.ppermute(tail, axis, [(i, (i + 1) % count) for i in range(count)])  8.47 us
    ppermute x10, waiting for transfers between devices, with_halo(): lax.ppermute(head, axis, [((i + 1) % count, i) for i in range(count)])  4.93 us
  transfers between devices with their start and end apart: 20, of which 10 were waited for; matrix products, arithmetic and copies ran while one was open for 7% of the time, Pallas kernels for 0%

commit v1 on v0

v1 whole, which is shorter than its diff:
```python
import functools

import jax
import jax.numpy as jnp
from jax import lax
from jax.experimental import pallas as pl
from jax.experimental.pallas import tpu as pltpu
from jax.sharding import PartitionSpec as P

advect_rate = 0.25
mix_floor = 0.2
mix_boost = 2.0
mix_slope = 2.0
mix_rate = 1.0
surface_stiffness = 2.0
thermal_steric = 0.5
haline_steric = 0.5
sterics = (thermal_steric, -haline_steric)
spread = 4.0 * surface_stiffness
F32 = jnp.float32
VMEM = pl.BlockSpec(memory_space=pltpu.VMEM)


def lanes_of(shape):
    return lax.broadcasted_iota(jnp.int32, shape, 1)


def rows_of(shape):
    return lax.broadcasted_iota(jnp.int32, shape, 0)


def roll(cells, shift, axis):
    size = cells.shape[axis]
    shift = shift % size
    return cells if shift == 0 else pltpu.roll(cells, shift, axis)


def wet_depth(mask_ref, levels_ref):
    return (mask_ref[...] * levels_ref[...]).astype(F32)


def pack_columns(mask_ref, levels_ref, eta_ref, tracer_ref, u_ref, east_ref, west_ref):
    count = u_ref.shape[0]
    level = wet_depth(mask_ref, levels_ref)
    lane = lanes_of(level.shape)
    width = level.shape[1]
    east = jnp.zeros_like(level)
    west = jnp.zeros_like(level)
    for k in range(count):
        fields = (tracer_ref[0, k], tracer_ref[1, k], jnp.where(level > k, u_ref[k], 0.0))
        for f, field in enumerate(fields):
            at = f * count + k
            turned = roll(field, at + 1, 1)
            east = jnp.where(lane == at, turned, east)
            if f < 2:
                west = jnp.where(lane == at + 1, turned, west)
    east_ref[0] = east
    west_ref[0] = west
    eta = eta_ref[...]
    east_ref[1] = jnp.where(lane >= width - 3, eta, roll(level, -3, 1))
    west_ref[1] = jnp.where(lane < 3, eta, roll(level, 3, 1))


def pack_rows(mask_ref, levels_ref, tracer_ref, v_ref, north_ref, south_ref):
    count, height, _ = v_ref.shape
    level = wet_depth(mask_ref, levels_ref)
    for f in range(2):
        north_ref[f * count : (f + 1) * count, :] = tracer_ref[f, :, height - 1, :]
        south_ref[f * count : (f + 1) * count, :] = tracer_ref[f, :, 0, :]
    last = v_ref[:, height - 1, :]
    north_ref[2 * count :, :] = jnp.where(rows_of(last.shape).astype(F32) < level[height - 1 :, :], last, 0.0)


def side_tiles(from_west, from_east):
    lane = lanes_of(from_west.shape)
    first = lane < from_west.shape[1] // 2
    both = jnp.where(first, from_east, from_west)
    return both, jnp.where(first, roll(both, -3, 1), roll(both, 3, 1))


def join_rows(mask_ref, levels_ref, eta_ref, west_ref, east_ref, north_in, south_in, north_ref, south_ref):
    level = wet_depth(mask_ref, levels_ref)
    eta_side, level_side = side_tiles(west_ref[1], east_ref[1])
    tiles = (eta_ref[...], eta_side, level, level_side)
    height = level.shape[0]
    start = north_in.shape[0]
    north_ref[:start, :] = north_in[...]
    for index, tile in enumerate(tiles):
        north_ref[start + 8 * index : start + 8 * index + 8, :] = tile[height - 8 :, :]
    start = south_in.shape[0]
    south_ref[:start, :] = south_in[...]
    for index, tile in enumerate(tiles):
        south_ref[start + 8 * index : start + 8 * index + 8, :] = tile[:8, :]


def surface_basis(eta_ext, level_ext, count, block):
    height, width = block
    depth = level_ext / count
    east_weight = (surface_stiffness / spread) * jnp.minimum(depth, roll(depth, -1, 1))
    north_weight = (surface_stiffness / spread) * jnp.minimum(depth, roll(depth, -1, 0))

    def scaled(field):
        east_flux = east_weight * (field - roll(field, -1, 1))
        north_flux = north_weight * (field - roll(field, -1, 0))
        return (east_flux - roll(east_flux, 1, 1)) + (north_flux - roll(north_flux, 1, 0))

    first = scaled(eta_ext)
    second = scaled(first) - first
    third = scaled(second)
    vectors = [x[:height, :width] for x in (eta_ext, first, second, third)]
    pairs = ((0, 0), (0, 1), (0, 2), (1, 1), (1, 2), (2, 2), (2, 3))
    lane = lanes_of((1, width))
    line = jnp.zeros((1, width), F32)
    for index, (a, b) in enumerate(pairs):
        product = jnp.sum(vectors[a] * vectors[b], axis=0, keepdims=True)
        line = jnp.where(lane == index, jnp.sum(product, axis=1, keepdims=True), line)
    return first, second, line


def galerkin(sums):
    d00, d01, d02, d11, d12, d22, d2q = [sums[:, i : i + 1] for i in range(7)]
    k00 = d00 + spread * d01
    k01 = d01 + spread * d11
    k02 = d02 + spread * d12
    k11 = d11 + spread * (d11 + d12)
    k12 = d12 + spread * (d12 + d22)
    k22 = d22 + spread * d2q
    i00 = 1.0 / k00
    s11 = k11 - k01 * k01 * i00
    s12 = k12 - k01 * k02 * i00
    s22 = k22 - k02 * k02 * i00
    g1 = spread * (d01 * d01 - d00 * d11) * i00
    g2 = spread * (d02 * d01 - d00 * d12) * i00
    i11 = 1.0 / s11
    c12 = s12 * i11
    last = s22 - s12 * c12
    y2 = jnp.where(last > 4e-7 * s22, (g2 - g1 * c12) / last, 0.0)
    y1 = (g1 - s12 * y2) * i11
    y0 = (d00 - k01 * y1 - k02 * y2) * i00
    return y0, y1, y2


def shifted_depths(level, level_ext):
    height, width = level.shape
    east = jnp.minimum(level_ext, roll(level_ext, -1, 1))[:height, :width]
    north = jnp.minimum(level_ext, roll(level_ext, -1, 0))[:height, :width]
    return east, north


def extended(own, side, north_msg, south_msg, start_north, start_south, slot):
    upper = [north_msg[start_north + 8 * s : start_north + 8 * s + 8, :] for s in (slot, slot + 1)]
    lower = [south_msg[start_south + 8 * s : start_south + 8 * s + 8, :] for s in (slot, slot + 1)]
    left = jnp.concatenate([own, upper[0], lower[0]], axis=0)
    right = jnp.concatenate([side, upper[1], lower[1]], axis=0)
    return jnp.concatenate([left, right], axis=1)


def west_flow(msg, level, count):
    lane = lanes_of(msg.shape)
    flow = jnp.where(lane < count, roll(msg, -2 * count, 1), roll(msg, -count, 1))
    layer = (lane % count).astype(F32)
    return jnp.where(layer < level[:, :1], flow, 0.0)


def south_flow(msg, level, count):
    flow = msg[2 * count : 3 * count, :]
    flow = jnp.where(rows_of(flow.shape).astype(F32) < level[:1, :], flow, 0.0)
    return jnp.concatenate([flow, flow], axis=0)


def column_kernel(
    mask_ref, levels_ref, eta_ref, tracer_ref, u_ref, v_ref, bar_ref,
    west_ref, east_ref, own_west_ref, north_ref, south_ref, own_south_ref,
    adjoint_ref, east_out, west_out, north_out, south_out, level_out, basis_out, sums_out,
    ratio_ref, slope_ref, value_ref,
):
    count, height, width = u_ref.shape
    level = wet_depth(mask_ref, levels_ref)
    eta_side, level_side = side_tiles(west_ref[1], east_ref[1])
    starts = (2 * count, 3 * count)
    eta_ext = extended(eta_ref[...], eta_side, north_ref, south_ref, *starts, 0)
    level_ext = extended(level, level_side, north_ref, south_ref, *starts, 2)
    first, second, line = surface_basis(eta_ext, level_ext, count, (height, width))
    basis_out[0] = eta_ext
    basis_out[1] = first
    basis_out[2] = second
    level_out[...] = level_ext
    sums_out[...] = jnp.broadcast_to(line, sums_out.shape)

    east_depth, north_depth = shifted_depths(level, level_ext)
    lane = lanes_of((height, width))
    row = rows_of((height, width))
    from_west, from_east = west_ref[0], east_ref[0]
    west_flux = 0.5 * west_flow(from_west, level, count) * (from_west + roll(own_west_ref[0], -1, 1))
    south_flux = (
        0.5
        * south_flow(south_ref, level, count)
        * (south_ref[: 2 * count, :] + own_south_ref[...])
    )

    def advected(k):
        east_flow = jnp.where(east_depth > k, 0.5 * u_ref[k], 0.0)
        north_flow = jnp.where(north_depth > k, 0.5 * v_ref[k], 0.0)
        wet_rate = jnp.where(level > k, advect_rate, 0.0)
        result = []
        for f in range(2):
            at = f * count + k
            c = tracer_ref[f, k]
            c_east = jnp.where(lane == width - 1, roll(from_east, width - 2 - at, 1), roll(c, -1, 1))
            c_north = jnp.where(row == height - 1, north_ref[at : at + 1, :], roll(c, -1, 0))
            flux_e = east_flow * (c + c_east)
            flux_n = north_flow * (c + c_north)
            flux_w = jnp.where(lane == 0, roll(west_flux, -at, 1), roll(flux_e, 1, 1))
            flux_s = jnp.where(row == 0, south_flux[at : at + 1, :], roll(flux_n, 1, 0))
            result.append(c - wet_rate * ((flux_e - flux_w) + (flux_n - flux_s)))
        return result

    now = advected(0)
    kappa_up = None
    ratio_up = None
    values = None
    for k in range(count):
        if k < count - 1:
            later = advected(k + 1)
            step = (now[1] - now[0]) - (later[1] - later[0])
            gate = jax.nn.sigmoid(mix_slope * step)
            wet_below = level > k + 1
            kappa = jnp.where(wet_below, mix_floor + mix_boost * gate, 0.0)
            slope_ref[k] = jnp.where(wet_below, (mix_boost * mix_slope) * gate * (1.0 - gate), 0.0)
            diagonal = 1.0 + mix_rate * kappa
        else:
            later = None
            kappa = None
            diagonal = 1.0
        if k > 0:
            diagonal = diagonal + mix_rate * kappa_up * (1.0 - ratio_up)
        inverse = 1.0 / diagonal
        sides = [now[0], now[1], bar_ref[0, k], bar_ref[1, k]]
        if k > 0:
            sides = [side + mix_rate * kappa_up * value for side, value in zip(sides, values)]
        values = [side * inverse for side in sides]
        for f in range(4):
            value_ref[f, k] = values[f]
        if kappa is not None:
            ratio = mix_rate * kappa * inverse
            ratio_ref[k] = ratio
            kappa_up, ratio_up = kappa, ratio
        now = later

    east_pack = jnp.zeros((height, width), F32)
    west_pack = jnp.zeros((height, width), F32)
    pull_below = None
    below = values
    for k in range(count - 2, -1, -1):
        ratio = ratio_ref[k]
        here = [value_ref[f, k] + ratio * below[f] for f in range(4)]
        pull = (-mix_rate) * slope_ref[k] * (
            (here[2] - below[2]) * (here[0] - below[0]) + (here[3] - below[3]) * (here[1] - below[1])
        )
        emit(adjoint_ref, k + 1, below, pull_below, pull)
        below, pull_below = here, pull
    emit(adjoint_ref, 0, below, pull_below, None)

    for f in range(2):
        for k in range(count):
            at = f * count + k
            turned = roll(adjoint_ref[f, k], at + 1, 1)
            east_pack = jnp.where(lane == at, turned, east_pack)
            west_pack = jnp.where(lane == at + 1, turned, west_pack)
        north_out[f * count : (f + 1) * count, :] = adjoint_ref[f, :, height - 1, :]
        south_out[f * count : (f + 1) * count, :] = adjoint_ref[f, :, 0, :]
    east_out[...] = east_pack
    west_out[...] = west_pack


def emit(adjoint_ref, k, values, pull_here, pull_above):
    if pull_here is None:
        change = -pull_above if pull_above is not None else 0.0
    elif pull_above is None:
        change = pull_here
    else:
        change = pull_here - pull_above
    adjoint_ref[0, k] = values[2] - change
    adjoint_ref[1, k] = values[3] + change


def final_kernel(
    sums_ref, basis_ref, level_ref, u_ref, v_ref, adjoint_ref,
    west_ref, south_ref, from_west_ref, from_east_ref, own_west_ref, from_north_ref, from_south_ref, own_south_ref,
    tracer_out, eta_out,
):
    count, height, width = u_ref.shape
    sums = jnp.sum(sums_ref[...], axis=0, keepdims=True)
    y0, y1, y2 = galerkin(sums)
    eta_ext = y0 * basis_ref[0] + (y1 * basis_ref[1] + y2 * basis_ref[2])
    level_ext = level_ref[...]
    eta = eta_ext[:height, :width]
    level = level_ext[:height, :width]
    eta_out[...] = eta
    east_depth, north_depth = shifted_depths(level, level_ext)
    lane = lanes_of((height, width))
    row = rows_of((height, width))

    def lane_values(tile, offset, column):
        place = lane - offset
        layer = (place % count).astype(F32)
        steric = jnp.where(place < count, sterics[0], sterics[1])
        depth = level_ext[:height, column : column + 1]
        return tile + jnp.where(layer < depth, steric * eta_ext[:height, column : column + 1], 0.0)

    def row_values(tile, line):
        at = rows_of(tile.shape)
        layer = (at % count).astype(F32)
        steric = jnp.where(at < count, sterics[0], sterics[1])
        depth = level_ext[line : line + 1, :width]
        return tile + jnp.where(layer < depth, steric * eta_ext[line : line + 1, :width], 0.0)

    last_lane = level_ext.shape[1] - 1
    last_row = level_ext.shape[0] - 1
    east_values = lane_values(from_east_ref[...], 1, width)
    west_values = lane_values(from_west_ref[...], 0, last_lane)
    first_values = lane_values(roll(own_west_ref[...], -1, 1), 0, 0)
    west_part = west_flow(west_ref[0], level, count) * (west_values - first_values)
    north_values = row_values(from_north_ref[...], height)
    south_values = row_values(from_south_ref[...], last_row)
    bottom_values = row_values(own_south_ref[...], 0)
    south_part = south_flow(south_ref, level, count) * (south_values - bottom_values)
    for k in range(count):
        east_flow = jnp.where(east_depth > k, u_ref[k], 0.0)
        north_flow = jnp.where(north_depth > k, v_ref[k], 0.0)
        wet_eta = jnp.where(level > k, eta, 0.0)
        for f in range(2):
            at = f * count + k
            y = adjoint_ref[f, k] + sterics[f] * wet_eta
            y_east = jnp.where(lane == width - 1, roll(east_values, width - 2 - at, 1), roll(y, -1, 1))
            y_north = jnp.where(row == height - 1, north_values[at : at + 1, :], roll(y, -1, 0))
            part_e = east_flow * (y - y_east)
            part_n = north_flow * (y - y_north)
            part_w = jnp.where(lane == 0, roll(west_part, -at, 1), roll(part_e, 1, 1))
            part_s = jnp.where(row == 0, south_part[at : at + 1, :], roll(part_n, 1, 0))
            tracer_out[f, k] = y - (0.5 * advect_rate) * ((part_e + part_w) + (part_n + part_s))


def call(kernel, outs, name, scratch=()):
    return pl.pallas_call(
        kernel,
        out_shape=[jax.ShapeDtypeStruct(shape, F32) for shape in outs],
        out_specs=[VMEM] * len(outs),
        scratch_shapes=list(scratch),
        name=name,
    )


def around(axis, cells, step, wrap):
    count = lax.axis_size(axis)
    pairs = [(i, (i + step) % count) for i in range(count)]
    if not wrap:
        pairs = [(i, j) for i, j in pairs if j == i + step]
    return lax.ppermute(cells, axis, pairs)


def per_device(tracers, uvel, vvel, sea_mask, levels, tracer_bar, eta_bar):
    _, count, height, width = tracers.shape
    devices = lax.axis_size("gx") * lax.axis_size("gy")
    tile = (height, width)
    surface = (sea_mask, levels, eta_bar)
    to_east, to_west = call(pack_columns, [(2,) + tile] * 2, "pack_columns")(*surface, tracers, uvel)
    from_west = around("gx", to_east, 1, True)
    from_east = around("gx", to_west, -1, True)
    rows_north, rows_south = call(pack_rows, [(3 * count, width), (2 * count, width)], "pack_rows")(
        sea_mask, levels, tracers, vvel
    )
    to_north, to_south = call(join_rows, [(3 * count + 32, width), (2 * count + 32, width)], "join_rows")(
        *surface, from_west, from_east, rows_north, rows_south
    )
    from_south = around("gy", to_north, 1, False)
    from_north = around("gy", to_south, -1, False)
    ext = (height + 16, 2 * width)
    adjoint, east2, west2, north2, south2, level_ext, basis, sums = call(
        column_kernel,
        [(2, count) + tile, tile, tile, (2 * count, width), (2 * count, width), ext, (3,) + ext, (devices, width)],
        "columns",
        [pltpu.VMEM((count,) + tile, F32), pltpu.VMEM((count,) + tile, F32), pltpu.VMEM((4, count) + tile, F32)],
    )(*surface, tracers, uvel, vvel, tracer_bar, from_west, from_east, to_west, from_north, from_south, rows_south)
    from_west2 = around("gx", east2, 1, True)
    from_east2 = around("gx", west2, -1, True)
    from_south2 = around("gy", north2, 1, False)
    from_north2 = around("gy", south2, -1, False)
    all_sums = lax.all_to_all(sums.reshape(devices, 1, width), ("gx", "gy"), 0, 0).reshape(devices, width)
    tracer_adj, eta_adj = call(final_kernel, [tracers.shape, tile], "retreat")(
        all_sums, basis, level_ext, uvel, vvel, adjoint,
        from_west, from_south, from_west2, from_east2, west2, from_north2, from_south2, south2,
    )
    return (tracer_adj, eta_adj)


def solution(mesh):
    return jax.shard_map(
        per_device,
        mesh=mesh,
        in_specs=(
            P(None, None, "gy", "gx"),
            P(None, "gy", "gx"),
            P(None, "gy", "gx"),
            P("gy", "gx"),
            P("gy", "gx"),
            P(None, None, "gy", "gx"),
            P("gy", "gx"),
        ),
        out_specs=(P(None, None, "gy", "gx"), P("gy", "gx")),
        check_vma=False,
    )
```

time: 211 us -> 43.9 us (0.21)
  the two profiles are of different devices: /device:TPU:0 before, /device:TPU:11 now
where the time goes in v1:
time: 43.9 us; the launch traced here: 43.5 us
  starting transfers between devices  18.9 us (43%)
  Pallas kernels  12 us (27%)
  waiting for transfers between devices  9.38 us (21%)
  local copies, waits for them, and re-layouts  2.44 us (6%)
  between operations  0.76 us (2%)
    ppermute x8, starting transfers between devices, around(): return lax.ppermute(cells, axis, pairs)  14.4 us
    ppermute x8, waiting for transfers between devices, around(): return lax.ppermute(cells, axis, pairs)  9.38 us
    all_to_all x1, starting transfers between devices, per_device(): lax.all_to_all(sums.reshape(devices, 1, width), ('gx', 'gy'), 0, 0)  4.5 us
    pallas_call x1, Pallas kernels, per_device(): call(column_kernel, [(2, count) + tile, tile, tile, (2 * count, width), (...  3.53 us
    pallas_call x1, Pallas kernels, per_device(): call(final_kernel, [tracers.shape, tile], 'retreat')  3.29 us
    unnamed x24, local copies, waits for them, and re-layouts  2.44 us
    pallas_call x1, Pallas kernels, per_device(): call(pack_columns, [(2,) + tile] * 2, 'pack_columns')  1.93 us
    pallas_call x1, Pallas kernels, per_device(): call(pack_rows, [(3 * count, width), (2 * count, width)], 'pack_rows')  1.74 us
  transfers between devices with their start and end apart: 9, of which 4 were waited for; matrix products, arithmetic and copies ran while one was open for 0% of the time, Pallas kernels for 4%

profile of v1, /device:TPU:11, one launch (start us, length us, event | category | flops | bytes accessed | tf_op | source)
XLA Modules:
  0.0 43.5 jit_solution(12704635672873316115)
XLA Ops:
  0.6 1.9 %pack_columns.1 = (f32[2,16,128]{2,1,0:T(8,128)}, f32[2,16,128]{2,1,0:T(8,128)}) custom-call(s32[16,128]{1,0:T(8,128)} %mask_ref.7, s32[16,128]{1,0:T(8,128)} %levels_ref.7, f32[16,128]{1,0:T(8,128)} %eta_ref.5, f32[2,24,16,128]{3,2,1,0:T(8,128)} %tracer_ref.5, f32[24,16,128]{2,1,0:T(8,128)} %u_ref.5), custom_call_target="tpu_custom_call" | custom-call | tf_op jit(solution)/shard_map/pack_columns/pallas_call | solution.py:367
  2.6 1.8 %collective-permute-start = (f32[2,16,128]{2,1,0:T(8,128)}, f32[2,16,128]{2,1,0:T(8,128)S(1)}, u32[]{:S(2)}, u32[]{:S(2)}) collective-permute-start(f32[2,16,128]{2,1,0:T(8,128)} %get-tuple-element.16), channel_id=1, source_target_pairs={{0,4},{4,8},{8,12},{12,16},{16,20},{20,24},{24,28},{28,0},{1,5},{5... | collective-permute-start | bytes 49160 | tf_op jit(solution)/shard_map/ppermute | solution.py:359
  4.3 0.0 collective-permute-start.1
  4.3 1.7 %pack_rows.1 = (f32[72,128]{1,0:T(8,128)}, f32[48,128]{1,0:T(8,128)}) custom-call(s32[16,128]{1,0:T(8,128)} %mask_ref.7, s32[16,128]{1,0:T(8,128)} %levels_ref.7, f32[2,24,16,128]{3,2,1,0:T(8,128)} %tracer_ref.5, f32[24,16,128]{2,1,0:T(8,128)} %v_ref.5), custom_call_target="tpu_custom_call" | custom-call | tf_op jit(solution)/shard_map/pack_rows/pallas_call | solution.py:370
  6.1 0.0 collective-permute-done.west_ref
  6.1 0.0 copy-start.1
  6.1 2.5 %collective-permute-done.1.east_ref = f32[2,16,128]{2,1,0:T(8,128)S(1)} collective-permute-done((f32[2,16,128]{2,1,0:T(8,128)}, f32[2,16,128]{2,1,0:T(8,128)S(1)}, u32[]{:S(2)}, u32[]{:S(2)}) %collective-permute-start.1) | collective-permute-done | bytes 16416 | tf_op jit(solution)/shard_map/ppermute | solution.py:359
  8.6 0.0 copy-start.3
  8.6 0.0 copy-done.1
  8.6 0.6 %copy-done.3 = f32[2,16,128]{2,1,0:T(8,128)} copy-done((f32[2,16,128]{2,1,0:T(8,128)}, f32[2,16,128]{2,1,0:T(8,128)S(1)}, u32[]{:S(2)}) %copy-start.3) | copy-done | bytes 16408
  9.2 1.5 %join_rows.1 = (f32[104,128]{1,0:T(8,128)}, f32[80,128]{1,0:T(8,128)}) custom-call(s32[16,128]{1,0:T(8,128)} %mask_ref.7, s32[16,128]{1,0:T(8,128)} %levels_ref.7, f32[16,128]{1,0:T(8,128)} %eta_ref.5, f32[2,16,128]{2,1,0:T(8,128)} %copy-done.1, f32[2,16,128]{2,1,0:T(8,128)} %copy-done.3, f32[72,128]{1,0:T(8,128)} %get-tuple-element.18.north_in, ...), custom_call_target="tpu_custom_call" | custom-call | tf_op jit(solution)/shard_map/join_rows/pallas_call | solution.py:373
  10.8 3.2 %collective-permute-start.3 = (f32[104,128]{1,0:T(8,128)}, f32[104,128]{1,0:T(8,128)S(1)}, u32[]{:S(2)}, u32[]{:S(2)}) collective-permute-start(f32[104,128]{1,0:T(8,128)} %get-tuple-element.21), channel_id=1, source_target_pairs={{0,1},{1,2},{2,3},{4,5},{5,6},{6,7},{8,9},{9,10},{10,11},{12,13},{... | collective-permute-start | bytes 159752 | tf_op jit(solution)/shard_map/ppermute | solution.py:359
  14.0 2.1 %collective-permute-start.2 = (f32[80,128]{1,0:T(8,128)}, f32[80,128]{1,0:T(8,128)S(1)}, u32[]{:S(2)}, u32[]{:S(2)}) collective-permute-start(f32[80,128]{1,0:T(8,128)} %get-tuple-element.20), channel_id=1, source_target_pairs={{1,0},{2,1},{3,2},{5,4},{6,5},{7,6},{9,8},{10,9},{11,10},{13,12},{... | collective-permute-start | bytes 122888 | tf_op jit(solution)/shard_map/ppermute | solution.py:359
  16.0 2.9 %collective-permute-done.2.north_ref = f32[80,128]{1,0:T(8,128)S(1)} collective-permute-done((f32[80,128]{1,0:T(8,128)}, f32[80,128]{1,0:T(8,128)S(1)}, u32[]{:S(2)}, u32[]{:S(2)}) %collective-permute-start.2) | collective-permute-done | bytes 40992 | tf_op jit(solution)/shard_map/ppermute | solution.py:359
  18.9 0.0 copy-start.4
  18.9 0.0 collective-permute-done.3.south_ref
  18.9 0.6 %copy-done.4 = f32[80,128]{1,0:T(8,128)} copy-done((f32[80,128]{1,0:T(8,128)}, f32[80,128]{1,0:T(8,128)S(1)}, u32[]{:S(2)}) %copy-start.4) | copy-done | bytes 40984
  19.5 0.0 copy-start
  19.5 0.6 %copy-done = f32[104,128]{1,0:T(8,128)} copy-done((f32[104,128]{1,0:T(8,128)}, f32[104,128]{1,0:T(8,128)S(1)}, u32[]{:S(2)}) %copy-start) | copy-done | bytes 53272
  20.1 3.5 %columns.1 = (f32[2,24,16,128]{3,2,1,0:T(8,128)}, f32[16,128]{1,0:T(8,128)}, f32[16,128]{1,0:T(8,128)}, f32[48,128]{1,0:T(8,128)}, f32[48,128]{1,0:T(8,128)}, /*...) custom-call(s32[16,128]{1,0:T(8,128)} %mask_ref.7, s32[16,128]{1,0:T(8,128)} %levels_ref.7, ...), custom_call_target="tpu_custom_call" | custom-call | tf_op jit(solution)/shard_map/columns/pallas_call | solution.py:379
  23.7 0.0 copy-start.5
  23.7 0.0 copy-start.11
  23.7 0.0 copy-start.8
  23.7 4.5 %all-to-all-start = ((f32[32,1,128]{2,1,0:T(1,128)}), f32[32,1,128]{2,1,0:T(1,128)S(1)}, u32[]{:S(2)}, u32[]{:S(2)}) async-start(f32[32,1,128]{2,1,0:T(1,128)} %bitcast.5), calls=%async_computation | async-start | bytes 32768 | tf_op jit(solution)/shard_map/all_to_all | solution.py:389
  28.2 3.1 %collective-permute-start.7 = (f32[48,128]{1,0:T(8,128)}, f32[48,128]{1,0:T(8,128)S(1)}, u32[]{:S(2)}, u32[]{:S(2)}) collective-permute-start(f32[48,128]{1,0:T(8,128)} %get-tuple-element.29), channel_id=1, source_target_pairs={{0,1},{1,2},{2,3},{4,5},{5,6},{6,7},{8,9},{9,10},{10,11},{12,13},{... | collective-permute-start | bytes 73736 | tf_op jit(solution)/shard_map/ppermute | solution.py:359
  31.3 0.0 copy-done.5
  31.3 2.2 %collective-permute-start.6 = (f32[48,128]{1,0:T(8,128)S(1)}, f32[48,128]{1,0:T(8,128)S(1)}, u32[]{:S(2)}, u32[]{:S(2)}) collective-permute-start(f32[48,128]{1,0:T(8,128)S(1)} %copy-done.5), channel_id=1, source_target_pairs={{1,0},{2,1},{3,2},{5,4},{6,5},{7,6},{9,8},{10,9},{11,10},{13,12},{... | collective-permute-start | bytes 73736 | tf_op jit(solution)/shard_map/ppermute | solution.py:359
  33.5 0.0 copy-done.11
  33.5 2.1 %collective-permute-start.4 = (f32[16,128]{1,0:T(8,128)S(1)}, f32[16,128]{1,0:T(8,128)S(1)}, u32[]{:S(2)}, u32[]{:S(2)}) collective-permute-start(f32[16,128]{1,0:T(8,128)S(1)} %copy-done.11), channel_id=1, source_target_pairs={{0,4},{4,8},{8,12},{12,16},{16,20},{20,24},{24,28},{28,0},{1,5},{5... | collective-permute-start | bytes 24584 | tf_op jit(solution)/shard_map/ppermute | solution.py:359
  35.6 0.0 copy-done.8
  35.6 0.0 collective-permute-start.5
  35.6 0.8 %collective-permute-done.4.from_west_ref = f32[16,128]{1,0:T(8,128)S(1)} collective-permute-done((f32[16,128]{1,0:T(8,128)S(1)}, f32[16,128]{1,0:T(8,128)S(1)}, u32[]{:S(2)}, u32[]{:S(2)}) %collective-permute-start.4) | collective-permute-done | bytes 8224 | tf_op jit(solution)/shard_map/ppermute | solution.py:359
  36.4 0.0 copy-start.9
  36.4 3.2 %collective-permute-done.5.from_east_ref = f32[16,128]{1,0:T(8,128)S(1)} collective-permute-done((f32[16,128]{1,0:T(8,128)S(1)}, f32[16,128]{1,0:T(8,128)S(1)}, u32[]{:S(2)}, u32[]{:S(2)}) %collective-permute-start.5) | collective-permute-done | bytes 8224 | tf_op jit(solution)/shard_map/ppermute | solution.py:359
  39.6 0.0 copy-start.10
  39.6 0.0 collective-permute-done.7.from_south_ref
  39.6 0.0 copy-start.6
  39.6 0.0 collective-permute-done.6.from_north_ref
  39.6 0.0 copy-start.7
  39.6 0.0 all-to-all-done
  39.6 0.0 copy-start.2
  39.6 0.0 copy-done.9
  39.6 0.5 %copy-done.10 = f32[16,128]{1,0:T(8,128)} copy-done((f32[16,128]{1,0:T(8,128)}, f32[16,128]{1,0:T(8,128)S(1)}, u32[]{:S(2)}) %copy-start.10) | copy-done | bytes 8216
  40.2 0.0 copy-done.6
  40.2 0.0 copy-done.7
  40.2 0.0 copy-done.2
  40.2 3.3 %retreat.1 = (f32[2,24,16,128]{3,2,1,0:T(8,128)}, f32[16,128]{1,0:T(8,128)}) custom-call(f32[32,128]{1,0:T(8,128)} %bitcast.4, f32[3,32,256]{2,1,0:T(8,128)} %get-tuple-element.23.basis_ref, f32[32,256]{1,0:T(8,128)} %get-tuple-element.24.level_ref, f32[24,16,128]{2,1,0:T(8,128)} %u_ref.5, f32[24,16,128]{2,1,0:T(8,128)} %v_ref.5, ...), custom_call_target="tpu_custom_call" | custom-call | tf_op jit(solution)/shard_map/retreat/pallas_call | solution.py:390
Async XLA Ops:
  2.6 3.5 %collective-permute-start = (f32[2,16,128]{2,1,0:T(8,128)}, f32[2,16,128]{2,1,0:T(8,128)S(1)}, u32[]{:S(2)}, u32[]{:S(2)}) collective-permute-start(f32[2,16,128]{2,1,0:T(8,128)} %get-tuple-element.16), channel_id=1, source_target_pairs={{0,4},{4,8},{8,12},{12,16},{16,20},{20,24},{24,28},{28,0},{1,5},{5... | collective-permute-start | bytes 49160 | tf_op jit(solution)/shard_map/ppermute | solution.py:359
  4.3 4.3 %collective-permute-start.1 = (f32[2,16,128]{2,1,0:T(8,128)}, f32[2,16,128]{2,1,0:T(8,128)S(1)}, u32[]{:S(2)}, u32[]{:S(2)}) collective-permute-start(f32[2,16,128]{2,1,0:T(8,128)} %get-tuple-element.17.own_west_ref), channel_id=1, source_target_pairs={{0,28},{4,0},{8,4},{12,8},{16,12},{20,16},{24,20},{28,24},{1,29},{... | collective-permute-start | bytes 49160 | tf_op jit(solution)/shard_map/ppermute | solution.py:359
  6.1 2.5 %copy-start.1 = (f32[2,16,128]{2,1,0:T(8,128)}, f32[2,16,128]{2,1,0:T(8,128)S(1)}, u32[]{:S(2)}) copy-start(f32[2,16,128]{2,1,0:T(8,128)S(1)} %collective-permute-done.west_ref) | copy-start | bytes 49156
  8.6 0.6 %copy-start.3 = (f32[2,16,128]{2,1,0:T(8,128)}, f32[2,16,128]{2,1,0:T(8,128)S(1)}, u32[]{:S(2)}) copy-start(f32[2,16,128]{2,1,0:T(8,128)S(1)} %collective-permute-done.1.east_ref) | copy-start | bytes 49156
  10.8 8.2 %collective-permute-start.3 = (f32[104,128]{1,0:T(8,128)}, f32[104,128]{1,0:T(8,128)S(1)}, u32[]{:S(2)}, u32[]{:S(2)}) collective-permute-start(f32[104,128]{1,0:T(8,128)} %get-tuple-element.21), channel_id=1, source_target_pairs={{0,1},{1,2},{2,3},{4,5},{5,6},{6,7},{8,9},{9,10},{10,11},{12,13},{... | collective-permute-start | bytes 159752 | tf_op jit(solution)/shard_map/ppermute | solution.py:359
  14.0 5.0 %collective-permute-start.2 = (f32[80,128]{1,0:T(8,128)}, f32[80,128]{1,0:T(8,128)S(1)}, u32[]{:S(2)}, u32[]{:S(2)}) collective-permute-start(f32[80,128]{1,0:T(8,128)} %get-tuple-element.20), channel_id=1, source_target_pairs={{1,0},{2,1},{3,2},{5,4},{6,5},{7,6},{9,8},{10,9},{11,10},{13,12},{... | collective-permute-start | bytes 122888 | tf_op jit(solution)/shard_map/ppermute | solution.py:359
  18.9 0.6 %copy-start.4 = (f32[80,128]{1,0:T(8,128)}, f32[80,128]{1,0:T(8,128)S(1)}, u32[]{:S(2)}) copy-start(f32[80,128]{1,0:T(8,128)S(1)} %collective-permute-done.2.north_ref) | copy-start | bytes 122884
  19.5 0.6 %copy-start = (f32[104,128]{1,0:T(8,128)}, f32[104,128]{1,0:T(8,128)S(1)}, u32[]{:S(2)}) copy-start(f32[104,128]{1,0:T(8,128)S(1)} %collective-permute-done.3.south_ref) | copy-start | bytes 159748
  23.7 7.6 %copy-start.5 = (f32[48,128]{1,0:T(8,128)S(1)}, f32[48,128]{1,0:T(8,128)}, u32[]{:S(2)}) copy-start(f32[48,128]{1,0:T(8,128)} %get-tuple-element.28.own_south_ref) | copy-start | bytes 73732
  23.7 9.8 %copy-start.11 = (f32[16,128]{1,0:T(8,128)S(1)}, f32[16,128]{1,0:T(8,128)}, u32[]{:S(2)}) copy-start(f32[16,128]{1,0:T(8,128)} %get-tuple-element.26) | copy-start | bytes 24580
  23.7 11.9 %copy-start.8 = (f32[16,128]{1,0:T(8,128)S(1)}, f32[16,128]{1,0:T(8,128)}, u32[]{:S(2)}) copy-start(f32[16,128]{1,0:T(8,128)} %get-tuple-element.27.own_west_ref) | copy-start | bytes 24580
  23.7 15.9 %all-to-all-start = ((f32[32,1,128]{2,1,0:T(1,128)}), f32[32,1,128]{2,1,0:T(1,128)S(1)}, u32[]{:S(2)}, u32[]{:S(2)}) async-start(f32[32,1,128]{2,1,0:T(1,128)} %bitcast.5), calls=%async_computation | async-start | bytes 32768 | tf_op jit(solution)/shard_map/all_to_all | solution.py:389
  28.2 11.4 %collective-permute-start.7 = (f32[48,128]{1,0:T(8,128)}, f32[48,128]{1,0:T(8,128)S(1)}, u32[]{:S(2)}, u32[]{:S(2)}) collective-permute-start(f32[48,128]{1,0:T(8,128)} %get-tuple-element.29), channel_id=1, source_target_pairs={{0,1},{1,2},{2,3},{4,5},{5,6},{6,7},{8,9},{9,10},{10,11},{12,13},{... | collective-permute-start | bytes 73736 | tf_op jit(solution)/shard_map/ppermute | solution.py:359
  31.3 8.3 %collective-permute-start.6 = (f32[48,128]{1,0:T(8,128)S(1)}, f32[48,128]{1,0:T(8,128)S(1)}, u32[]{:S(2)}, u32[]{:S(2)}) collective-permute-start(f32[48,128]{1,0:T(8,128)S(1)} %copy-done.5), channel_id=1, source_target_pairs={{1,0},{2,1},{3,2},{5,4},{6,5},{7,6},{9,8},{10,9},{11,10},{13,12},{... | collective-permute-start | bytes 73736 | tf_op jit(solution)/shard_map/ppermute | solution.py:359
  33.5 2.9 %collective-permute-start.4 = (f32[16,128]{1,0:T(8,128)S(1)}, f32[16,128]{1,0:T(8,128)S(1)}, u32[]{:S(2)}, u32[]{:S(2)}) collective-permute-start(f32[16,128]{1,0:T(8,128)S(1)} %copy-done.11), channel_id=1, source_target_pairs={{0,4},{4,8},{8,12},{12,16},{16,20},{20,24},{24,28},{28,0},{1,5},{5... | collective-permute-start | bytes 24584 | tf_op jit(solution)/shard_map/ppermute | solution.py:359
  35.6 4.0 %collective-permute-start.5 = (f32[16,128]{1,0:T(8,128)S(1)}, f32[16,128]{1,0:T(8,128)S(1)}, u32[]{:S(2)}, u32[]{:S(2)}) collective-permute-start(f32[16,128]{1,0:T(8,128)S(1)} %copy-done.8), channel_id=1, source_target_pairs={{0,28},{4,0},{8,4},{12,8},{16,12},{20,16},{24,20},{28,24},{1,29},{... | collective-permute-start | bytes 24584 | tf_op jit(solution)/shard_map/ppermute | solution.py:359
  36.4 3.2 %copy-start.9 = (f32[16,128]{1,0:T(8,128)}, f32[16,128]{1,0:T(8,128)S(1)}, u32[]{:S(2)}) copy-start(f32[16,128]{1,0:T(8,128)S(1)} %collective-permute-done.4.from_west_ref) | copy-start | bytes 24580
  39.6 0.6 %copy-start.10 = (f32[16,128]{1,0:T(8,128)}, f32[16,128]{1,0:T(8,128)S(1)}, u32[]{:S(2)}) copy-start(f32[16,128]{1,0:T(8,128)S(1)} %collective-permute-done.5.from_east_ref) | copy-start | bytes 24580
  39.6 0.6 %copy-start.6 = (f32[48,128]{1,0:T(8,128)}, f32[48,128]{1,0:T(8,128)S(1)}, u32[]{:S(2)}) copy-start(f32[48,128]{1,0:T(8,128)S(1)} %collective-permute-done.7.from_south_ref) | copy-start | bytes 73732
  39.6 0.6 %copy-start.7 = (f32[48,128]{1,0:T(8,128)}, f32[48,128]{1,0:T(8,128)S(1)}, u32[]{:S(2)}) copy-start(f32[48,128]{1,0:T(8,128)S(1)} %collective-permute-done.6.from_north_ref) | copy-start | bytes 73732
  39.6 0.6 %copy-start.2 = (f32[32,1,128]{2,1,0:T(1,128)}, f32[32,1,128]{2,1,0:T(1,128)S(1)}, u32[]{:S(2)}) copy-start(f32[32,1,128]{2,1,0:T(1,128)S(1)} %all-to-all-done) | copy-start | bytes 49156

commit v2 on v0

v2 whole, which is shorter than its diff:
```python
import jax
import jax.numpy as jnp
from jax import lax
from jax.experimental import pallas as pl
from jax.experimental.pallas import tpu as pltpu
from jax.sharding import PartitionSpec as P

advect_rate = 0.25
mix_floor = 0.2
mix_boost = 2.0
mix_slope = 2.0
mix_rate = 1.0
surface_stiffness = 2.0
thermal_steric = 0.5
haline_steric = 0.5
sterics = (thermal_steric, -haline_steric)
spread = 4.0 * surface_stiffness
F32 = jnp.float32
VMEM = pl.BlockSpec(memory_space=pltpu.VMEM)
SMEM = pl.BlockSpec(memory_space=pltpu.SMEM)
U_TILE, V_TILE, BAR_TILE, SURFACE_TILE = 2, 3, 4, 6


def lanes_of(shape):
    return lax.broadcasted_iota(jnp.int32, shape, 1)


def rows_of(shape):
    return lax.broadcasted_iota(jnp.int32, shape, 0)


def roll(cells, shift, axis):
    size = cells.shape[axis]
    shift = shift % size
    return cells if shift == 0 else pltpu.roll(cells, shift, axis)


def wet_depth(mask_ref, levels_ref):
    return (mask_ref[...] * levels_ref[...]).astype(F32)


def layer_rows(count, width):
    return rows_of((count, width)).astype(F32)


def pack_columns(mask_ref, levels_ref, eta_ref, tracer_ref, u_ref, v_ref, bar_ref, out_ref):
    count, height, width = u_ref.shape
    lane = lanes_of((height, width))
    group = lane // 4
    tiles = [jnp.zeros((height, width), F32)] * SURFACE_TILE
    for k in range(count):
        fields = (tracer_ref[0, k], tracer_ref[1, k], u_ref[k], v_ref[k], bar_ref[0, k], bar_ref[1, k])
        here = group == k
        tiles = [jnp.where(here, roll(field, 4 * k + 2, 1), tile) for field, tile in zip(fields, tiles)]
    for index, tile in enumerate(tiles):
        out_ref[index] = tile
    level = wet_depth(mask_ref, levels_ref)
    depth = jnp.where(lane < width // 2, roll(level, 3, 1), roll(level, -3, 1))
    out_ref[SURFACE_TILE] = jnp.where((lane < 3) | (lane >= width - 3), eta_ref[...], depth)


class Sides:
    def __init__(self, parity_ref, first_ref, second_ref, level):
        self.parity = parity_ref[0]
        self.refs = (first_ref, second_ref)
        self.level = level
        self.shape = level.shape
        lane = lanes_of(self.shape)
        self.lane = lane
        self.layer = (lane // 4).astype(F32)
        self.eastern = lane % 4 == 1
        east, west = self.pick(SURFACE_TILE)
        half = lane < self.shape[1] // 2
        self.eta = jnp.where(half, east, west)
        self.depth = jnp.where(half, roll(self.eta, -3, 1), roll(self.eta, 3, 1))

    def pick(self, tile):
        first, second = (ref[tile] for ref in self.refs)
        even = jnp.full(self.shape, self.parity, jnp.int32) == 0
        return jnp.where(even, first, second), jnp.where(even, second, first)

    def inner(self, tile):
        east, west = self.pick(tile)
        return jnp.where(self.eastern, roll(east, -1, 1), roll(west, 1, 1))

    def outer(self, tile):
        east, west = self.pick(tile)
        return jnp.where(self.eastern, roll(east, -2, 1), roll(west, 2, 1))

    def columns(self, cells, east, west):
        return jnp.where(self.eastern, cells[:, east : east + 1], cells[:, west : west + 1])

    def edge_flow(self, own_ref, u_inner):
        width = self.shape[1]
        own_depth = self.columns(self.level, width - 1, 0)
        beyond = self.columns(self.depth, 0, width - 1)
        flow = jnp.where(self.eastern, own_ref[U_TILE], u_inner)
        return jnp.where(self.layer < jnp.minimum(own_depth, beyond), flow, 0.0)


def pack_rows(mask_ref, levels_ref, tracer_ref, u_ref, v_ref, bar_ref, c_out, n_out, u_out, b_out, v_out):
    count, height, width = u_ref.shape
    level = wet_depth(mask_ref, levels_ref)
    layer = layer_rows(count, width)
    for side, (row, inside, face) in enumerate(((height - 1, height - 2, height - 2), (0, 1, 0))):
        depth = jnp.minimum(level[row : row + 1, :], level[inside : inside + 1, :])
        flow = jnp.where(layer < depth, 0.5 * v_ref[:, face, :], 0.0)
        u_out[side] = u_ref[:, row, :]
        for f in range(2):
            part = slice(f * count, (f + 1) * count)
            c = tracer_ref[f, :, row, :]
            c_out[side, part, :] = c
            n_out[side, part, :] = flow * (c + tracer_ref[f, :, inside, :])
            b_out[side, part, :] = bar_ref[f, :, row, :]
    v_out[...] = jnp.where(layer < level[height - 1 :, :], v_ref[:, height - 1, :], 0.0)


def join_rows(
    parity_ref, mask_ref, levels_ref, eta_ref, own_ref, first_ref, second_ref, c_ref, n_ref, u_ref, b_ref, v_ref,
    north_ref, south_ref,
):
    count, width = v_ref.shape
    level = wet_depth(mask_ref, levels_ref)
    height = level.shape[0]
    sides = Sides(parity_ref, first_ref, second_ref, level)
    inner = [sides.inner(f) for f in range(2)]
    flow = 0.5 * sides.edge_flow(own_ref, sides.inner(U_TILE))
    flux = [flow * (own_ref[f] + inner[f]) for f in range(2)]
    layer = layer_rows(count, width)
    lane = lanes_of((count, width))
    level_row = rows_of((count, width))
    pad = jnp.zeros((8, width), F32)
    for side, (row, sign, out_ref) in enumerate(((height - 1, -1.0, north_ref), (0, 1.0, south_ref))):
        depth = level[row : row + 1, :]
        east_flow = jnp.where(layer < jnp.minimum(depth, roll(depth, -1, 1)), 0.5 * u_ref[side], 0.0)
        rate = jnp.where(layer < depth, advect_rate, 0.0)
        for f in range(2):
            part = slice(f * count, (f + 1) * count)
            c = c_ref[side, part, :]
            line = flux[f][row : row + 1, :]
            east_end, west_end = (
                jnp.sum(jnp.where(lane == 4 * level_row + m, line, 0.0), axis=1, keepdims=True) for m in (1, 2)
            )
            flux_e = jnp.where(lane == width - 1, east_end, east_flow * (c + roll(c, -1, 1)))
            flux_w = jnp.where(lane == 0, west_end, roll(flux_e, 1, 1))
            out_ref[part, :] = c
            out_ref[2 * count + f * count : 2 * count + (f + 1) * count, :] = c - rate * (
                (flux_e - flux_w) + sign * n_ref[side, part, :]
            )
        out_ref[4 * count : 6 * count, :] = b_ref[side]
    start = 6 * count
    north_ref[start : start + count, :] = v_ref[...]
    row8 = rows_of((8, width))
    for index, (eta, depth) in enumerate(((eta_ref[...], level), (sides.eta, sides.depth))):
        at = start + 8 * index
        south_ref[at : at + 8, :] = jnp.where(row8 < 4, eta[:8, :], roll(depth[:8, :], 4, 0))
        at += count
        north_ref[at : at + 8, :] = jnp.where(row8 < 4, roll(depth[height - 8 :, :], 4, 0), eta[height - 8 :, :])
    v_inner = sides.inner(V_TILE)
    at = start + 16
    south_ref[at : at + 8, :] = jnp.where(row8 == 0, inner[0][:1, :], jnp.where(row8 == 1, inner[1][:1, :], pad))
    at += count
    north_ref[at : at + 8, :] = jnp.where(
        row8 == 0,
        inner[0][height - 1 :, :],
        jnp.where(row8 == 1, inner[1][height - 1 :, :], jnp.where(row8 == 2, v_inner[height - 1 :, :], pad)),
    )


def extended(own, side, north, south, turn):
    row8 = rows_of((8, own.shape[1]))
    parts = []
    for index, tile in enumerate((own, side)):
        up, down = (roll(msg[8 * index : 8 * index + 8, :], turn, 0) for msg in (north, south))
        parts.append(jnp.concatenate([tile, jnp.where(row8 < 4, up, down)], axis=0))
    return jnp.concatenate(parts, axis=1)


def surface_kernel(
    parity_ref, mask_ref, levels_ref, eta_ref, first_ref, second_ref, north_ref, south_ref,
    basis_out, level_out, sums_out, *, count,
):
    level = wet_depth(mask_ref, levels_ref)
    height, width = level.shape
    sides = Sides(parity_ref, first_ref, second_ref, level)
    north = north_ref[6 * count : 6 * count + 16, :]
    south = south_ref[7 * count : 7 * count + 16, :]
    eta_ext = extended(eta_ref[...], sides.eta, north, south, 0)
    level_ext = extended(level, sides.depth, north, south, 4)
    level_out[...] = level_ext
    depth = level_ext / count
    east_weight = (surface_stiffness / spread) * jnp.minimum(depth, roll(depth, -1, 1))
    north_weight = (surface_stiffness / spread) * jnp.minimum(depth, roll(depth, -1, 0))

    def scaled(field):
        east_flux = east_weight * (field - roll(field, -1, 1))
        north_flux = north_weight * (field - roll(field, -1, 0))
        return (east_flux - roll(east_flux, 1, 1)) + (north_flux - roll(north_flux, 1, 0))

    first = scaled(eta_ext)
    second = scaled(first) - first
    third = scaled(second)
    basis_out[0] = eta_ext
    basis_out[1] = first
    basis_out[2] = second
    vectors = [x[:height, :width] for x in (eta_ext, first, second, third)]
    pairs = ((0, 0), (0, 1), (0, 2), (1, 1), (1, 2), (2, 2), (2, 3))
    row = rows_of((8, width))
    table = jnp.zeros((8, width), F32)
    for index, (a, b) in enumerate(pairs):
        table = jnp.where(row == index, jnp.sum(vectors[a] * vectors[b], axis=0, keepdims=True), table)
    totals = jnp.sum(table, axis=1, keepdims=True)
    line = jnp.sum(jnp.where(lanes_of((8, width)) == row, totals, 0.0), axis=0, keepdims=True)
    sums_out[...] = jnp.broadcast_to(line, sums_out.shape)


def galerkin(sums):
    d00, d01, d02, d11, d12, d22, d2q = [sums[:, i : i + 1] for i in range(7)]
    k00 = d00 + spread * d01
    k01 = d01 + spread * d11
    k02 = d02 + spread * d12
    k11 = d11 + spread * (d11 + d12)
    k12 = d12 + spread * (d12 + d22)
    k22 = d22 + spread * d2q
    i00 = 1.0 / k00
    s11 = k11 - k01 * k01 * i00
    s12 = k12 - k01 * k02 * i00
    s22 = k22 - k02 * k02 * i00
    g1 = spread * (d01 * d01 - d00 * d11) * i00
    g2 = spread * (d02 * d01 - d00 * d12) * i00
    i11 = 1.0 / s11
    c12 = s12 * i11
    last = s22 - s12 * c12
    y2 = jnp.where(last > 4e-7 * s22, (g2 - g1 * c12) / last, 0.0)
    y1 = (g1 - s12 * y2) * i11
    y0 = (d00 - k01 * y1 - k02 * y2) * i00
    return y0, y1, y2


def column_kernel(
    parity_ref, mask_ref, levels_ref, tracer_ref, u_ref, v_ref, bar_ref,
    own_ref, first_ref, second_ref, c_rows, v_row, north_ref, south_ref, level_ref,
    base_out, flow_out,
    side_ref, turn_ref, ratio_ref, slope_ref, value_ref, adjoint_ref,
):
    count, height, width = u_ref.shape
    level_ext = level_ref[...]
    level = level_ext[:height, :width]
    sides = Sides(parity_ref, first_ref, second_ref, level)
    lane, row = lanes_of((height, width)), rows_of((height, width))
    layer = layer_rows(count, width)
    last_row, last_lane = level_ext.shape[0] - 1, level_ext.shape[1] - 1

    inner = [sides.inner(f) for f in range(2)]
    u_inner, v_inner = sides.inner(U_TILE), sides.inner(V_TILE)
    edge_flow = sides.edge_flow(own_ref, u_inner)
    edge_flux = [0.5 * edge_flow * (own_ref[f] + inner[f]) for f in range(2)]
    depth_in = sides.columns(sides.depth, 0, width - 1)
    depth_out = sides.columns(sides.depth, 1, width - 2)
    far_flow = jnp.where(sides.eastern, u_inner, sides.outer(U_TILE))
    far_flow = jnp.where(sides.layer < jnp.minimum(depth_in, depth_out), far_flow, 0.0)
    corner_depth = [
        jnp.where(sides.eastern[:1], level_ext[r : r + 1, width : width + 1], level_ext[r : r + 1, last_lane:])
        for r in (height, last_row)
    ]
    corner_north = north_ref[6 * count + 16 : 6 * count + 24, :]
    corner_south = south_ref[7 * count + 16 : 7 * count + 24, :]
    depth_up = jnp.where(row == height - 1, corner_depth[0], roll(depth_in, -1, 0))
    up_flow = jnp.where(sides.layer < jnp.minimum(depth_in, depth_up), v_inner, 0.0)
    low_flow = jnp.where(
        sides.layer[:1] < jnp.minimum(depth_in[:1], corner_depth[1]), corner_south[2:3, :], 0.0
    )
    rate = jnp.where(sides.layer < depth_in, advect_rate, 0.0)
    outward = jnp.where(sides.eastern, 1.0, -1.0)
    beyond = []
    for f in range(2):
        c = inner[f]
        far_flux = 0.5 * far_flow * (c + sides.outer(f))
        c_up = jnp.where(row == height - 1, corner_north[f : f + 1, :], roll(c, -1, 0))
        flux_n = 0.5 * up_flow * (c + c_up)
        low_flux = 0.5 * low_flow * (corner_south[f : f + 1, :] + c[:1])
        flux_s = jnp.where(row == 0, low_flux, roll(flux_n, 1, 0))
        beyond.append(c - rate * (outward * (far_flux - edge_flux[f]) + (flux_n - flux_s)))
    beyond += [sides.inner(BAR_TILE), sides.inner(BAR_TILE + 1), depth_in]
    filler = jnp.zeros((width - height * len(beyond), width), F32)
    turned = jnp.transpose(jnp.concatenate(beyond + [filler], axis=0))

    south_flow = jnp.where(layer < level[:1, :], south_ref[6 * count : 7 * count, :], 0.0)
    north_flow = jnp.where(layer < level_ext[height : height + 1, :width], v_row[...], 0.0)
    south_flux, north_flux = [], []
    side_ref[...] = jnp.zeros_like(side_ref)
    for f in range(2):
        part = slice(f * count, (f + 1) * count)
        summed = slice(2 * count + f * count, 2 * count + (f + 1) * count)
        bars = slice(4 * count + f * count, 4 * count + (f + 1) * count)
        south_flux.append(0.5 * south_flow * (south_ref[part, :] + c_rows[1, part, :]))
        north_flux.append(0.5 * north_flow * (c_rows[0, part, :] + north_ref[part, :]))
        side_ref[f, pl.ds(4, count, stride=8), :] = south_ref[summed, :] - advect_rate * south_flux[f]
        side_ref[f, pl.ds(5, count, stride=8), :] = north_ref[summed, :] + advect_rate * north_flux[f]
        side_ref[2 + f, pl.ds(4, count, stride=8), :] = south_ref[bars, :]
        side_ref[2 + f, pl.ds(5, count, stride=8), :] = north_ref[bars, :]
    for f in range(4):
        turn_ref[f] = roll(turned, -height * f, 1)
        for m in (1, 2):
            side_ref[f, pl.ds(m, count, stride=8), :] = turn_ref[f, pl.ds(m, count, stride=4), :]
    row8 = rows_of((8, width))
    side_level = roll(turned[:8, :], -4 * height, 1)
    side_level = jnp.where((row8 == 1) | (row8 == 2), side_level, 0.0)
    side_level = jnp.where(row8 == 4, level_ext[last_row:, :width], side_level)
    side_level = jnp.where(row8 == 5, level_ext[height : height + 1, :width], side_level)
    level_all = jnp.concatenate([level, side_level], axis=0)

    east_depth = jnp.minimum(level_ext, roll(level_ext, -1, 1))[:height, :width]
    north_depth = jnp.minimum(level_ext, roll(level_ext, -1, 0))[:height, :width]

    def with_side(own, f, k):
        return jnp.concatenate([own, side_ref[f, 8 * k : 8 * k + 8, :]], axis=0)

    def advected(k):
        flow_e = jnp.where(east_depth > k, 0.5 * u_ref[k], 0.0)
        flow_n = jnp.where(north_depth > k, 0.5 * v_ref[k], 0.0)
        wet_rate = jnp.where(level > k, advect_rate, 0.0)
        result = []
        for f in range(2):
            c = tracer_ref[f, k]
            ends = roll(edge_flux[f], -(4 * k + 2), 1)
            flux_e = jnp.where(lane == width - 1, ends, flow_e * (c + roll(c, -1, 1)))
            flux_w = jnp.where(lane == 0, ends, roll(flux_e, 1, 1))
            flux_n = jnp.where(row == height - 1, north_flux[f][k : k + 1, :], flow_n * (c + roll(c, -1, 0)))
            flux_s = jnp.where(row == 0, south_flux[f][k : k + 1, :], roll(flux_n, 1, 0))
            result.append(with_side(c - wet_rate * ((flux_e - flux_w) + (flux_n - flux_s)), f, k))
        return result

    now = advected(0)
    kappa_up = ratio_up = values = None
    for k in range(count):
        diagonal = 1.0
        kappa = later = None
        if k < count - 1:
            later = advected(k + 1)
            step = (now[1] - now[0]) - (later[1] - later[0])
            gate = jax.nn.sigmoid(mix_slope * step)
            wet_below = level_all > k + 1
            kappa = jnp.where(wet_below, mix_floor + mix_boost * gate, 0.0)
            slope_ref[k] = jnp.where(wet_below, (mix_boost * mix_slope) * gate * (1.0 - gate), 0.0)
            diagonal = diagonal + mix_rate * kappa
        if k > 0:
            diagonal = diagonal + mix_rate * kappa_up * (1.0 - ratio_up)
        inverse = 1.0 / diagonal
        right = [now[0], now[1], with_side(bar_ref[0, k], 2, k), with_side(bar_ref[1, k], 3, k)]
        if k > 0:
            right = [cells + mix_rate * kappa_up * value for cells, value in zip(right, values)]
        values = [cells * inverse for cells in right]
        for f in range(4):
            value_ref[f, k] = values[f]
        if kappa is not None:
            ratio_up, kappa_up = mix_rate * kappa * inverse, kappa
            ratio_ref[k] = ratio_up
        now = later

    def emit(k, cells, change):
        for f, sign in ((0, -1.0), (1, 1.0)):
            full = cells[2 + f] + sign * change
            adjoint_ref[f, k] = full[:height, :]
            side_ref[f, 8 * k : 8 * k + 8, :] = full[height:, :]

    below = values
    pull_below = None
    for k in range(count - 2, -1, -1):
        here = [value_ref[f, k] + ratio_ref[k] * below[f] for f in range(4)]
        pull = (-mix_rate) * slope_ref[k] * (
            (here[2] - below[2]) * (here[0] - below[0]) + (here[3] - below[3]) * (here[1] - below[1])
        )
        emit(k + 1, below, -pull if pull_below is None else pull_below - pull)
        below, pull_below = here, pull
    emit(0, below, pull_below)

    for f in range(2):
        for m in (1, 2):
            turn_ref[f, pl.ds(m, count, stride=4), :] = side_ref[f, pl.ds(m, count, stride=8), :]
    wide = lanes_of((width, width)) < height
    back = jnp.transpose(jnp.where(wide, turn_ref[0], roll(turn_ref[1], height, 1)))
    ends_of = [back[f * height : (f + 1) * height, :] for f in range(2)]
    south_line = [side_ref[f, pl.ds(4, count, stride=8), :] for f in range(2)]
    north_line = [side_ref[f, pl.ds(5, count, stride=8), :] for f in range(2)]
    for k in range(count):
        flow_e = jnp.where(east_depth > k, u_ref[k], 0.0)
        flow_n = jnp.where(north_depth > k, v_ref[k], 0.0)
        ends_flow = roll(edge_flow, -(4 * k + 2), 1)
        low = south_flow[k : k + 1, :]
        flow_out[0, k] = flow_e
        flow_out[1, k] = jnp.where(lane == 0, ends_flow, roll(flow_e, 1, 1))
        flow_out[2, k] = flow_n
        flow_out[3, k] = jnp.where(row == 0, low, roll(flow_n, 1, 0))
        for f in range(2):
            y = adjoint_ref[f, k]
            ends = roll(ends_of[f], -(4 * k + 2), 1)
            y_east = jnp.where(lane == width - 1, ends, roll(y, -1, 1))
            y_north = jnp.where(row == height - 1, north_line[f][k : k + 1, :], roll(y, -1, 0))
            part_e = flow_e * (y - y_east)
            part_n = flow_n * (y - y_north)
            part_w = jnp.where(lane == 0, ends_flow * (ends - y), roll(part_e, 1, 1))
            part_s = jnp.where(row == 0, low * (south_line[f][k : k + 1, :] - y), roll(part_n, 1, 0))
            base_out[f, k] = y - (0.5 * advect_rate) * ((part_e + part_w) + (part_n + part_s))


def final_kernel(sums_ref, basis_ref, level_ref, base_ref, flow_ref, tracer_out, eta_out):
    _, count, height, width = base_ref.shape
    y0, y1, y2 = galerkin(jnp.sum(sums_ref[...], axis=0, keepdims=True))
    eta_ext = y0 * basis_ref[0] + (y1 * basis_ref[1] + y2 * basis_ref[2])
    eta = eta_ext[:height, :width]
    level = level_ref[:height, :width]
    eta_out[...] = eta
    half = 0.5 * advect_rate
    east = half * (eta_ext - roll(eta_ext, -1, 1))
    north = half * (eta_ext - roll(eta_ext, -1, 0))
    west = roll(east, 1, 1)[:height, :width]
    south = roll(north, 1, 0)[:height, :width]
    east, north = east[:height, :width], north[:height, :width]
    for k in range(count):
        part = (flow_ref[0, k] * east + flow_ref[1, k] * west) + (flow_ref[2, k] * north + flow_ref[3, k] * south)
        share = jnp.where(level > k, eta, 0.0) - part
        for f in range(2):
            tracer_out[f, k] = base_ref[f, k] + sterics[f] * share


def call(kernel, outs, name, specs=None, scratch=(), cost=None):
    def run(*operands):
        return pl.pallas_call(
            kernel,
            out_shape=[jax.ShapeDtypeStruct(shape, F32) for shape in outs],
            in_specs=specs or [VMEM] * len(operands),
            out_specs=[VMEM] * len(outs),
            scratch_shapes=list(scratch),
            cost_estimate=cost,
            name=name,
        )(*operands)

    return run


def swap(cells, axis, first):
    count = lax.axis_size(axis)
    pairs = []
    for i in range(first, count, 2):
        j = (i + 1) % count
        pairs += [(i, j), (j, i)]
    return lax.ppermute(cells, axis, pairs)


def shift(cells, axis, step):
    count = lax.axis_size(axis)
    return lax.ppermute(cells, axis, [(i, i + step) for i in range(count) if 0 <= i + step < count])


def per_device(tracers, uvel, vvel, sea_mask, levels, tracer_bar, eta_bar):
    _, count, height, width = tracers.shape
    devices = lax.axis_size("gx") * lax.axis_size("gy")
    tile = (height, width)
    rows = (2, 2 * count, width)
    depths = (sea_mask, levels)
    parity = (lax.axis_index("gx") % 2).astype(jnp.int32).reshape(1)
    (own,) = call(pack_columns, [(SURFACE_TILE + 1,) + tile], "pack_columns")(
        *depths, eta_bar, tracers, uvel, vvel, tracer_bar
    )
    first, second = swap(own, "gx", 0), swap(own, "gx", 1)
    c_rows, n_rows, u_rows, b_rows, v_row = call(
        pack_rows, [rows, rows, (2, count, width), rows, (count, width)], "pack_rows"
    )(*depths, tracers, uvel, vvel, tracer_bar)
    to_north, to_south = call(
        join_rows, [(7 * count + 24, width), (6 * count + 24, width)], "join_rows", [SMEM] + [VMEM] * 11
    )(parity, *depths, eta_bar, own, first, second, c_rows, n_rows, u_rows, b_rows, v_row)
    from_south, from_north = shift(to_north, "gy", 1), shift(to_south, "gy", -1)
    ext = (height + 8, 2 * width)

    def surface(*refs):
        surface_kernel(*refs, count=count)

    basis, level_ext, sums = call(
        surface, [(3,) + ext, ext, (devices, width)], "surface", [SMEM] + [VMEM] * 7
    )(parity, *depths, eta_bar, first, second, from_north, from_south)
    all_sums = lax.all_to_all(sums.reshape(devices, 1, width), ("gx", "gy"), 0, 0).reshape(devices, width)
    taller = (height + 8, width)
    base, flows = call(
        column_kernel,
        [(2, count) + tile, (4, count) + tile],
        "columns",
        [SMEM] + [VMEM] * 14,
        [
            pltpu.VMEM((4, 8 * count, width), F32),
            pltpu.VMEM((4, width, width), F32),
            pltpu.VMEM((count,) + taller, F32),
            pltpu.VMEM((count,) + taller, F32),
            pltpu.VMEM((4, count) + taller, F32),
            pltpu.VMEM((2, count) + tile, F32),
        ],
        pl.CostEstimate(flops=400 * count * height * width, transcendentals=count * height * width, bytes_accessed=1 << 22),
    )(parity, *depths, tracers, uvel, vvel, tracer_bar, own, first, second, c_rows, v_row, from_north, from_south, level_ext)
    tracer_adj, eta_adj = call(final_kernel, [tracers.shape, tile], "finish")(all_sums, basis, level_ext, base, flows)
    return (tracer_adj, eta_adj)


def solution(mesh):
    return jax.shard_map(
        per_device,
        mesh=mesh,
        in_specs=(
            P(None, None, "gy", "gx"),
            P(None, "gy", "gx"),
            P(None, "gy", "gx"),
            P("gy", "gx"),
            P("gy", "gx"),
            P(None, None, "gy", "gx"),
            P("gy", "gx"),
        ),
        out_specs=(P(None, None, "gy", "gx"), P("gy", "gx")),
        check_vma=False,
    )
```

time: 211 us -> 41.1 us (0.19)
  blocking collectives: 120 us -> 0 us
  other arithmetic: 21 us -> 0 us
  starting transfers between devices: 33.9 us -> 13.3 us
  Pallas kernels: 0 us -> 18 us
  waiting for transfers between devices: 17.8 us -> 6.22 us
  between operations: 11.5 us -> 0.66 us
  local copies, waits for them, and re-layouts: 5.63 us -> 2.51 us
    psum x3 -> x0, blocking collectives: 120 us -> none  [paired_sums(): lax.psum((jnp.sum(residual * residual), jnp.sum(residual * image)), ('gx'...]
    ppermute x20 -> x4, starting transfers between devices: 33.9 us -> 9.32 us  [the longest x2 5.96 us: shift(): lax.ppermute(cells, axis, [(i, i + step) for i in range(count) if 0 <= i...]
    pallas_call x0 -> x6, Pallas kernels: none -> 18 us  [run(): pl.pallas_call(kernel, out_shape=[jax.ShapeDtypeStruct(shape, F32) for sh...]
    ppermute x20 -> x4, waiting for transfers between devices: 17.8 us -> 5.34 us  [the longest x2 5.29 us: shift(): lax.ppermute(cells, axis, [(i, i + step) for i in range(count) if 0 <= i...]
    mul x31 -> x0, other arithmetic: 7.29 us -> none  [the longest x2 2.52 us: advance(): north_flow[None] * 0.5]
    reduce_sum x24 -> x0, other arithmetic: 4.63 us -> none  [the longest x3 2.77 us: paired_sums(): jnp.sum(residual * image)]
    all_to_all x0 -> x1, starting transfers between devices: none -> 4 us  [per_device(): lax.all_to_all(sums.reshape(devices, 1, width), ('gx', 'gy'), 0, 0)]
    concatenate x2 -> x0, other arithmetic: 3.68 us -> none  [the longest x1 2.41 us: with_halo(): jnp.concatenate([lax.ppermute(tail, axis, [(i, (i + 1) % count) for i in...]
  transfers between devices with their start and end apart: 20 -> 5, of which waited for: 10 -> 2; matrix products, arithmetic and copies ran while one was open for 7% -> 0% of each run, Pallas kernels for 0% -> 21%
where the time goes in v2:
time: 41.1 us; the launch traced here: 40.7 us
  Pallas kernels  18 us (44%)
  starting transfers between devices  13.3 us (32%)
  waiting for transfers between devices  6.22 us (15%)
  local copies, waits for them, and re-layouts  2.51 us (6%)
  between operations  0.66 us (2%)
    pallas_call x6, Pallas kernels, run(): pl.pallas_call(kernel, out_shape=[jax.ShapeDtypeStruct(shape, F32) for sh...  18 us
    ppermute x2, starting transfers between devices, shift(): lax.ppermute(cells, axis, [(i, i + step) for i in range(count) if 0 <= i...  5.96 us
    ppermute x2, waiting for transfers between devices, shift(): lax.ppermute(cells, axis, [(i, i + step) for i in range(count) if 0 <= i...  5.29 us
    all_to_all x1, starting transfers between devices, per_device(): lax.all_to_all(sums.reshape(devices, 1, width), ('gx', 'gy'), 0, 0)  4 us
    ppermute x2, starting transfers between devices, swap(): return lax.ppermute(cells, axis, pairs)  3.36 us
    unnamed x10, local copies, waits for them, and re-layouts  2.51 us
    all_to_all x1, waiting for transfers between devices, per_device(): lax.all_to_all(sums.reshape(devices, 1, width), ('gx', 'gy'), 0, 0)  0.88 us
  transfers between devices with their start and end apart: 5, of which 2 were waited for; matrix products, arithmetic and copies ran while one was open for 0% of the time, Pallas kernels for 21%

profile of v2, /device:TPU:0, one launch (start us, length us, event | category | flops | bytes accessed | tf_op | source)
XLA Modules:
  0.0 40.7 jit_solution(14097296443657467371)
XLA Ops:
  0.6 2.3 %pack_columns.1.own_ref = f32[7,16,128]{2,1,0:T(8,128)} custom-call(s32[16,128]{1,0:T(8,128)} %mask_ref.7, s32[16,128]{1,0:T(8,128)} %levels_ref.7, f32[16,128]{1,0:T(8,128)} %refs_3_.1, f32[2,24,16,128]{3,2,1,0:T(8,128)} %tracer_ref.5, f32[24,16,128]{2,1,0:T(8,128)} %u_ref.5, f32[24,16,128]{2,1,0:T(8,128)} %v_ref.5, f32[2,24,16,128]{3,2,1,0:T(8,128)} %bar_ref.5), custom_call_target="tpu_custom_call" | custom-call | tf_op jit(solution)/shard_map/pack_columns/pallas_call | solution.py:429
  2.9 3.4 %collective-permute-start.1 = (f32[7,16,128]{2,1,0:T(8,128)}, f32[7,16,128]{2,1,0:T(8,128)S(1)}, u32[]{:S(2)}, u32[]{:S(2)}) collective-permute-start(f32[7,16,128]{2,1,0:T(8,128)} %pack_columns.1.own_ref), channel_id=1, source_target_pairs={{4,8},{8,4},{12,16},{16,12},{20,24},{24,20},{28,0},{0,28},{5,9},{9... | collective-permute-start | bytes 172040 | tf_op jit(solution)/shard_map/ppermute | solution.py:448
  6.3 0.0 collective-permute-start
  6.3 2.1 %pack_rows.1 = (f32[2,48,128]{2,1,0:T(8,128)}, f32[2,48,128]{2,1,0:T(8,128)}, f32[2,24,128]{2,1,0:T(8,128)}, f32[2,48,128]{2,1,0:T(8,128)}, f32[24,128]{1,0:T(8,128)}) custom-call(s32[16,128]{1,0:T(8,128)} %mask_ref.7, s32[16,128]{1,0:T(8,128)} %levels_ref.7, f32[2,24,16,128]{3,2,1,0:T(8,128)} %tracer_ref.5, f32[24,16,128]{2,1,0:T(8,128)} %u_ref.5, ...), custom_call_target="tpu_custom_call" | custom-call | tf_op jit(solution)/shard_map/pack_rows/pallas_call | solution.py:429
  8.4 0.0 collective-permute-done.1.second_ref.refs_5_
  8.4 0.0 copy-start
  8.4 0.0 collective-permute-done.first_ref.refs_4_
  8.5 0.0 copy-start.1
  8.5 0.6 %copy-done = f32[7,16,128]{2,1,0:T(8,128)} copy-done((f32[7,16,128]{2,1,0:T(8,128)}, f32[7,16,128]{2,1,0:T(8,128)S(1)}, u32[]{:S(2)}) %copy-start) | copy-done | bytes 57368
  9.1 0.0 copy-done.1
  9.1 2.0 %join_rows.1 = (f32[192,128]{1,0:T(8,128)}, f32[168,128]{1,0:T(8,128)}) custom-call(s32[1]{0:T(128)} %bitcast.parity_ref.refs_0_, s32[16,128]{1,0:T(8,128)} %mask_ref.7, s32[16,128]{1,0:T(8,128)} %levels_ref.7, f32[16,128]{1,0:T(8,128)} %refs_3_.1, f32[7,16,128]{2,1,0:T(8,128)} %pack_columns.1.own_ref, f32[7,16,128]{2,1,0:T(8,128)} %copy-done.1, ...), custom_call_target="tpu_custom_call" | custom-call | tf_op jit(solution)/shard_map/join_rows/pallas_call | solution.py:429
  11.1 4.7 %collective-permute-start.3 = (f32[192,128]{1,0:T(8,128)}, f32[192,128]{1,0:T(8,128)S(1)}, u32[]{:S(2)}, u32[]{:S(2)}) collective-permute-start(f32[192,128]{1,0:T(8,128)} %get-tuple-element.20), channel_id=1, source_target_pairs={{0,1},{1,2},{2,3},{4,5},{5,6},{6,7},{8,9},{9,10},{10,11},{12,13},{... | collective-permute-start | bytes 294920 | tf_op jit(solution)/shard_map/ppermute | solution.py:453
  15.8 1.3 %collective-permute-start.2 = (f32[168,128]{1,0:T(8,128)}, f32[168,128]{1,0:T(8,128)S(1)}, u32[]{:S(2)}, u32[]{:S(2)}) collective-permute-start(f32[168,128]{1,0:T(8,128)} %get-tuple-element.19), channel_id=1, source_target_pairs={{1,0},{2,1},{3,2},{5,4},{6,5},{7,6},{9,8},{10,9},{11,10},{13,12},{... | collective-permute-start | bytes 258056 | tf_op jit(solution)/shard_map/ppermute | solution.py:453
  17.1 5.3 %collective-permute-done.2.refs_6_.north_ref = f32[168,128]{1,0:T(8,128)S(1)} collective-permute-done((f32[168,128]{1,0:T(8,128)}, f32[168,128]{1,0:T(8,128)S(1)}, u32[]{:S(2)}, u32[]{:S(2)}) %collective-permute-start.2) | collective-permute-done | bytes 86048 | tf_op jit(solution)/shard_map/ppermute | solution.py:453
  22.3 0.0 copy-start.3
  22.4 0.0 collective-permute-done.3.refs_7_.south_ref
  22.4 0.6 %copy-done.3 = f32[168,128]{1,0:T(8,128)} copy-done((f32[168,128]{1,0:T(8,128)}, f32[168,128]{1,0:T(8,128)S(1)}, u32[]{:S(2)}) %copy-start.3) | copy-done | bytes 86040
  23.0 0.0 copy-start.2
  23.0 0.6 %copy-done.2 = f32[192,128]{1,0:T(8,128)} copy-done((f32[192,128]{1,0:T(8,128)}, f32[192,128]{1,0:T(8,128)S(1)}, u32[]{:S(2)}) %copy-start.2) | copy-done | bytes 98328
  23.6 2.2 %surface.1 = (f32[3,24,256]{2,1,0:T(8,128)}, f32[24,256]{1,0:T(8,128)}, f32[32,128]{1,0:T(8,128)}) custom-call(s32[1]{0:T(128)} %bitcast.parity_ref.refs_0_, s32[16,128]{1,0:T(8,128)} %mask_ref.7, s32[16,128]{1,0:T(8,128)} %levels_ref.7, f32[16,128]{1,0:T(8,128)} %refs_3_.1, f32[7,16,128]{2,1,0:T(8,128)} %copy-done.1, f32[7,16,128]{2,1,0:T(8,128)} %copy-done, ...), custom_call_target="tpu_custom_call" | custom-call | tf_op jit(solution)/shard_map/surface/pallas_call | solution.py:429
  25.9 4.0 %all-to-all-start = ((f32[32,1,128]{2,1,0:T(1,128)}), f32[32,1,128]{2,1,0:T(1,128)S(1)}, u32[]{:S(2)}, u32[]{:S(2)}) async-start(f32[32,1,128]{2,1,0:T(1,128)} %bitcast.6), calls=%async_computation | async-start | bytes 32768 | tf_op jit(solution)/shard_map/all_to_all | solution.py:482
  29.9 6.3 %columns.1 = (f32[2,24,16,128]{3,2,1,0:T(8,128)}, f32[4,24,16,128]{3,2,1,0:T(8,128)}) custom-call(s32[1]{0:T(128)} %bitcast.parity_ref.refs_0_, s32[16,128]{1,0:T(8,128)} %mask_ref.7, s32[16,128]{1,0:T(8,128)} %levels_ref.7, f32[2,24,16,128]{3,2,1,0:T(8,128)} %tracer_ref.5, f32[24,16,128]{2,1,0:T(8,128)} %u_ref.5, f32[24,16,128]{2,1,0:T(8,128)} %v_ref.5, ...), custom_call_target="tpu_custom_call" | custom-call | flops 19660800 | bytes 4194304 | tf_op jit(solution)/shard_map/columns/pallas_call | solution.py:429
  36.2 0.9 %all-to-all-done = f32[32,1,128]{2,1,0:T(1,128)S(1)} async-done(((f32[32,1,128]{2,1,0:T(1,128)}), f32[32,1,128]{2,1,0:T(1,128)S(1)}, u32[]{:S(2)}, u32[]{:S(2)}) %all-to-all-start) | async-done | bytes 16416 | tf_op jit(solution)/shard_map/all_to_all | solution.py:482
  37.1 0.0 copy-start.4
  37.1 0.6 %copy-done.4 = f32[32,1,128]{2,1,0:T(1,128)} copy-done((f32[32,1,128]{2,1,0:T(1,128)}, f32[32,1,128]{2,1,0:T(1,128)S(1)}, u32[]{:S(2)}) %copy-start.4) | copy-done | bytes 16408
  37.7 3.0 %finish.1 = (f32[2,24,16,128]{3,2,1,0:T(8,128)}, f32[16,128]{1,0:T(8,128)}) custom-call(f32[32,128]{1,0:T(8,128)} %bitcast.5, f32[3,24,256]{2,1,0:T(8,128)} %get-tuple-element.22.basis_ref, f32[24,256]{1,0:T(8,128)} %get-tuple-element.23.level_ref, f32[2,24,16,128]{3,2,1,0:T(8,128)} %get-tuple-element.24.base_ref, f32[4,24,16,128]{3,2,1,0:T(8,128)} %get-tuple-element.25.flow_ref), custom_call_target="tpu_custom_call" | custom-call | tf_op jit(solution)/shard_map/finish/pallas_call | solution.py:429
Async XLA Ops:
  2.9 5.5 %collective-permute-start.1 = (f32[7,16,128]{2,1,0:T(8,128)}, f32[7,16,128]{2,1,0:T(8,128)S(1)}, u32[]{:S(2)}, u32[]{:S(2)}) collective-permute-start(f32[7,16,128]{2,1,0:T(8,128)} %pack_columns.1.own_ref), channel_id=1, source_target_pairs={{4,8},{8,4},{12,16},{16,12},{20,24},{24,20},{28,0},{0,28},{5,9},{9... | collective-permute-start | bytes 172040 | tf_op jit(solution)/shard_map/ppermute | solution.py:448
  6.3 2.1 %collective-permute-start = (f32[7,16,128]{2,1,0:T(8,128)}, f32[7,16,128]{2,1,0:T(8,128)S(1)}, u32[]{:S(2)}, u32[]{:S(2)}) collective-permute-start(f32[7,16,128]{2,1,0:T(8,128)} %pack_columns.1.own_ref), channel_id=1, source_target_pairs={{0,4},{4,0},{8,12},{12,8},{16,20},{20,16},{24,28},{28,24},{1,5},{5... | collective-permute-start | bytes 172040 | tf_op jit(solution)/shard_map/ppermute | solution.py:448
  8.4 0.6 %copy-start = (f32[7,16,128]{2,1,0:T(8,128)}, f32[7,16,128]{2,1,0:T(8,128)S(1)}, u32[]{:S(2)}) copy-start(f32[7,16,128]{2,1,0:T(8,128)S(1)} %collective-permute-done.1.second_ref.refs_5_) | copy-start | bytes 172036
  8.5 0.6 %copy-start.1 = (f32[7,16,128]{2,1,0:T(8,128)}, f32[7,16,128]{2,1,0:T(8,128)S(1)}, u32[]{:S(2)}) copy-start(f32[7,16,128]{2,1,0:T(8,128)S(1)} %collective-permute-done.first_ref.refs_4_) | copy-start | bytes 172036
  11.1 11.3 %collective-permute-start.3 = (f32[192,128]{1,0:T(8,128)}, f32[192,128]{1,0:T(8,128)S(1)}, u32[]{:S(2)}, u32[]{:S(2)}) collective-permute-start(f32[192,128]{1,0:T(8,128)} %get-tuple-element.20), channel_id=1, source_target_pairs={{0,1},{1,2},{2,3},{4,5},{5,6},{6,7},{8,9},{9,10},{10,11},{12,13},{... | collective-permute-start | bytes 294920 | tf_op jit(solution)/shard_map/ppermute | solution.py:453
  15.8 6.6 %collective-permute-start.2 = (f32[168,128]{1,0:T(8,128)}, f32[168,128]{1,0:T(8,128)S(1)}, u32[]{:S(2)}, u32[]{:S(2)}) collective-permute-start(f32[168,128]{1,0:T(8,128)} %get-tuple-element.19), channel_id=1, source_target_pairs={{1,0},{2,1},{3,2},{5,4},{6,5},{7,6},{9,8},{10,9},{11,10},{13,12},{... | collective-permute-start | bytes 258056 | tf_op jit(solution)/shard_map/ppermute | solution.py:453
  22.3 0.6 %copy-start.3 = (f32[168,128]{1,0:T(8,128)}, f32[168,128]{1,0:T(8,128)S(1)}, u32[]{:S(2)}) copy-start(f32[168,128]{1,0:T(8,128)S(1)} %collective-permute-done.2.refs_6_.north_ref) | copy-start | bytes 258052
  23.0 0.6 %copy-start.2 = (f32[192,128]{1,0:T(8,128)}, f32[192,128]{1,0:T(8,128)S(1)}, u32[]{:S(2)}) copy-start(f32[192,128]{1,0:T(8,128)S(1)} %collective-permute-done.3.refs_7_.south_ref) | copy-start | bytes 294916
  25.9 11.2 %all-to-all-start = ((f32[32,1,128]{2,1,0:T(1,128)}), f32[32,1,128]{2,1,0:T(1,128)S(1)}, u32[]{:S(2)}, u32[]{:S(2)}) async-start(f32[32,1,128]{2,1,0:T(1,128)} %bitcast.6), calls=%async_computation | async-start | bytes 32768 | tf_op jit(solution)/shard_map/all_to_all | solution.py:482
  37.1 0.6 %copy-start.4 = (f32[32,1,128]{2,1,0:T(1,128)}, f32[32,1,128]{2,1,0:T(1,128)S(1)}, u32[]{:S(2)}) copy-start(f32[32,1,128]{2,1,0:T(1,128)S(1)} %all-to-all-done) | copy-start | bytes 49156

commit v3 on v2

--- a/solution.py
+++ b/solution.py
@@ -18,6 +18,7 @@
 F32 = jnp.float32
 VMEM = pl.BlockSpec(memory_space=pltpu.VMEM)
 SMEM = pl.BlockSpec(memory_space=pltpu.SMEM)
+vmem_grant = 8 << 20
 U_TILE, V_TILE, BAR_TILE, SURFACE_TILE = 2, 3, 4, 6
 
 
@@ -433,6 +434,7 @@
             out_specs=[VMEM] * len(outs),
             scratch_shapes=list(scratch),
             cost_estimate=cost,
+            compiler_params=pltpu.CompilerParams(vmem_limit_bytes=vmem_grant),
             name=name,
         )(*operands)
 

time: 41.1 us -> 38.3 us (0.932)
  Pallas kernels: 18 us -> 7.69 us
  local copies, waits for them, and re-layouts: 2.51 us -> 6.62 us
  waiting for transfers between devices: 6.22 us -> 9.25 us
    pallas_call x6, Pallas kernels: 18 us -> 7.69 us  [run(): pl.pallas_call(kernel, out_shape=[jax.ShapeDtypeStruct(shape, F32) for sh...]
    unnamed x10 -> x28, local copies, waits for them, and re-layouts: 2.51 us -> 6.62 us
    all_to_all x1, waiting for transfers between devices: 0.88 us -> 3.18 us  [per_device(): lax.all_to_all(sums.reshape(devices, 1, width), ('gx', 'gy'), 0, 0)]
    ppermute x2, waiting for transfers between devices: 0.05 us -> 0.99 us  [swap(): return lax.ppermute(cells, axis, pairs)]
  transfers between devices with their start and end apart: 5 -> 5, of which waited for: 2 -> 3; matrix products, arithmetic and copies ran while one was open for 0% -> 0% of each run, Pallas kernels for 21% -> 11%
where the time goes in v3:
time: 38.3 us; the launch traced here: 37.8 us
  starting transfers between devices  13.5 us (35%)
  waiting for transfers between devices  9.25 us (24%)
  Pallas kernels  7.69 us (20%)
  local copies, waits for them, and re-layouts  6.62 us (17%)
  between operations  0.75 us (2%)
    pallas_call x6, Pallas kernels, run(): pl.pallas_call(kernel, out_shape=[jax.ShapeDtypeStruct(shape, F32) for sh...  7.69 us
    unnamed x28, local copies, waits for them, and re-layouts  6.62 us
    ppermute x2, starting transfers between devices, shift(): lax.ppermute(cells, axis, [(i, i + step) for i in range(count) if 0 <= i...  6.04 us
    ppermute x2, waiting for transfers between devices, shift(): lax.ppermute(cells, axis, [(i, i + step) for i in range(count) if 0 <= i...  5.08 us
    all_to_all x1, starting transfers between devices, per_device(): lax.all_to_all(sums.reshape(devices, 1, width), ('gx', 'gy'), 0, 0)  4 us
    ppermute x2, starting transfers between devices, swap(): return lax.ppermute(cells, axis, pairs)  3.43 us
    all_to_all x1, waiting for transfers between devices, per_device(): lax.all_to_all(sums.reshape(devices, 1, width), ('gx', 'gy'), 0, 0)  3.18 us
    ppermute x2, waiting for transfers between devices, swap(): return lax.ppermute(cells, axis, pairs)  0.99 us
  transfers between devices with their start and end apart: 5, of which 3 were waited for; matrix products, arithmetic and copies ran while one was open for 0% of the time, Pallas kernels for 11%

profile of v3, /device:TPU:0, one launch (start us, length us, event | category | flops | bytes accessed | tf_op | source)
XLA Modules:
  0.0 37.8 jit_solution(17099467628002335363)
XLA Ops:
  0.6 0.0 copy-start
  0.6 1.0 %copy-done = f32[2,24,16,128]{3,2,1,0:T(8,128)S(1)} copy-done((f32[2,24,16,128]{3,2,1,0:T(8,128)S(1)}, f32[2,24,16,128]{3,2,1,0:T(8,128)}, u32[]{:S(2)}) %copy-start) | copy-done | bytes 393240
  1.6 0.0 copy-start.2
  1.6 1.0 %copy-done.2 = f32[2,24,16,128]{3,2,1,0:T(8,128)S(1)} copy-done((f32[2,24,16,128]{3,2,1,0:T(8,128)S(1)}, f32[2,24,16,128]{3,2,1,0:T(8,128)}, u32[]{:S(2)}) %copy-start.2) | copy-done | bytes 393240
  2.6 0.0 copy-start.4
  2.6 0.9 %copy-done.4 = f32[24,16,128]{2,1,0:T(8,128)S(1)} copy-done((f32[24,16,128]{2,1,0:T(8,128)S(1)}, f32[24,16,128]{2,1,0:T(8,128)}, u32[]{:S(2)}) %copy-start.4) | copy-done | bytes 196632
  3.6 0.0 copy-start.6
  3.6 0.9 %copy-done.6 = f32[24,16,128]{2,1,0:T(8,128)S(1)} copy-done((f32[24,16,128]{2,1,0:T(8,128)S(1)}, f32[24,16,128]{2,1,0:T(8,128)}, u32[]{:S(2)}) %copy-start.6) | copy-done | bytes 196632
  4.5 0.0 copy-start.8
  4.5 0.7 %copy-done.8 = s32[16,128]{1,0:T(8,128)S(1)} copy-done((s32[16,128]{1,0:T(8,128)S(1)}, s32[16,128]{1,0:T(8,128)}, u32[]{:S(2)}) %copy-start.8) | copy-done | bytes 8216
  5.2 0.0 copy-start.10
  5.2 0.7 %copy-done.10 = s32[16,128]{1,0:T(8,128)S(1)} copy-done((s32[16,128]{1,0:T(8,128)S(1)}, s32[16,128]{1,0:T(8,128)}, u32[]{:S(2)}) %copy-start.10) | copy-done | bytes 8216
  5.9 0.0 copy-start.12
  5.9 0.7 %copy-done.12 = f32[16,128]{1,0:T(8,128)S(1)} copy-done((f32[16,128]{1,0:T(8,128)S(1)}, f32[16,128]{1,0:T(8,128)}, u32[]{:S(2)}) %copy-start.12) | copy-done | bytes 8216
  6.6 0.0 copy-start.1
  6.6 0.0 copy-start.3
  6.6 0.0 copy-start.5
  6.6 0.0 copy-start.7
  6.6 0.4 %pack_columns.1.own_ref = f32[7,16,128]{2,1,0:T(8,128)S(1)} custom-call(s32[16,128]{1,0:T(8,128)S(1)} %copy-done.8, s32[16,128]{1,0:T(8,128)S(1)} %copy-done.10, f32[16,128]{1,0:T(8,128)S(1)} %copy-done.12, f32[2,24,16,128]{3,2,1,0:T(8,128)S(1)} %copy-done, f32[24,16,128]{2,1,0:T(8,128)S(1)} %copy-done.4, f32[24,16,128]{2,1,0:T(8,128)S(1)} %copy-done.6, ...), custom_call_target="tpu_custom_call" | custom-call | tf_op jit(solution)/shard_map/pack_columns/pallas_call | solution.py:430
  7.0 3.4 %collective-permute-start.1 = (f32[7,16,128]{2,1,0:T(8,128)S(1)}, f32[7,16,128]{2,1,0:T(8,128)S(1)}, u32[]{:S(2)}, u32[]{:S(2)}) collective-permute-start(f32[7,16,128]{2,1,0:T(8,128)S(1)} %pack_columns.1.own_ref), channel_id=1, source_target_pairs={{4,8},{8,4},{12,16},{16,12},{20,24},{24,20},{28,0},{0,28},{5,9},{9... | collective-permute-start | bytes 172040 | tf_op jit(solution)/shard_map/ppermute | solution.py:450
  10.4 0.0 collective-permute-start
  10.4 0.0 copy-start.11
  10.4 0.0 copy-start.9
  10.4 0.0 copy-done.1
  10.4 0.0 copy-done.3
  10.4 0.0 copy-done.5
  10.4 0.0 copy-done.7
  10.4 0.7 %copy-done.11 = s32[16,128]{1,0:T(8,128)S(1)} copy-done((s32[16,128]{1,0:T(8,128)S(1)}, s32[16,128]{1,0:T(8,128)}, u32[]{:S(2)}) %copy-start.11) | copy-done | bytes 8216
  11.1 0.0 copy-done.9
  11.1 0.1 pack_rows.1
  11.3 0.0 copy-start.13
  11.3 1.0 %collective-permute-done.1.second_ref.refs_5_ = f32[7,16,128]{2,1,0:T(8,128)S(1)} collective-permute-done((f32[7,16,128]{2,1,0:T(8,128)S(1)}, f32[7,16,128]{2,1,0:T(8,128)S(1)}, u32[]{:S(2)}, u32[]{:S(2)}) %collective-permute-start.1) | collective-permute-done | bytes 57376 | tf_op jit(solution)/shard_map/ppermute | solution.py:450
  12.3 0.0 collective-permute-done.first_ref.refs_4_
  12.3 0.0 copy-done.13
  12.3 0.3 join_rows.1
  12.6 4.7 %collective-permute-start.3 = (f32[192,128]{1,0:T(8,128)S(1)}, f32[192,128]{1,0:T(8,128)S(1)}, u32[]{:S(2)}, u32[]{:S(2)}) collective-permute-start(f32[192,128]{1,0:T(8,128)S(1)} %get-tuple-element.20), channel_id=1, source_target_pairs={{0,1},{1,2},{2,3},{4,5},{5,6},{6,7},{8,9},{9,10},{10,11},{12,13},{... | collective-permute-start | bytes 294920 | tf_op jit(solution)/shard_map/ppermute | solution.py:455
  17.4 1.3 %collective-permute-start.2 = (f32[168,128]{1,0:T(8,128)S(1)}, f32[168,128]{1,0:T(8,128)S(1)}, u32[]{:S(2)}, u32[]{:S(2)}) collective-permute-start(f32[168,128]{1,0:T(8,128)S(1)} %get-tuple-element.19), channel_id=1, source_target_pairs={{1,0},{2,1},{3,2},{5,4},{6,5},{7,6},{9,8},{10,9},{11,10},{13,12},{... | collective-permute-start | bytes 258056 | tf_op jit(solution)/shard_map/ppermute | solution.py:455
  18.7 5.1 %collective-permute-done.2.refs_6_.north_ref = f32[168,128]{1,0:T(8,128)S(1)} collective-permute-done((f32[168,128]{1,0:T(8,128)S(1)}, f32[168,128]{1,0:T(8,128)S(1)}, u32[]{:S(2)}, u32[]{:S(2)}) %collective-permute-start.2) | collective-permute-done | bytes 86048 | tf_op jit(solution)/shard_map/ppermute | solution.py:455
  23.7 0.0 collective-permute-done.3.refs_7_.south_ref
  23.7 1.2 %surface.1 = (f32[3,24,256]{2,1,0:T(8,128)S(1)}, f32[24,256]{1,0:T(8,128)S(1)}, f32[32,128]{1,0:T(8,128)}) custom-call(s32[1]{0:T(128)} %bitcast.parity_ref.refs_0_, s32[16,128]{1,0:T(8,128)S(1)} %copy-done.9, s32[16,128]{1,0:T(8,128)S(1)} %copy-done.11, f32[16,128]{1,0:T(8,128)S(1)} %copy-done.13, f32[7,16,128]{2,1,0:T(8,128)S(1)} %collective-permute-done.first_ref.refs_4_, ...), custom_call_target="tpu_custom_call" | custom-call | tf_op jit(solution)/shard_map/surface/pallas_call | solution.py:430
  24.9 4.0 %all-to-all-start = ((f32[32,1,128]{2,1,0:T(1,128)}), f32[32,1,128]{2,1,0:T(1,128)S(1)}, u32[]{:S(2)}, u32[]{:S(2)}) async-start(f32[32,1,128]{2,1,0:T(1,128)} %bitcast.2), calls=%async_computation | async-start | bytes 32768 | tf_op jit(solution)/shard_map/all_to_all | solution.py:484
  28.9 3.9 %columns.1 = (f32[2,24,16,128]{3,2,1,0:T(8,128)S(1)}, f32[4,24,16,128]{3,2,1,0:T(8,128)S(1)}) custom-call(s32[1]{0:T(128)} %bitcast.parity_ref.refs_0_, s32[16,128]{1,0:T(8,128)S(1)} %copy-done.9, s32[16,128]{1,0:T(8,128)S(1)} %copy-done.11, f32[2,24,16,128]{3,2,1,0:T(8,128)S(1)} %copy-done.1, f32[24,16,128]{2,1,0:T(8,128)S(1)} %copy-done.5, ...), custom_call_target="tpu_custom_call" | custom-call | flops 19660800 | bytes 4194304 | tf_op jit(solution)/shard_map/columns/pallas_call | solution.py:430
  32.9 3.2 %all-to-all-done = f32[32,1,128]{2,1,0:T(1,128)S(1)} async-done(((f32[32,1,128]{2,1,0:T(1,128)}), f32[32,1,128]{2,1,0:T(1,128)S(1)}, u32[]{:S(2)}, u32[]{:S(2)}) %all-to-all-start) | async-done | bytes 16416 | tf_op jit(solution)/shard_map/all_to_all | solution.py:484
  36.1 1.7 %finish.1 = (f32[2,24,16,128]{3,2,1,0:T(8,128)}, f32[16,128]{1,0:T(8,128)}) custom-call(f32[32,128]{1,0:T(8,128)S(1)} %bitcast.5, f32[3,24,256]{2,1,0:T(8,128)S(1)} %get-tuple-element.22.basis_ref, f32[24,256]{1,0:T(8,128)S(1)} %get-tuple-element.23.level_ref, f32[2,24,16,128]{3,2,1,0:T(8,128)S(1)} %get-tuple-element.24.base_ref, ...), custom_call_target="tpu_custom_call" | custom-call | tf_op jit(solution)/shard_map/finish/pallas_call | solution.py:430
Async XLA Ops:
  0.6 1.0 %copy-start = (f32[2,24,16,128]{3,2,1,0:T(8,128)S(1)}, f32[2,24,16,128]{3,2,1,0:T(8,128)}, u32[]{:S(2)}) copy-start(f32[2,24,16,128]{3,2,1,0:T(8,128)} %tracer_ref.5) | copy-start | bytes 1179652
  1.6 1.0 %copy-start.2 = (f32[2,24,16,128]{3,2,1,0:T(8,128)S(1)}, f32[2,24,16,128]{3,2,1,0:T(8,128)}, u32[]{:S(2)}) copy-start(f32[2,24,16,128]{3,2,1,0:T(8,128)} %bar_ref.5) | copy-start | bytes 1179652
  2.6 0.9 %copy-start.4 = (f32[24,16,128]{2,1,0:T(8,128)S(1)}, f32[24,16,128]{2,1,0:T(8,128)}, u32[]{:S(2)}) copy-start(f32[24,16,128]{2,1,0:T(8,128)} %u_ref.5) | copy-start | bytes 589828
  3.6 0.9 %copy-start.6 = (f32[24,16,128]{2,1,0:T(8,128)S(1)}, f32[24,16,128]{2,1,0:T(8,128)}, u32[]{:S(2)}) copy-start(f32[24,16,128]{2,1,0:T(8,128)} %v_ref.5) | copy-start | bytes 589828
  4.5 0.7 %copy-start.8 = (s32[16,128]{1,0:T(8,128)S(1)}, s32[16,128]{1,0:T(8,128)}, u32[]{:S(2)}) copy-start(s32[16,128]{1,0:T(8,128)} %mask_ref.7) | copy-start | bytes 24580
  5.2 0.7 %copy-start.10 = (s32[16,128]{1,0:T(8,128)S(1)}, s32[16,128]{1,0:T(8,128)}, u32[]{:S(2)}) copy-start(s32[16,128]{1,0:T(8,128)} %levels_ref.7) | copy-start | bytes 24580
  5.9 0.7 %copy-start.12 = (f32[16,128]{1,0:T(8,128)S(1)}, f32[16,128]{1,0:T(8,128)}, u32[]{:S(2)}) copy-start(f32[16,128]{1,0:T(8,128)} %refs_3_.1) | copy-start | bytes 24580
  6.6 3.8 %copy-start.1 = (f32[2,24,16,128]{3,2,1,0:T(8,128)S(1)}, f32[2,24,16,128]{3,2,1,0:T(8,128)}, u32[]{:S(2)}) copy-start(f32[2,24,16,128]{3,2,1,0:T(8,128)} %tracer_ref.5) | copy-start | bytes 1179652
  6.6 3.8 %copy-start.3 = (f32[2,24,16,128]{3,2,1,0:T(8,128)S(1)}, f32[2,24,16,128]{3,2,1,0:T(8,128)}, u32[]{:S(2)}) copy-start(f32[2,24,16,128]{3,2,1,0:T(8,128)} %bar_ref.5) | copy-start | bytes 1179652
  6.6 3.9 %copy-start.5 = (f32[24,16,128]{2,1,0:T(8,128)S(1)}, f32[24,16,128]{2,1,0:T(8,128)}, u32[]{:S(2)}) copy-start(f32[24,16,128]{2,1,0:T(8,128)} %u_ref.5) | copy-start | bytes 589828
  6.6 3.9 %copy-start.7 = (f32[24,16,128]{2,1,0:T(8,128)S(1)}, f32[24,16,128]{2,1,0:T(8,128)}, u32[]{:S(2)}) copy-start(f32[24,16,128]{2,1,0:T(8,128)} %v_ref.5) | copy-start | bytes 589828
  7.0 5.3 %collective-permute-start.1 = (f32[7,16,128]{2,1,0:T(8,128)S(1)}, f32[7,16,128]{2,1,0:T(8,128)S(1)}, u32[]{:S(2)}, u32[]{:S(2)}) collective-permute-start(f32[7,16,128]{2,1,0:T(8,128)S(1)} %pack_columns.1.own_ref), channel_id=1, source_target_pairs={{4,8},{8,4},{12,16},{16,12},{20,24},{24,20},{28,0},{0,28},{5,9},{9... | collective-permute-start | bytes 172040 | tf_op jit(solution)/shard_map/ppermute | solution.py:450
  10.4 1.9 %collective-permute-start = (f32[7,16,128]{2,1,0:T(8,128)S(1)}, f32[7,16,128]{2,1,0:T(8,128)S(1)}, u32[]{:S(2)}, u32[]{:S(2)}) collective-permute-start(f32[7,16,128]{2,1,0:T(8,128)S(1)} %pack_columns.1.own_ref), channel_id=1, source_target_pairs={{0,4},{4,0},{8,12},{12,8},{16,20},{20,16},{24,28},{28,24},{1,5},{5... | collective-permute-start | bytes 172040 | tf_op jit(solution)/shard_map/ppermute | solution.py:450
  10.4 0.7 %copy-start.11 = (s32[16,128]{1,0:T(8,128)S(1)}, s32[16,128]{1,0:T(8,128)}, u32[]{:S(2)}) copy-start(s32[16,128]{1,0:T(8,128)} %levels_ref.7) | copy-start | bytes 24580
  10.4 0.7 %copy-start.9 = (s32[16,128]{1,0:T(8,128)S(1)}, s32[16,128]{1,0:T(8,128)}, u32[]{:S(2)}) copy-start(s32[16,128]{1,0:T(8,128)} %mask_ref.7) | copy-start | bytes 24580
  11.3 1.0 %copy-start.13 = (f32[16,128]{1,0:T(8,128)S(1)}, f32[16,128]{1,0:T(8,128)}, u32[]{:S(2)}) copy-start(f32[16,128]{1,0:T(8,128)} %refs_3_.1) | copy-start | bytes 24580
  12.6 11.1 %collective-permute-start.3 = (f32[192,128]{1,0:T(8,128)S(1)}, f32[192,128]{1,0:T(8,128)S(1)}, u32[]{:S(2)}, u32[]{:S(2)}) collective-permute-start(f32[192,128]{1,0:T(8,128)S(1)} %get-tuple-element.20), channel_id=1, source_target_pairs={{0,1},{1,2},{2,3},{4,5},{5,6},{6,7},{8,9},{9,10},{10,11},{12,13},{... | collective-permute-start | bytes 294920 | tf_op jit(solution)/shard_map/ppermute | solution.py:455
  17.4 6.4 %collective-permute-start.2 = (f32[168,128]{1,0:T(8,128)S(1)}, f32[168,128]{1,0:T(8,128)S(1)}, u32[]{:S(2)}, u32[]{:S(2)}) collective-permute-start(f32[168,128]{1,0:T(8,128)S(1)} %get-tuple-element.19), channel_id=1, source_target_pairs={{1,0},{2,1},{3,2},{5,4},{6,5},{7,6},{9,8},{10,9},{11,10},{13,12},{... | collective-permute-start | bytes 258056 | tf_op jit(solution)/shard_map/ppermute | solution.py:455
  24.9 11.1 %all-to-all-start = ((f32[32,1,128]{2,1,0:T(1,128)}), f32[32,1,128]{2,1,0:T(1,128)S(1)}, u32[]{:S(2)}, u32[]{:S(2)}) async-start(f32[32,1,128]{2,1,0:T(1,128)} %bitcast.2), calls=%async_computation | async-start | bytes 32768 | tf_op jit(solution)/shard_map/all_to_all | solution.py:484

commit v4 on v3

--- a/solution.py
+++ b/solution.py
@@ -18,7 +18,9 @@
 F32 = jnp.float32
 VMEM = pl.BlockSpec(memory_space=pltpu.VMEM)
 SMEM = pl.BlockSpec(memory_space=pltpu.SMEM)
+HBM = pl.BlockSpec(memory_space=pltpu.HBM)
 vmem_grant = 8 << 20
+chunk = 6
 U_TILE, V_TILE, BAR_TILE, SURFACE_TILE = 2, 3, 4, 6
 
 
@@ -36,26 +38,40 @@
     return cells if shift == 0 else pltpu.roll(cells, shift, axis)
 
 
-def wet_depth(mask_ref, levels_ref):
-    return (mask_ref[...] * levels_ref[...]).astype(F32)
-
-
 def layer_rows(count, width):
     return rows_of((count, width)).astype(F32)
 
 
-def pack_columns(mask_ref, levels_ref, eta_ref, tracer_ref, u_ref, v_ref, bar_ref, out_ref):
+def pack_columns(
+    mask_in, levels_in, eta_in, tracer_in, u_in, v_in, bar_in,
+    out_ref, level_ref, eta_ref, tracer_ref, u_ref, v_ref, bar_ref,
+    mask_ref, levels_ref, sems,
+):
+    pairs = (
+        (tracer_in, tracer_ref), (u_in, u_ref), (v_in, v_ref), (bar_in, bar_ref),
+        (mask_in, mask_ref), (levels_in, levels_ref), (eta_in, eta_ref),
+    )
+    copies = [pltpu.make_async_copy(source, target, sems.at[i]) for i, (source, target) in enumerate(pairs)]
+    for copy in copies:
+        copy.start()
     count, height, width = u_ref.shape
     lane = lanes_of((height, width))
     group = lane // 4
-    tiles = [jnp.zeros((height, width), F32)] * SURFACE_TILE
-    for k in range(count):
-        fields = (tracer_ref[0, k], tracer_ref[1, k], u_ref[k], v_ref[k], bar_ref[0, k], bar_ref[1, k])
-        here = group == k
-        tiles = [jnp.where(here, roll(field, 4 * k + 2, 1), tile) for field, tile in zip(fields, tiles)]
-    for index, tile in enumerate(tiles):
+    fields = (
+        (copies[0], tracer_ref.at[0]), (None, tracer_ref.at[1]), (copies[1], u_ref), (copies[2], v_ref),
+        (copies[3], bar_ref.at[0]), (None, bar_ref.at[1]),
+    )
+    for index, (copy, field) in enumerate(fields):
+        if copy is not None:
+            copy.wait()
+        tile = jnp.zeros((height, width), F32)
+        for k in range(count):
+            tile = jnp.where(group == k, roll(field[k], 4 * k + 2, 1), tile)
         out_ref[index] = tile
-    level = wet_depth(mask_ref, levels_ref)
+    for copy in copies[4:]:
+        copy.wait()
+    level = (mask_ref[...] * levels_ref[...]).astype(F32)
+    level_ref[...] = level
     depth = jnp.where(lane < width // 2, roll(level, 3, 1), roll(level, -3, 1))
     out_ref[SURFACE_TILE] = jnp.where((lane < 3) | (lane >= width - 3), eta_ref[...], depth)
 
@@ -77,7 +93,7 @@
 
     def pick(self, tile):
         first, second = (ref[tile] for ref in self.refs)
-        even = jnp.full(self.shape, self.parity, jnp.int32) == 0
+        even = is_even(self.parity, self.shape)
         return jnp.where(even, first, second), jnp.where(even, second, first)
 
     def inner(self, tile):
@@ -99,9 +115,9 @@
         return jnp.where(self.layer < jnp.minimum(own_depth, beyond), flow, 0.0)
 
 
-def pack_rows(mask_ref, levels_ref, tracer_ref, u_ref, v_ref, bar_ref, c_out, n_out, u_out, b_out, v_out):
+def pack_rows(level_ref, tracer_ref, u_ref, v_ref, bar_ref, c_out, n_out, u_out, b_out, v_out):
     count, height, width = u_ref.shape
-    level = wet_depth(mask_ref, levels_ref)
+    level = level_ref[...]
     layer = layer_rows(count, width)
     for side, (row, inside, face) in enumerate(((height - 1, height - 2, height - 2), (0, 1, 0))):
         depth = jnp.minimum(level[row : row + 1, :], level[inside : inside + 1, :])
@@ -116,76 +132,96 @@
     v_out[...] = jnp.where(layer < level[height - 1 :, :], v_ref[:, height - 1, :], 0.0)
 
 
+class Message:
+    def __init__(self, count):
+        self.tracers = [slice(f * count, (f + 1) * count) for f in range(2)]
+        self.summed = [slice(f * count, (f + 1) * count) for f in range(2, 4)]
+        self.bars = [slice(f * count, (f + 1) * count) for f in range(4, 6)]
+        self.v = slice(6 * count, 7 * count)
+        self.surface = [slice(7 * count + 8 * i, 7 * count + 8 * i + 8) for i in range(2)]
+        self.corner = slice(7 * count + 16, 7 * count + 24)
+        self.rows = 7 * count + 24
+
+
+def is_even(index, shape):
+    return jnp.full(shape, index, jnp.int32) == 0
+
+
 def join_rows(
-    parity_ref, mask_ref, levels_ref, eta_ref, own_ref, first_ref, second_ref, c_ref, n_ref, u_ref, b_ref, v_ref,
-    north_ref, south_ref,
+    parity_ref, level_ref, eta_ref, own_ref, first_ref, second_ref, c_ref, n_ref, u_ref, b_ref, v_ref,
+    first_out, second_out,
 ):
     count, width = v_ref.shape
-    level = wet_depth(mask_ref, levels_ref)
+    level = level_ref[...]
     height = level.shape[0]
+    plan = Message(count)
     sides = Sides(parity_ref, first_ref, second_ref, level)
     inner = [sides.inner(f) for f in range(2)]
+    v_inner = sides.inner(V_TILE)
     flow = 0.5 * sides.edge_flow(own_ref, sides.inner(U_TILE))
     flux = [flow * (own_ref[f] + inner[f]) for f in range(2)]
     layer = layer_rows(count, width)
     lane = lanes_of((count, width))
     level_row = rows_of((count, width))
-    pad = jnp.zeros((8, width), F32)
-    for side, (row, sign, out_ref) in enumerate(((height - 1, -1.0, north_ref), (0, 1.0, south_ref))):
+    row8 = rows_of((8, width))
+    no_flow, pad = jnp.zeros((count, width), F32), jnp.zeros((8, width), F32)
+
+    def put(part, north, south):
+        even = is_even(parity_ref[1], north.shape)
+        first_out[part, :] = jnp.where(even, north, south)
+        second_out[part, :] = jnp.where(even, south, north)
+
+    def summed(side, f, row, sign):
         depth = level[row : row + 1, :]
         east_flow = jnp.where(layer < jnp.minimum(depth, roll(depth, -1, 1)), 0.5 * u_ref[side], 0.0)
         rate = jnp.where(layer < depth, advect_rate, 0.0)
-        for f in range(2):
-            part = slice(f * count, (f + 1) * count)
-            c = c_ref[side, part, :]
-            line = flux[f][row : row + 1, :]
-            east_end, west_end = (
-                jnp.sum(jnp.where(lane == 4 * level_row + m, line, 0.0), axis=1, keepdims=True) for m in (1, 2)
-            )
-            flux_e = jnp.where(lane == width - 1, east_end, east_flow * (c + roll(c, -1, 1)))
-            flux_w = jnp.where(lane == 0, west_end, roll(flux_e, 1, 1))
-            out_ref[part, :] = c
-            out_ref[2 * count + f * count : 2 * count + (f + 1) * count, :] = c - rate * (
-                (flux_e - flux_w) + sign * n_ref[side, part, :]
-            )
-        out_ref[4 * count : 6 * count, :] = b_ref[side]
-    start = 6 * count
-    north_ref[start : start + count, :] = v_ref[...]
-    row8 = rows_of((8, width))
-    for index, (eta, depth) in enumerate(((eta_ref[...], level), (sides.eta, sides.depth))):
-        at = start + 8 * index
-        south_ref[at : at + 8, :] = jnp.where(row8 < 4, eta[:8, :], roll(depth[:8, :], 4, 0))
-        at += count
-        north_ref[at : at + 8, :] = jnp.where(row8 < 4, roll(depth[height - 8 :, :], 4, 0), eta[height - 8 :, :])
-    v_inner = sides.inner(V_TILE)
-    at = start + 16
-    south_ref[at : at + 8, :] = jnp.where(row8 == 0, inner[0][:1, :], jnp.where(row8 == 1, inner[1][:1, :], pad))
-    at += count
-    north_ref[at : at + 8, :] = jnp.where(
-        row8 == 0,
-        inner[0][height - 1 :, :],
-        jnp.where(row8 == 1, inner[1][height - 1 :, :], jnp.where(row8 == 2, v_inner[height - 1 :, :], pad)),
-    )
+        c = c_ref[side, plan.tracers[f], :]
+        line = flux[f][row : row + 1, :]
+        east_end, west_end = (
+            jnp.sum(jnp.where(lane == 4 * level_row + m, line, 0.0), axis=1, keepdims=True) for m in (1, 2)
+        )
+        flux_e = jnp.where(lane == width - 1, east_end, east_flow * (c + roll(c, -1, 1)))
+        flux_w = jnp.where(lane == 0, west_end, roll(flux_e, 1, 1))
+        return c - rate * ((flux_e - flux_w) + sign * n_ref[side, plan.tracers[f], :])
+
+    for f in range(2):
+        part = plan.tracers[f]
+        put(part, c_ref[0, part, :], c_ref[1, part, :])
+        put(plan.summed[f], summed(0, f, height - 1, -1.0), summed(1, f, 0, 1.0))
+        put(plan.bars[f], b_ref[0, part, :], b_ref[1, part, :])
+    put(plan.v, v_ref[...], no_flow)
+    for part, eta, depth in zip(plan.surface, (eta_ref[...], sides.eta), (level, sides.depth)):
+        north = jnp.where(row8 < 4, roll(depth[height - 8 :, :], 4, 0), eta[height - 8 :, :])
+        put(part, north, jnp.where(row8 < 4, eta[:8, :], roll(depth[:8, :], 4, 0)))
+    lines = [inner[0], inner[1], v_inner]
+    north = south = pad
+    for index, cells in enumerate(lines):
+        north = jnp.where(row8 == index, cells[height - 1 :, :], north)
+        south = jnp.where(row8 == index, cells[:1, :], south)
+    put(plan.corner, north, south)
 
 
 def extended(own, side, north, south, turn):
     row8 = rows_of((8, own.shape[1]))
     parts = []
     for index, tile in enumerate((own, side)):
-        up, down = (roll(msg[8 * index : 8 * index + 8, :], turn, 0) for msg in (north, south))
+        up, down = (roll(msg[index], turn, 0) for msg in (north, south))
         parts.append(jnp.concatenate([tile, jnp.where(row8 < 4, up, down)], axis=0))
     return jnp.concatenate(parts, axis=1)
 
 
 def surface_kernel(
-    parity_ref, mask_ref, levels_ref, eta_ref, first_ref, second_ref, north_ref, south_ref,
+    parity_ref, level_ref, eta_ref, first_ref, second_ref, first_row, second_row,
     basis_out, level_out, sums_out, *, count,
 ):
-    level = wet_depth(mask_ref, levels_ref)
+    level = level_ref[...]
     height, width = level.shape
     sides = Sides(parity_ref, first_ref, second_ref, level)
-    north = north_ref[6 * count : 6 * count + 16, :]
-    south = south_ref[7 * count : 7 * count + 16, :]
+    north, south = [], []
+    for part in Message(count).surface:
+        even = is_even(parity_ref[1], (8, width))
+        north.append(jnp.where(even, first_row[part, :], second_row[part, :]))
+        south.append(jnp.where(even, second_row[part, :], first_row[part, :]))
     eta_ext = extended(eta_ref[...], sides.eta, north, south, 0)
     level_ext = extended(level, sides.depth, north, south, 4)
     level_out[...] = level_ext
@@ -193,10 +229,12 @@
     east_weight = (surface_stiffness / spread) * jnp.minimum(depth, roll(depth, -1, 1))
     north_weight = (surface_stiffness / spread) * jnp.minimum(depth, roll(depth, -1, 0))
 
+    west_weight, south_weight = roll(east_weight, 1, 1), roll(north_weight, 1, 0)
+
     def scaled(field):
-        east_flux = east_weight * (field - roll(field, -1, 1))
-        north_flux = north_weight * (field - roll(field, -1, 0))
-        return (east_flux - roll(east_flux, 1, 1)) + (north_flux - roll(north_flux, 1, 0))
+        along_x = east_weight * (field - roll(field, -1, 1)) + west_weight * (field - roll(field, 1, 1))
+        along_y = north_weight * (field - roll(field, -1, 0)) + south_weight * (field - roll(field, 1, 0))
+        return along_x + along_y
 
     first = scaled(eta_ext)
     second = scaled(first) - first
@@ -239,8 +277,8 @@
 
 
 def column_kernel(
-    parity_ref, mask_ref, levels_ref, tracer_ref, u_ref, v_ref, bar_ref,
-    own_ref, first_ref, second_ref, c_rows, v_row, north_ref, south_ref, level_ref,
+    parity_ref, tracer_ref, u_ref, v_ref, bar_ref,
+    own_ref, first_ref, second_ref, c_rows, v_row, first_row, second_row, level_ref,
     base_out, flow_out,
     side_ref, turn_ref, ratio_ref, slope_ref, value_ref, adjoint_ref,
 ):
@@ -251,6 +289,16 @@
     lane, row = lanes_of((height, width)), rows_of((height, width))
     layer = layer_rows(count, width)
     last_row, last_lane = level_ext.shape[0] - 1, level_ext.shape[1] - 1
+    plan = Message(count)
+
+    def from_north(part):
+        even = is_even(parity_ref[1], (part.stop - part.start, width))
+        return jnp.where(even, first_row[part, :], second_row[part, :])
+
+    def from_south(part):
+        even = is_even(parity_ref[1], (part.stop - part.start, width))
+        return jnp.where(even, second_row[part, :], first_row[part, :])
+
 
     inner = [sides.inner(f) for f in range(2)]
     u_inner, v_inner = sides.inner(U_TILE), sides.inner(V_TILE)
@@ -264,8 +312,7 @@
         jnp.where(sides.eastern[:1], level_ext[r : r + 1, width : width + 1], level_ext[r : r + 1, last_lane:])
         for r in (height, last_row)
     ]
-    corner_north = north_ref[6 * count + 16 : 6 * count + 24, :]
-    corner_south = south_ref[7 * count + 16 : 7 * count + 24, :]
+    corner_north, corner_south = from_north(plan.corner), from_south(plan.corner)
     depth_up = jnp.where(row == height - 1, corner_depth[0], roll(depth_in, -1, 0))
     up_flow = jnp.where(sides.layer < jnp.minimum(depth_in, depth_up), v_inner, 0.0)
     low_flow = jnp.where(
@@ -286,20 +333,18 @@
     filler = jnp.zeros((width - height * len(beyond), width), F32)
     turned = jnp.transpose(jnp.concatenate(beyond + [filler], axis=0))
 
-    south_flow = jnp.where(layer < level[:1, :], south_ref[6 * count : 7 * count, :], 0.0)
+    south_flow = jnp.where(layer < level[:1, :], from_south(plan.v), 0.0)
     north_flow = jnp.where(layer < level_ext[height : height + 1, :width], v_row[...], 0.0)
     south_flux, north_flux = [], []
     side_ref[...] = jnp.zeros_like(side_ref)
     for f in range(2):
-        part = slice(f * count, (f + 1) * count)
-        summed = slice(2 * count + f * count, 2 * count + (f + 1) * count)
-        bars = slice(4 * count + f * count, 4 * count + (f + 1) * count)
-        south_flux.append(0.5 * south_flow * (south_ref[part, :] + c_rows[1, part, :]))
-        north_flux.append(0.5 * north_flow * (c_rows[0, part, :] + north_ref[part, :]))
-        side_ref[f, pl.ds(4, count, stride=8), :] = south_ref[summed, :] - advect_rate * south_flux[f]
-        side_ref[f, pl.ds(5, count, stride=8), :] = north_ref[summed, :] + advect_rate * north_flux[f]
-        side_ref[2 + f, pl.ds(4, count, stride=8), :] = south_ref[bars, :]
-        side_ref[2 + f, pl.ds(5, count, stride=8), :] = north_ref[bars, :]
+        part = plan.tracers[f]
+        south_flux.append(0.5 * south_flow * (from_south(part) + c_rows[1, part, :]))
+        north_flux.append(0.5 * north_flow * (c_rows[0, part, :] + from_north(part)))
+        side_ref[f, pl.ds(4, count, stride=8), :] = from_south(plan.summed[f]) - advect_rate * south_flux[f]
+        side_ref[f, pl.ds(5, count, stride=8), :] = from_north(plan.summed[f]) + advect_rate * north_flux[f]
+        side_ref[2 + f, pl.ds(4, count, stride=8), :] = from_south(plan.bars[f])
+        side_ref[2 + f, pl.ds(5, count, stride=8), :] = from_north(plan.bars[f])
     for f in range(4):
         turn_ref[f] = roll(turned, -height * f, 1)
         for m in (1, 2):
@@ -405,13 +450,15 @@
             base_out[f, k] = y - (0.5 * advect_rate) * ((part_e + part_w) + (part_n + part_s))
 
 
-def final_kernel(sums_ref, basis_ref, level_ref, base_ref, flow_ref, tracer_out, eta_out):
+def final_kernel(sums_ref, basis_ref, level_ref, base_ref, flow_ref, tracer_hbm, eta_hbm, tracer_out, eta_out, sems):
     _, count, height, width = base_ref.shape
     y0, y1, y2 = galerkin(jnp.sum(sums_ref[...], axis=0, keepdims=True))
     eta_ext = y0 * basis_ref[0] + (y1 * basis_ref[1] + y2 * basis_ref[2])
     eta = eta_ext[:height, :width]
     level = level_ref[:height, :width]
     eta_out[...] = eta
+    copies = [pltpu.make_async_copy(eta_out, eta_hbm, sems.at[0])]
+    copies[0].start()
     half = 0.5 * advect_rate
     east = half * (eta_ext - roll(eta_ext, -1, 1))
     north = half * (eta_ext - roll(eta_ext, -1, 0))
@@ -423,15 +470,22 @@
         share = jnp.where(level > k, eta, 0.0) - part
         for f in range(2):
             tracer_out[f, k] = base_ref[f, k] + sterics[f] * share
-
-
-def call(kernel, outs, name, specs=None, scratch=(), cost=None):
+        if (k + 1) % chunk == 0 or k == count - 1:
+            levels = pl.ds(k - k % chunk, k % chunk + 1)
+            at = len(copies)
+            copies.append(pltpu.make_async_copy(tracer_out.at[:, levels], tracer_hbm.at[:, levels], sems.at[at]))
+            copies[-1].start()
+    for copy in copies:
+        copy.wait()
+
+
+def call(kernel, outs, name, specs=None, scratch=(), cost=None, out_spec=VMEM):
     def run(*operands):
         return pl.pallas_call(
             kernel,
             out_shape=[jax.ShapeDtypeStruct(shape, F32) for shape in outs],
             in_specs=specs or [VMEM] * len(operands),
-            out_specs=[VMEM] * len(outs),
+            out_specs=[out_spec] * len(outs),
             scratch_shapes=list(scratch),
             cost_estimate=cost,
             compiler_params=pltpu.CompilerParams(vmem_limit_bytes=vmem_grant),
@@ -441,18 +495,14 @@
     return run
 
 
-def swap(cells, axis, first):
+def swap(cells, axis, first, wrap):
     count = lax.axis_size(axis)
     pairs = []
     for i in range(first, count, 2):
-        j = (i + 1) % count
-        pairs += [(i, j), (j, i)]
+        if i + 1 < count or wrap:
+            j = (i + 1) % count
+            pairs += [(i, j), (j, i)]
     return lax.ppermute(cells, axis, pairs)
-
-
-def shift(cells, axis, step):
-    count = lax.axis_size(axis)
-    return lax.ppermute(cells, axis, [(i, i + step) for i in range(count) if 0 <= i + step < count])
 
 
 def per_device(tracers, uvel, vvel, sea_mask, levels, tracer_bar, eta_bar):
@@ -460,45 +510,60 @@
     devices = lax.axis_size("gx") * lax.axis_size("gy")
     tile = (height, width)
     rows = (2, 2 * count, width)
-    depths = (sea_mask, levels)
-    parity = (lax.axis_index("gx") % 2).astype(jnp.int32).reshape(1)
-    (own,) = call(pack_columns, [(SURFACE_TILE + 1,) + tile], "pack_columns")(
-        *depths, eta_bar, tracers, uvel, vvel, tracer_bar
-    )
-    first, second = swap(own, "gx", 0), swap(own, "gx", 1)
+    parity = jnp.stack([lax.axis_index("gx") % 2, lax.axis_index("gy") % 2]).astype(jnp.int32)
+    field = (count,) + tile
+    inputs = (sea_mask, levels, eta_bar, tracers, uvel, vvel, tracer_bar)
+    own, level, eta, tracers, uvel, vvel, tracer_bar = call(
+        pack_columns,
+        [(SURFACE_TILE + 1,) + tile, tile, tile, (2,) + field, field, field, (2,) + field],
+        "pack_columns",
+        [HBM] * 7,
+        [pltpu.VMEM(tile, jnp.int32), pltpu.VMEM(tile, jnp.int32), pltpu.SemaphoreType.DMA((7,))],
+    )(*(pltpu.with_memory_space_constraint(x, pltpu.HBM) for x in inputs))
+    first, second = swap(own, "gx", 0, True), swap(own, "gx", 1, True)
     c_rows, n_rows, u_rows, b_rows, v_row = call(
         pack_rows, [rows, rows, (2, count, width), rows, (count, width)], "pack_rows"
-    )(*depths, tracers, uvel, vvel, tracer_bar)
-    to_north, to_south = call(
-        join_rows, [(7 * count + 24, width), (6 * count + 24, width)], "join_rows", [SMEM] + [VMEM] * 11
-    )(parity, *depths, eta_bar, own, first, second, c_rows, n_rows, u_rows, b_rows, v_row)
-    from_south, from_north = shift(to_north, "gy", 1), shift(to_south, "gy", -1)
+    )(level, tracers, uvel, vvel, tracer_bar)
+    plan = Message(count)
+    message = (plan.rows, width)
+    first_msg, second_msg = call(join_rows, [message, message], "join_rows", [SMEM] + [VMEM] * 10)(
+        parity, level, eta, own, first, second, c_rows, n_rows, u_rows, b_rows, v_row
+    )
+    first_row, second_row = swap(first_msg, "gy", 0, False), swap(second_msg, "gy", 1, False)
     ext = (height + 8, 2 * width)
 
     def surface(*refs):
         surface_kernel(*refs, count=count)
 
-    basis, level_ext, sums = call(
-        surface, [(3,) + ext, ext, (devices, width)], "surface", [SMEM] + [VMEM] * 7
-    )(parity, *depths, eta_bar, first, second, from_north, from_south)
+    basis, level_ext, sums = call(surface, [(3,) + ext, ext, (devices, width)], "surface", [SMEM] + [VMEM] * 6)(
+        parity, level, eta, first, second, first_row, second_row
+    )
     all_sums = lax.all_to_all(sums.reshape(devices, 1, width), ("gx", "gy"), 0, 0).reshape(devices, width)
-    taller = (height + 8, width)
+    taller = (count, height + 8, width)
     base, flows = call(
         column_kernel,
-        [(2, count) + tile, (4, count) + tile],
+        [(2,) + field, (4,) + field],
         "columns",
-        [SMEM] + [VMEM] * 14,
+        [SMEM] + [VMEM] * 12,
         [
             pltpu.VMEM((4, 8 * count, width), F32),
             pltpu.VMEM((4, width, width), F32),
-            pltpu.VMEM((count,) + taller, F32),
-            pltpu.VMEM((count,) + taller, F32),
-            pltpu.VMEM((4, count) + taller, F32),
-            pltpu.VMEM((2, count) + tile, F32),
+            pltpu.VMEM(taller, F32),
+            pltpu.VMEM(taller, F32),
+            pltpu.VMEM((4,) + taller, F32),
+            pltpu.VMEM((2,) + field, F32),
         ],
         pl.CostEstimate(flops=400 * count * height * width, transcendentals=count * height * width, bytes_accessed=1 << 22),
-    )(parity, *depths, tracers, uvel, vvel, tracer_bar, own, first, second, c_rows, v_row, from_north, from_south, level_ext)
-    tracer_adj, eta_adj = call(final_kernel, [tracers.shape, tile], "finish")(all_sums, basis, level_ext, base, flows)
+    )(parity, tracers, uvel, vvel, tracer_bar, own, first, second, c_rows, v_row, first_row, second_row, level_ext)
+    pieces = (count + chunk - 1) // chunk
+    tracer_adj, eta_adj = call(
+        final_kernel,
+        [(2,) + field, tile],
+        "finish",
+        None,
+        [pltpu.VMEM((2,) + field, F32), pltpu.VMEM(tile, F32), pltpu.SemaphoreType.DMA((pieces + 1,))],
+        out_spec=HBM,
+    )(all_sums, basis, level_ext, base, flows)
     return (tracer_adj, eta_adj)
 
 

time: 38.3 us -> 33.2 us (0.87)
  local copies, waits for them, and re-layouts: 6.62 us -> 0 us
  Pallas kernels: 7.69 us -> 10.4 us
  waiting for transfers between devices: 9.25 us -> 6.77 us
  starting transfers between devices: 13.5 us -> 15 us
    unnamed x28 -> x0, local copies, waits for them, and re-layouts: 6.62 us -> none
    ppermute x2 -> x0, starting transfers between devices: 6.04 us -> none  [shift(): lax.ppermute(cells, axis, [(i, i + step) for i in range(count) if 0 <= i...]
    ppermute x2 -> x0, waiting for transfers between devices: 5.08 us -> none  [shift(): lax.ppermute(cells, axis, [(i, i + step) for i in range(count) if 0 <= i...]
    all_to_all x1, starting transfers between devices: 4 us -> 8.47 us  [per_device(): lax.all_to_all(sums.reshape(devices, 1, width), ('gx', 'gy'), 0, 0)]
    ppermute x2 -> x4, starting transfers between devices: 3.43 us -> 6.56 us  [swap(): return lax.ppermute(cells, axis, pairs)]
    ppermute x2 -> x4, waiting for transfers between devices: 0.99 us -> 4.05 us  [swap(): return lax.ppermute(cells, axis, pairs)]
    pallas_call x6, Pallas kernels: 7.69 us -> 10.4 us  [run(): pl.pallas_call(kernel, out_shape=[jax.ShapeDtypeStruct(shape, F32) for sh...]
    all_to_all x1, waiting for transfers between devices: 3.18 us -> 2.73 us  [per_device(): lax.all_to_all(sums.reshape(devices, 1, width), ('gx', 'gy'), 0, 0)]
  transfers between devices with their start and end apart: 5 -> 5, of which waited for: 3 -> 3; matrix products, arithmetic and copies ran while one was open for 0% -> 0% of each run, Pallas kernels for 11% -> 14%
where the time goes in v4:
time: 33.2 us; the launch traced here: 33 us
  starting transfers between devices  15 us (45%)
  Pallas kernels  10.4 us (31%)
  waiting for transfers between devices  6.77 us (20%)
  between operations  0.67 us (2%)
    pallas_call x6, Pallas kernels, run(): pl.pallas_call(kernel, out_shape=[jax.ShapeDtypeStruct(shape, F32) for sh...  10.4 us
    all_to_all x1, starting transfers between devices, per_device(): lax.all_to_all(sums.reshape(devices, 1, width), ('gx', 'gy'), 0, 0)  8.47 us
    ppermute x4, starting transfers between devices, swap(): return lax.ppermute(cells, axis, pairs)  6.56 us
    ppermute x4, waiting for transfers between devices, swap(): return lax.ppermute(cells, axis, pairs)  4.05 us
    all_to_all x1, waiting for transfers between devices, per_device(): lax.all_to_all(sums.reshape(devices, 1, width), ('gx', 'gy'), 0, 0)  2.73 us
  transfers between devices with their start and end apart: 5, of which 3 were waited for; matrix products, arithmetic and copies ran while one was open for 0% of the time, Pallas kernels for 14%

profile of v4, /device:TPU:0, one launch (start us, length us, event | category | flops | bytes accessed | tf_op | source)
XLA Modules:
  0.0 33.0 jit_solution(8544116560226497578)
XLA Ops:
  0.6 1.7 %pack_columns.1 = (f32[7,16,128]{2,1,0:T(8,128)S(1)}, f32[16,128]{1,0:T(8,128)S(1)}, f32[16,128]{1,0:T(8,128)S(1)}, f32[2,24,16,128]{3,2,1,0:T(8,128)S(1)}, f32[...) custom-call(s32[16,128]{1,0:T(8,128)} %mask_in.1, s32[16,128]{1,0:T(8,128)} %levels_in.1, ...), custom_call_target="tpu_custom_call" | custom-call | tf_op jit(solution)/shard_map/pack_columns/pallas_call | solution.py:484
  2.4 0.6 %collective-permute-start = (f32[7,16,128]{2,1,0:T(8,128)S(1)}, f32[7,16,128]{2,1,0:T(8,128)S(1)}, u32[]{:S(2)}, u32[]{:S(2)}) collective-permute-start(f32[7,16,128]{2,1,0:T(8,128)S(1)} %get-tuple-element.23.own_ref), channel_id=1, source_target_pairs={{0,4},{4,0},{8,12},{12,8},{16,20},{20,16},{24,28},{28,24},{1,5},{5... | collective-permute-start | bytes 172040 | tf_op jit(solution)/shard_map/ppermute | solution.py:505
  2.9 3.5 %collective-permute-start.1 = (f32[7,16,128]{2,1,0:T(8,128)S(1)}, f32[7,16,128]{2,1,0:T(8,128)S(1)}, u32[]{:S(2)}, u32[]{:S(2)}) collective-permute-start(f32[7,16,128]{2,1,0:T(8,128)S(1)} %get-tuple-element.23.own_ref), channel_id=1, source_target_pairs={{4,8},{8,4},{12,16},{16,12},{20,24},{24,20},{28,0},{0,28},{5,9},{9... | collective-permute-start | bytes 172040 | tf_op jit(solution)/shard_map/ppermute | solution.py:505
  6.5 0.1 pack_rows.1
  6.6 0.1 pad_add_fusion.parity_ref.refs_0_
  6.7 0.0 collective-permute-done.first_ref.refs_3_
  6.7 1.6 %collective-permute-done.1.second_ref.refs_4_ = f32[7,16,128]{2,1,0:T(8,128)S(1)} collective-permute-done((f32[7,16,128]{2,1,0:T(8,128)S(1)}, f32[7,16,128]{2,1,0:T(8,128)S(1)}, u32[]{:S(2)}, u32[]{:S(2)}) %collective-permute-start.1) | collective-permute-done | bytes 57376 | tf_op jit(solution)/shard_map/ppermute | solution.py:505
  8.3 0.9 %join_rows.1 = (f32[192,128]{1,0:T(8,128)S(1)}, f32[192,128]{1,0:T(8,128)S(1)}) custom-call(s32[2]{0:T(128)S(1)} %pad_add_fusion.parity_ref.refs_0_, f32[16,128]{1,0:T(8,128)S(1)} %get-tuple-element.21.level_ref.refs_1_, f32[16,128]{1,0:T(8,128)S(1)} %get-tuple-element.22.eta_ref.refs_2_, f32[7,16,128]{2,1,0:T(8,128)S(1)} %get-tuple-element.23.own_ref, ...), custom_call_target="tpu_custom_call" | custom-call | tf_op jit(solution)/shard_map/join_rows/pallas_call | solution.py:484
  9.2 1.8 %collective-permute-start.2 = (f32[192,128]{1,0:T(8,128)S(1)}, f32[192,128]{1,0:T(8,128)S(1)}, u32[]{:S(2)}, u32[]{:S(2)}) collective-permute-start(f32[192,128]{1,0:T(8,128)S(1)} %get-tuple-element.33), channel_id=1, source_target_pairs={{0,1},{1,0},{2,3},{3,2},{4,5},{5,4},{6,7},{7,6},{8,9},{9,8},{10,11... | collective-permute-start | bytes 294920 | tf_op jit(solution)/shard_map/ppermute | solution.py:505
  11.0 0.7 %collective-permute-start.3 = (f32[192,128]{1,0:T(8,128)S(1)}, f32[192,128]{1,0:T(8,128)S(1)}, u32[]{:S(2)}, u32[]{:S(2)}) collective-permute-start(f32[192,128]{1,0:T(8,128)S(1)} %get-tuple-element.34), channel_id=1, source_target_pairs={{1,2},{2,1},{5,6},{6,5},{9,10},{10,9},{13,14},{14,13},{17,18},{18,... | collective-permute-start | bytes 294920 | tf_op jit(solution)/shard_map/ppermute | solution.py:505
  11.6 2.4 %collective-permute-done.2.refs_5_.first_row = f32[192,128]{1,0:T(8,128)S(1)} collective-permute-done((f32[192,128]{1,0:T(8,128)S(1)}, f32[192,128]{1,0:T(8,128)S(1)}, u32[]{:S(2)}, u32[]{:S(2)}) %collective-permute-start.2) | collective-permute-done | bytes 98336 | tf_op jit(solution)/shard_map/ppermute | solution.py:505
  14.0 0.0 collective-permute-done.3.refs_6_.second_row
  14.0 1.6 %surface.1 = (f32[3,24,256]{2,1,0:T(8,128)S(1)}, f32[24,256]{1,0:T(8,128)S(1)}, f32[32,128]{1,0:T(8,128)}) custom-call(s32[2]{0:T(128)S(1)} %pad_add_fusion.parity_ref.refs_0_, f32[16,128]{1,0:T(8,128)S(1)} %get-tuple-element.21.level_ref.refs_1_, f32[16,128]{1,0:T(8,128)S(1)} %get-tuple-element.22.eta_ref.refs_2_, ...), custom_call_target="tpu_custom_call" | custom-call | tf_op jit(solution)/shard_map/surface/pallas_call | solution.py:484
  15.7 8.5 %all-to-all-start = ((f32[32,1,128]{2,1,0:T(1,128)}), f32[32,1,128]{2,1,0:T(1,128)S(1)}, u32[]{:S(2)}, u32[]{:S(2)}) async-start(f32[32,1,128]{2,1,0:T(1,128)} %bitcast.3), calls=%async_computation | async-start | bytes 32768 | tf_op jit(solution)/shard_map/all_to_all | solution.py:541
  24.1 4.4 %columns.1 = (f32[2,24,16,128]{3,2,1,0:T(8,128)S(1)}, f32[4,24,16,128]{3,2,1,0:T(8,128)S(1)}) custom-call(s32[2]{0:T(128)S(1)} %pad_add_fusion.parity_ref.refs_0_, f32[2,24,16,128]{3,2,1,0:T(8,128)S(1)} %get-tuple-element.24.tracer_ref, f32[24,16,128]{2,1,0:T(8,128)S(1)} %get-tuple-element.25.u_ref, f32[24,16,128]{2,1,0:T(8,128)S(1)} %get-tuple-element.26.v_ref, ...), custom_call_target="tpu_custom_call" | custom-call | flops 19660800 | bytes 4194304 | tf_op jit(solution)/shard_map/columns/pallas_call | solution.py:484
  28.5 2.7 %all-to-all-done = f32[32,1,128]{2,1,0:T(1,128)S(1)} async-done(((f32[32,1,128]{2,1,0:T(1,128)}), f32[32,1,128]{2,1,0:T(1,128)S(1)}, u32[]{:S(2)}, u32[]{:S(2)}) %all-to-all-start) | async-done | bytes 16416 | tf_op jit(solution)/shard_map/all_to_all | solution.py:541
  31.3 1.7 %finish.1 = (f32[2,24,16,128]{3,2,1,0:T(8,128)}, f32[16,128]{1,0:T(8,128)}) custom-call(f32[32,128]{1,0:T(8,128)S(1)} %bitcast.6, f32[3,24,256]{2,1,0:T(8,128)S(1)} %get-tuple-element.36.basis_ref, f32[24,256]{1,0:T(8,128)S(1)} %get-tuple-element.37.level_ref, f32[2,24,16,128]{3,2,1,0:T(8,128)S(1)} %get-tuple-element.38.base_ref, ...), custom_call_target="tpu_custom_call" | custom-call | tf_op jit(solution)/shard_map/finish/pallas_call | solution.py:484
Async XLA Ops:
  2.4 4.3 %collective-permute-start = (f32[7,16,128]{2,1,0:T(8,128)S(1)}, f32[7,16,128]{2,1,0:T(8,128)S(1)}, u32[]{:S(2)}, u32[]{:S(2)}) collective-permute-start(f32[7,16,128]{2,1,0:T(8,128)S(1)} %get-tuple-element.23.own_ref), channel_id=1, source_target_pairs={{0,4},{4,0},{8,12},{12,8},{16,20},{20,16},{24,28},{28,24},{1,5},{5... | collective-permute-start | bytes 172040 | tf_op jit(solution)/shard_map/ppermute | solution.py:505
  2.9 5.4 %collective-permute-start.1 = (f32[7,16,128]{2,1,0:T(8,128)S(1)}, f32[7,16,128]{2,1,0:T(8,128)S(1)}, u32[]{:S(2)}, u32[]{:S(2)}) collective-permute-start(f32[7,16,128]{2,1,0:T(8,128)S(1)} %get-tuple-element.23.own_ref), channel_id=1, source_target_pairs={{4,8},{8,4},{12,16},{16,12},{20,24},{24,20},{28,0},{0,28},{5,9},{9... | collective-permute-start | bytes 172040 | tf_op jit(solution)/shard_map/ppermute | solution.py:505
  9.2 4.9 %collective-permute-start.2 = (f32[192,128]{1,0:T(8,128)S(1)}, f32[192,128]{1,0:T(8,128)S(1)}, u32[]{:S(2)}, u32[]{:S(2)}) collective-permute-start(f32[192,128]{1,0:T(8,128)S(1)} %get-tuple-element.33), channel_id=1, source_target_pairs={{0,1},{1,0},{2,3},{3,2},{4,5},{5,4},{6,7},{7,6},{8,9},{9,8},{10,11... | collective-permute-start | bytes 294920 | tf_op jit(solution)/shard_map/ppermute | solution.py:505
  11.0 3.1 %collective-permute-start.3 = (f32[192,128]{1,0:T(8,128)S(1)}, f32[192,128]{1,0:T(8,128)S(1)}, u32[]{:S(2)}, u32[]{:S(2)}) collective-permute-start(f32[192,128]{1,0:T(8,128)S(1)} %get-tuple-element.34), channel_id=1, source_target_pairs={{1,2},{2,1},{5,6},{6,5},{9,10},{10,9},{13,14},{14,13},{17,18},{18,... | collective-permute-start | bytes 294920 | tf_op jit(solution)/shard_map/ppermute | solution.py:505
  15.7 15.6 %all-to-all-start = ((f32[32,1,128]{2,1,0:T(1,128)}), f32[32,1,128]{2,1,0:T(1,128)S(1)}, u32[]{:S(2)}, u32[]{:S(2)}) async-start(f32[32,1,128]{2,1,0:T(1,128)} %bitcast.3), calls=%async_computation | async-start | bytes 32768 | tf_op jit(solution)/shard_map/all_to_all | solution.py:541

commit v5 on v4

--- a/solution.py
+++ b/solution.py
@@ -17,7 +17,6 @@
 spread = 4.0 * surface_stiffness
 F32 = jnp.float32
 VMEM = pl.BlockSpec(memory_space=pltpu.VMEM)
-SMEM = pl.BlockSpec(memory_space=pltpu.SMEM)
 HBM = pl.BlockSpec(memory_space=pltpu.HBM)
 vmem_grant = 8 << 20
 chunk = 6
@@ -77,8 +76,7 @@
 
 
 class Sides:
-    def __init__(self, parity_ref, first_ref, second_ref, level):
-        self.parity = parity_ref[0]
+    def __init__(self, first_ref, second_ref, level):
         self.refs = (first_ref, second_ref)
         self.level = level
         self.shape = level.shape
@@ -93,7 +91,7 @@
 
     def pick(self, tile):
         first, second = (ref[tile] for ref in self.refs)
-        even = is_even(self.parity, self.shape)
+        even = is_even("gx", self.shape)
         return jnp.where(even, first, second), jnp.where(even, second, first)
 
     def inner(self, tile):
@@ -143,19 +141,19 @@
         self.rows = 7 * count + 24
 
 
-def is_even(index, shape):
-    return jnp.full(shape, index, jnp.int32) == 0
+def is_even(axis, shape):
+    return jnp.full(shape, lax.rem(lax.axis_index(axis), 2), jnp.int32) == 0
 
 
 def join_rows(
-    parity_ref, level_ref, eta_ref, own_ref, first_ref, second_ref, c_ref, n_ref, u_ref, b_ref, v_ref,
+    level_ref, eta_ref, own_ref, first_ref, second_ref, c_ref, n_ref, u_ref, b_ref, v_ref,
     first_out, second_out,
 ):
     count, width = v_ref.shape
     level = level_ref[...]
     height = level.shape[0]
     plan = Message(count)
-    sides = Sides(parity_ref, first_ref, second_ref, level)
+    sides = Sides(first_ref, second_ref, level)
     inner = [sides.inner(f) for f in range(2)]
     v_inner = sides.inner(V_TILE)
     flow = 0.5 * sides.edge_flow(own_ref, sides.inner(U_TILE))
@@ -167,7 +165,7 @@
     no_flow, pad = jnp.zeros((count, width), F32), jnp.zeros((8, width), F32)
 
     def put(part, north, south):
-        even = is_even(parity_ref[1], north.shape)
+        even = is_even("gy", north.shape)
         first_out[part, :] = jnp.where(even, north, south)
         second_out[part, :] = jnp.where(even, south, north)
 
@@ -211,15 +209,15 @@
 
 
 def surface_kernel(
-    parity_ref, level_ref, eta_ref, first_ref, second_ref, first_row, second_row,
+    level_ref, eta_ref, first_ref, second_ref, first_row, second_row,
     basis_out, level_out, sums_out, *, count,
 ):
     level = level_ref[...]
     height, width = level.shape
-    sides = Sides(parity_ref, first_ref, second_ref, level)
+    sides = Sides(first_ref, second_ref, level)
     north, south = [], []
     for part in Message(count).surface:
-        even = is_even(parity_ref[1], (8, width))
+        even = is_even("gy", (8, width))
         north.append(jnp.where(even, first_row[part, :], second_row[part, :]))
         south.append(jnp.where(even, second_row[part, :], first_row[part, :]))
     eta_ext = extended(eta_ref[...], sides.eta, north, south, 0)
@@ -277,7 +275,7 @@
 
 
 def column_kernel(
-    parity_ref, tracer_ref, u_ref, v_ref, bar_ref,
+    tracer_ref, u_ref, v_ref, bar_ref,
     own_ref, first_ref, second_ref, c_rows, v_row, first_row, second_row, level_ref,
     base_out, flow_out,
     side_ref, turn_ref, ratio_ref, slope_ref, value_ref, adjoint_ref,
@@ -285,18 +283,18 @@
     count, height, width = u_ref.shape
     level_ext = level_ref[...]
     level = level_ext[:height, :width]
-    sides = Sides(parity_ref, first_ref, second_ref, level)
+    sides = Sides(first_ref, second_ref, level)
     lane, row = lanes_of((height, width)), rows_of((height, width))
     layer = layer_rows(count, width)
     last_row, last_lane = level_ext.shape[0] - 1, level_ext.shape[1] - 1
     plan = Message(count)
 
     def from_north(part):
-        even = is_even(parity_ref[1], (part.stop - part.start, width))
+        even = is_even("gy", (part.stop - part.start, width))
         return jnp.where(even, first_row[part, :], second_row[part, :])
 
     def from_south(part):
-        even = is_even(parity_ref[1], (part.stop - part.start, width))
+        even = is_even("gy", (part.stop - part.start, width))
         return jnp.where(even, second_row[part, :], first_row[part, :])
 
 
@@ -510,7 +508,6 @@
     devices = lax.axis_size("gx") * lax.axis_size("gy")
     tile = (height, width)
     rows = (2, 2 * count, width)
-    parity = jnp.stack([lax.axis_index("gx") % 2, lax.axis_index("gy") % 2]).astype(jnp.int32)
     field = (count,) + tile
     inputs = (sea_mask, levels, eta_bar, tracers, uvel, vvel, tracer_bar)
     own, level, eta, tracers, uvel, vvel, tracer_bar = call(
@@ -526,8 +523,8 @@
     )(level, tracers, uvel, vvel, tracer_bar)
     plan = Message(count)
     message = (plan.rows, width)
-    first_msg, second_msg = call(join_rows, [message, message], "join_rows", [SMEM] + [VMEM] * 10)(
-        parity, level, eta, own, first, second, c_rows, n_rows, u_rows, b_rows, v_row
+    first_msg, second_msg = call(join_rows, [message, message], "join_rows")(
+        level, eta, own, first, second, c_rows, n_rows, u_rows, b_rows, v_row
     )
     first_row, second_row = swap(first_msg, "gy", 0, False), swap(second_msg, "gy", 1, False)
     ext = (height + 8, 2 * width)
@@ -535,8 +532,8 @@
     def surface(*refs):
         surface_kernel(*refs, count=count)
 
-    basis, level_ext, sums = call(surface, [(3,) + ext, ext, (devices, width)], "surface", [SMEM] + [VMEM] * 6)(
-        parity, level, eta, first, second, first_row, second_row
+    basis, level_ext, sums = call(surface, [(3,) + ext, ext, (devices, width)], "surface")(
+        level, eta, first, second, first_row, second_row
     )
     all_sums = lax.all_to_all(sums.reshape(devices, 1, width), ("gx", "gy"), 0, 0).reshape(devices, width)
     taller = (count, height + 8, width)
@@ -544,7 +541,7 @@
         column_kernel,
         [(2,) + field, (4,) + field],
         "columns",
-        [SMEM] + [VMEM] * 12,
+        None,
         [
             pltpu.VMEM((4, 8 * count, width), F32),
             pltpu.VMEM((4, width, width), F32),
@@ -554,7 +551,7 @@
             pltpu.VMEM((2,) + field, F32),
         ],
         pl.CostEstimate(flops=400 * count * height * width, transcendentals=count * height * width, bytes_accessed=1 << 22),
-    )(parity, tracers, uvel, vvel, tracer_bar, own, first, second, c_rows, v_row, first_row, second_row, level_ext)
+    )(tracers, uvel, vvel, tracer_bar, own, first, second, c_rows, v_row, first_row, second_row, level_ext)
     pieces = (count + chunk - 1) // chunk
     tracer_adj, eta_adj = call(
         final_kernel,

time: 33.2 us -> 32.1 us (0.967)
  Pallas kernels: 10.4 us -> 8.72 us
  waiting for transfers between devices: 6.77 us -> 7.49 us
    pallas_call x6, Pallas kernels: 10.4 us -> 8.72 us  [run(): pl.pallas_call(kernel, out_shape=[jax.ShapeDtypeStruct(shape, F32) for sh...]
    all_to_all x1, waiting for transfers between devices: 2.73 us -> 3.37 us  [per_device(): lax.all_to_all(sums.reshape(devices, 1, width), ('gx', 'gy'), 0, 0)]
  transfers between devices with their start and end apart: 5 -> 5, of which waited for: 3 -> 3; matrix products, arithmetic and copies ran while one was open for 0% -> 0% of each run, Pallas kernels for 14% -> 12%
where the time goes in v5:
time: 32.1 us; the launch traced here: 31.9 us
  starting transfers between devices  15 us (47%)
  Pallas kernels  8.72 us (27%)
  waiting for transfers between devices  7.49 us (23%)
  between operations  0.68 us (2%)
    pallas_call x6, Pallas kernels, run(): pl.pallas_call(kernel, out_shape=[jax.ShapeDtypeStruct(shape, F32) for sh...  8.72 us
    all_to_all x1, starting transfers between devices, per_device(): lax.all_to_all(sums.reshape(devices, 1, width), ('gx', 'gy'), 0, 0)  8.47 us
    ppermute x4, starting transfers between devices, swap(): return lax.ppermute(cells, axis, pairs)  6.56 us
    ppermute x4, waiting for transfers between devices, swap(): return lax.ppermute(cells, axis, pairs)  4.12 us
    all_to_all x1, waiting for transfers between devices, per_device(): lax.all_to_all(sums.reshape(devices, 1, width), ('gx', 'gy'), 0, 0)  3.37 us
  transfers between devices with their start and end apart: 5, of which 3 were waited for; matrix products, arithmetic and copies ran while one was open for 0% of the time, Pallas kernels for 12%

profile of v5, /device:TPU:0, one launch (start us, length us, event | category | flops | bytes accessed | tf_op | source)
XLA Modules:
  0.0 31.9 jit_solution(12059981256037348451)
XLA Ops:
  0.6 1.7 %pack_columns.1 = (f32[7,16,128]{2,1,0:T(8,128)S(1)}, f32[16,128]{1,0:T(8,128)S(1)}, f32[16,128]{1,0:T(8,128)S(1)}, f32[2,24,16,128]{3,2,1,0:T(8,128)S(1)}, f32[...) custom-call(s32[16,128]{1,0:T(8,128)} %mask_in.1, s32[16,128]{1,0:T(8,128)} %levels_in.1, ...), custom_call_target="tpu_custom_call" | custom-call | tf_op jit(solution)/shard_map/pack_columns/pallas_call | solution.py:482
  2.4 0.6 %collective-permute-start = (f32[7,16,128]{2,1,0:T(8,128)S(1)}, f32[7,16,128]{2,1,0:T(8,128)S(1)}, u32[]{:S(2)}, u32[]{:S(2)}) collective-permute-start(f32[7,16,128]{2,1,0:T(8,128)S(1)} %get-tuple-element.23.own_ref), channel_id=1, source_target_pairs={{0,4},{4,0},{8,12},{12,8},{16,20},{20,16},{24,28},{28,24},{1,5},{5... | collective-permute-start | bytes 172040 | tf_op jit(solution)/shard_map/ppermute | solution.py:503
  2.9 3.5 %collective-permute-start.1 = (f32[7,16,128]{2,1,0:T(8,128)S(1)}, f32[7,16,128]{2,1,0:T(8,128)S(1)}, u32[]{:S(2)}, u32[]{:S(2)}) collective-permute-start(f32[7,16,128]{2,1,0:T(8,128)S(1)} %get-tuple-element.23.own_ref), channel_id=1, source_target_pairs={{4,8},{8,4},{12,16},{16,12},{20,24},{24,20},{28,0},{0,28},{5,9},{9... | collective-permute-start | bytes 172040 | tf_op jit(solution)/shard_map/ppermute | solution.py:503
  6.5 0.1 pack_rows.1
  6.6 0.0 collective-permute-done.first_ref.refs_2_
  6.6 1.7 %collective-permute-done.1.second_ref.refs_3_ = f32[7,16,128]{2,1,0:T(8,128)S(1)} collective-permute-done((f32[7,16,128]{2,1,0:T(8,128)S(1)}, f32[7,16,128]{2,1,0:T(8,128)S(1)}, u32[]{:S(2)}, u32[]{:S(2)}) %collective-permute-start.1) | collective-permute-done | bytes 57376 | tf_op jit(solution)/shard_map/ppermute | solution.py:503
  8.3 0.3 %join_rows.1 = (f32[192,128]{1,0:T(8,128)S(1)}, f32[192,128]{1,0:T(8,128)S(1)}) custom-call(f32[16,128]{1,0:T(8,128)S(1)} %get-tuple-element.21.level_ref.refs_0_, f32[16,128]{1,0:T(8,128)S(1)} %get-tuple-element.22.eta_ref.refs_1_, f32[7,16,128]{2,1,0:T(8,128)S(1)} %get-tuple-element.23.own_ref, f32[7,16,128]{2,1,0:T(8,128)S(1)} %collective-permute-done.first_ref.refs_2_, ...), custom_call_target="tpu_custom_call" | custom-call | tf_op jit(solution)/shard_map/join_rows/pallas_call | solution.py:482
  8.7 1.8 %collective-permute-start.2 = (f32[192,128]{1,0:T(8,128)S(1)}, f32[192,128]{1,0:T(8,128)S(1)}, u32[]{:S(2)}, u32[]{:S(2)}) collective-permute-start(f32[192,128]{1,0:T(8,128)S(1)} %get-tuple-element.33), channel_id=1, source_target_pairs={{0,1},{1,0},{2,3},{3,2},{4,5},{5,4},{6,7},{7,6},{8,9},{9,8},{10,11... | collective-permute-start | bytes 294920 | tf_op jit(solution)/shard_map/ppermute | solution.py:503
  10.5 0.7 %collective-permute-start.3 = (f32[192,128]{1,0:T(8,128)S(1)}, f32[192,128]{1,0:T(8,128)S(1)}, u32[]{:S(2)}, u32[]{:S(2)}) collective-permute-start(f32[192,128]{1,0:T(8,128)S(1)} %get-tuple-element.34), channel_id=1, source_target_pairs={{1,2},{2,1},{5,6},{6,5},{9,10},{10,9},{13,14},{14,13},{17,18},{18,... | collective-permute-start | bytes 294920 | tf_op jit(solution)/shard_map/ppermute | solution.py:503
  11.1 2.4 %collective-permute-done.2.refs_4_.first_row = f32[192,128]{1,0:T(8,128)S(1)} collective-permute-done((f32[192,128]{1,0:T(8,128)S(1)}, f32[192,128]{1,0:T(8,128)S(1)}, u32[]{:S(2)}, u32[]{:S(2)}) %collective-permute-start.2) | collective-permute-done | bytes 98336 | tf_op jit(solution)/shard_map/ppermute | solution.py:503
  13.5 0.0 collective-permute-done.3.refs_5_.second_row
  13.5 1.1 %surface.1 = (f32[3,24,256]{2,1,0:T(8,128)S(1)}, f32[24,256]{1,0:T(8,128)S(1)}, f32[32,128]{1,0:T(8,128)}) custom-call(f32[16,128]{1,0:T(8,128)S(1)} %get-tuple-element.21.level_ref.refs_0_, f32[16,128]{1,0:T(8,128)S(1)} %get-tuple-element.22.eta_ref.refs_1_, f32[7,16,128]{2,1,0:T(8,128)S(1)} %collective-permute-done.first_ref.refs_2_, ...), custom_call_target="tpu_custom_call" | custom-call | tf_op jit(solution)/shard_map/surface/pallas_call | solution.py:482
  14.6 8.5 %all-to-all-start = ((f32[32,1,128]{2,1,0:T(1,128)}), f32[32,1,128]{2,1,0:T(1,128)S(1)}, u32[]{:S(2)}, u32[]{:S(2)}) async-start(f32[32,1,128]{2,1,0:T(1,128)} %bitcast.1), calls=%async_computation | async-start | bytes 32768 | tf_op jit(solution)/shard_map/all_to_all | solution.py:538
  23.1 3.7 %columns.1 = (f32[2,24,16,128]{3,2,1,0:T(8,128)S(1)}, f32[4,24,16,128]{3,2,1,0:T(8,128)S(1)}) custom-call(f32[2,24,16,128]{3,2,1,0:T(8,128)S(1)} %get-tuple-element.24.tracer_ref, f32[24,16,128]{2,1,0:T(8,128)S(1)} %get-tuple-element.25.u_ref, f32[24,16,128]{2,1,0:T(8,128)S(1)} %get-tuple-element.26.v_ref, f32[2,24,16,128]{3,2,1,0:T(8,128)S(1)} %get-tuple-element.27.bar_ref, ...), custom_call_target="tpu_custom_call" | custom-call | flops 19660800 | bytes 4194304 | tf_op jit(solution)/shard_map/columns/pallas_call | solution.py:482
  26.8 3.4 %all-to-all-done = f32[32,1,128]{2,1,0:T(1,128)S(1)} async-done(((f32[32,1,128]{2,1,0:T(1,128)}), f32[32,1,128]{2,1,0:T(1,128)S(1)}, u32[]{:S(2)}, u32[]{:S(2)}) %all-to-all-start) | async-done | bytes 16416 | tf_op jit(solution)/shard_map/all_to_all | solution.py:538
  30.2 1.7 %finish.1 = (f32[2,24,16,128]{3,2,1,0:T(8,128)}, f32[16,128]{1,0:T(8,128)}) custom-call(f32[32,128]{1,0:T(8,128)S(1)} %bitcast.4, f32[3,24,256]{2,1,0:T(8,128)S(1)} %get-tuple-element.36.basis_ref, f32[24,256]{1,0:T(8,128)S(1)} %get-tuple-element.37.level_ref, f32[2,24,16,128]{3,2,1,0:T(8,128)S(1)} %get-tuple-element.38.base_ref, ...), custom_call_target="tpu_custom_call" | custom-call | tf_op jit(solution)/shard_map/finish/pallas_call | solution.py:482
Async XLA Ops:
  2.4 4.2 %collective-permute-start = (f32[7,16,128]{2,1,0:T(8,128)S(1)}, f32[7,16,128]{2,1,0:T(8,128)S(1)}, u32[]{:S(2)}, u32[]{:S(2)}) collective-permute-start(f32[7,16,128]{2,1,0:T(8,128)S(1)} %get-tuple-element.23.own_ref), channel_id=1, source_target_pairs={{0,4},{4,0},{8,12},{12,8},{16,20},{20,16},{24,28},{28,24},{1,5},{5... | collective-permute-start | bytes 172040 | tf_op jit(solution)/shard_map/ppermute | solution.py:503
  2.9 5.4 %collective-permute-start.1 = (f32[7,16,128]{2,1,0:T(8,128)S(1)}, f32[7,16,128]{2,1,0:T(8,128)S(1)}, u32[]{:S(2)}, u32[]{:S(2)}) collective-permute-start(f32[7,16,128]{2,1,0:T(8,128)S(1)} %get-tuple-element.23.own_ref), channel_id=1, source_target_pairs={{4,8},{8,4},{12,16},{16,12},{20,24},{24,20},{28,0},{0,28},{5,9},{9... | collective-permute-start | bytes 172040 | tf_op jit(solution)/shard_map/ppermute | solution.py:503
  8.7 4.9 %collective-permute-start.2 = (f32[192,128]{1,0:T(8,128)S(1)}, f32[192,128]{1,0:T(8,128)S(1)}, u32[]{:S(2)}, u32[]{:S(2)}) collective-permute-start(f32[192,128]{1,0:T(8,128)S(1)} %get-tuple-element.33), channel_id=1, source_target_pairs={{0,1},{1,0},{2,3},{3,2},{4,5},{5,4},{6,7},{7,6},{8,9},{9,8},{10,11... | collective-permute-start | bytes 294920 | tf_op jit(solution)/shard_map/ppermute | solution.py:503
  10.5 3.1 %collective-permute-start.3 = (f32[192,128]{1,0:T(8,128)S(1)}, f32[192,128]{1,0:T(8,128)S(1)}, u32[]{:S(2)}, u32[]{:S(2)}) collective-permute-start(f32[192,128]{1,0:T(8,128)S(1)} %get-tuple-element.34), channel_id=1, source_target_pairs={{1,2},{2,1},{5,6},{6,5},{9,10},{10,9},{13,14},{14,13},{17,18},{18,... | collective-permute-start | bytes 294920 | tf_op jit(solution)/shard_map/ppermute | solution.py:503
  14.6 15.6 %all-to-all-start = ((f32[32,1,128]{2,1,0:T(1,128)}), f32[32,1,128]{2,1,0:T(1,128)S(1)}, u32[]{:S(2)}, u32[]{:S(2)}) async-start(f32[32,1,128]{2,1,0:T(1,128)} %bitcast.1), calls=%async_computation | async-start | bytes 32768 | tf_op jit(solution)/shard_map/all_to_all | solution.py:538

commit v6 on v5

--- a/solution.py
+++ b/solution.py
@@ -166,8 +166,8 @@
 
     def put(part, north, south):
         even = is_even("gy", north.shape)
-        first_out[part, :] = jnp.where(even, north, south)
-        second_out[part, :] = jnp.where(even, south, north)
+        first_out[part, :] = jnp.where(even, south, north)
+        second_out[part, :] = jnp.where(even, north, south)
 
     def summed(side, f, row, sign):
         depth = level[row : row + 1, :]
@@ -218,8 +218,8 @@
     north, south = [], []
     for part in Message(count).surface:
         even = is_even("gy", (8, width))
-        north.append(jnp.where(even, first_row[part, :], second_row[part, :]))
-        south.append(jnp.where(even, second_row[part, :], first_row[part, :]))
+        north.append(jnp.where(even, second_row[part, :], first_row[part, :]))
+        south.append(jnp.where(even, first_row[part, :], second_row[part, :]))
     eta_ext = extended(eta_ref[...], sides.eta, north, south, 0)
     level_ext = extended(level, sides.depth, north, south, 4)
     level_out[...] = level_ext
@@ -276,8 +276,8 @@
 
 def column_kernel(
     tracer_ref, u_ref, v_ref, bar_ref,
-    own_ref, first_ref, second_ref, c_rows, v_row, first_row, second_row, level_ref,
-    base_out, flow_out,
+    own_ref, first_ref, second_ref, c_rows, v_row, first_row, second_row, level_ref, basis_ref,
+    base_out, share_out,
     side_ref, turn_ref, ratio_ref, slope_ref, value_ref, adjoint_ref,
 ):
     count, height, width = u_ref.shape
@@ -291,11 +291,11 @@
 
     def from_north(part):
         even = is_even("gy", (part.stop - part.start, width))
-        return jnp.where(even, first_row[part, :], second_row[part, :])
+        return jnp.where(even, second_row[part, :], first_row[part, :])
 
     def from_south(part):
         even = is_even("gy", (part.stop - part.start, width))
-        return jnp.where(even, second_row[part, :], first_row[part, :])
+        return jnp.where(even, first_row[part, :], second_row[part, :])
 
 
     inner = [sides.inner(f) for f in range(2)]
@@ -427,15 +427,23 @@
     ends_of = [back[f * height : (f + 1) * height, :] for f in range(2)]
     south_line = [side_ref[f, pl.ds(4, count, stride=8), :] for f in range(2)]
     north_line = [side_ref[f, pl.ds(5, count, stride=8), :] for f in range(2)]
+    steps = []
+    for b in range(3):
+        field = basis_ref[b]
+        east = (0.5 * advect_rate) * (field - roll(field, -1, 1))
+        north = (0.5 * advect_rate) * (field - roll(field, -1, 0))
+        around = (field, east, roll(east, 1, 1), north, roll(north, 1, 0))
+        steps.append([cells[:height, :width] for cells in around])
     for k in range(count):
         flow_e = jnp.where(east_depth > k, u_ref[k], 0.0)
         flow_n = jnp.where(north_depth > k, v_ref[k], 0.0)
         ends_flow = roll(edge_flow, -(4 * k + 2), 1)
         low = south_flow[k : k + 1, :]
-        flow_out[0, k] = flow_e
-        flow_out[1, k] = jnp.where(lane == 0, ends_flow, roll(flow_e, 1, 1))
-        flow_out[2, k] = flow_n
-        flow_out[3, k] = jnp.where(row == 0, low, roll(flow_n, 1, 0))
+        flow_w = jnp.where(lane == 0, ends_flow, roll(flow_e, 1, 1))
+        flow_s = jnp.where(row == 0, low, roll(flow_n, 1, 0))
+        for b, (field, east, west, north, south) in enumerate(steps):
+            part = (flow_e * east + flow_w * west) + (flow_n * north + flow_s * south)
+            share_out[b, k] = jnp.where(level > k, field, 0.0) - part
         for f in range(2):
             y = adjoint_ref[f, k]
             ends = roll(ends_of[f], -(4 * k + 2), 1)
@@ -448,24 +456,18 @@
             base_out[f, k] = y - (0.5 * advect_rate) * ((part_e + part_w) + (part_n + part_s))
 
 
-def final_kernel(sums_ref, basis_ref, level_ref, base_ref, flow_ref, tracer_hbm, eta_hbm, tracer_out, eta_out, sems):
+def final_kernel(sums_ref, basis_ref, base_ref, share_ref, tracer_hbm, eta_hbm, tracer_out, eta_out, sems):
     _, count, height, width = base_ref.shape
     y0, y1, y2 = galerkin(jnp.sum(sums_ref[...], axis=0, keepdims=True))
-    eta_ext = y0 * basis_ref[0] + (y1 * basis_ref[1] + y2 * basis_ref[2])
-    eta = eta_ext[:height, :width]
-    level = level_ref[:height, :width]
-    eta_out[...] = eta
+
+    def combined(fields):
+        return y0 * fields[0] + (y1 * fields[1] + y2 * fields[2])
+
+    eta_out[...] = combined([basis_ref[b, :height, :width] for b in range(3)])
     copies = [pltpu.make_async_copy(eta_out, eta_hbm, sems.at[0])]
     copies[0].start()
-    half = 0.5 * advect_rate
-    east = half * (eta_ext - roll(eta_ext, -1, 1))
-    north = half * (eta_ext - roll(eta_ext, -1, 0))
-    west = roll(east, 1, 1)[:height, :width]
-    south = roll(north, 1, 0)[:height, :width]
-    east, north = east[:height, :width], north[:height, :width]
     for k in range(count):
-        part = (flow_ref[0, k] * east + flow_ref[1, k] * west) + (flow_ref[2, k] * north + flow_ref[3, k] * south)
-        share = jnp.where(level > k, eta, 0.0) - part
+        share = combined([share_ref[b, k] for b in range(3)])
         for f in range(2):
             tracer_out[f, k] = base_ref[f, k] + sterics[f] * share
         if (k + 1) % chunk == 0 or k == count - 1:
@@ -526,7 +528,7 @@
     first_msg, second_msg = call(join_rows, [message, message], "join_rows")(
         level, eta, own, first, second, c_rows, n_rows, u_rows, b_rows, v_row
     )
-    first_row, second_row = swap(first_msg, "gy", 0, False), swap(second_msg, "gy", 1, False)
+    first_row, second_row = swap(first_msg, "gy", 1, False), swap(second_msg, "gy", 0, False)
     ext = (height + 8, 2 * width)
 
     def surface(*refs):
@@ -537,9 +539,9 @@
     )
     all_sums = lax.all_to_all(sums.reshape(devices, 1, width), ("gx", "gy"), 0, 0).reshape(devices, width)
     taller = (count, height + 8, width)
-    base, flows = call(
+    base, shares = call(
         column_kernel,
-        [(2,) + field, (4,) + field],
+        [(2,) + field, (3,) + field],
         "columns",
         None,
         [
@@ -551,7 +553,7 @@
             pltpu.VMEM((2,) + field, F32),
         ],
         pl.CostEstimate(flops=400 * count * height * width, transcendentals=count * height * width, bytes_accessed=1 << 22),
-    )(tracers, uvel, vvel, tracer_bar, own, first, second, c_rows, v_row, first_row, second_row, level_ext)
+    )(tracers, uvel, vvel, tracer_bar, own, first, second, c_rows, v_row, first_row, second_row, level_ext, basis)
     pieces = (count + chunk - 1) // chunk
     tracer_adj, eta_adj = call(
         final_kernel,
@@ -560,7 +562,7 @@
         None,
         [pltpu.VMEM((2,) + field, F32), pltpu.VMEM(tile, F32), pltpu.SemaphoreType.DMA((pieces + 1,))],
         out_spec=HBM,
-    )(all_sums, basis, level_ext, base, flows)
+    )(all_sums, basis, base, shares)
     return (tracer_adj, eta_adj)
 
 

time: 32.1 us -> 30.9 us (0.963)
  starting transfers between devices: 15 us -> 13.7 us
    all_to_all x1, starting transfers between devices: 8.47 us -> 4.28 us  [per_device(): lax.all_to_all(sums.reshape(devices, 1, width), ('gx', 'gy'), 0, 0)]
    ppermute x4, starting transfers between devices: 6.56 us -> 9.39 us  [swap(): return lax.ppermute(cells, axis, pairs)]
    ppermute x4, waiting for transfers between devices: 4.12 us -> 4.5 us  [swap(): return lax.ppermute(cells, axis, pairs)]
  transfers between devices with their start and end apart: 5 -> 5, of which waited for: 3 -> 3; matrix products, arithmetic and copies ran while one was open for 0% -> 0% of each run, Pallas kernels for 12% -> 13%
where the time goes in v6:
time: 30.9 us; the launch traced here: 30.8 us
  starting transfers between devices  13.7 us (44%)
  Pallas kernels  8.77 us (28%)
  waiting for transfers between devices  7.64 us (25%)
  between operations  0.68 us (2%)
    ppermute x4, starting transfers between devices, swap(): return lax.ppermute(cells, axis, pairs)  9.39 us
    pallas_call x6, Pallas kernels, run(): pl.pallas_call(kernel, out_shape=[jax.ShapeDtypeStruct(shape, F32) for sh...  8.77 us
    ppermute x4, waiting for transfers between devices, swap(): return lax.ppermute(cells, axis, pairs)  4.5 us
    all_to_all x1, starting transfers between devices, per_device(): lax.all_to_all(sums.reshape(devices, 1, width), ('gx', 'gy'), 0, 0)  4.28 us
    all_to_all x1, waiting for transfers between devices, per_device(): lax.all_to_all(sums.reshape(devices, 1, width), ('gx', 'gy'), 0, 0)  3.15 us
  transfers between devices with their start and end apart: 5, of which 3 were waited for; matrix products, arithmetic and copies ran while one was open for 0% of the time, Pallas kernels for 13%

profile of v6, /device:TPU:0, one launch (start us, length us, event | category | flops | bytes accessed | tf_op | source)
XLA Modules:
  0.0 30.8 jit_solution(5443580795224101794)
XLA Ops:
  0.6 1.7 %pack_columns.1 = (f32[7,16,128]{2,1,0:T(8,128)S(1)}, f32[16,128]{1,0:T(8,128)S(1)}, f32[16,128]{1,0:T(8,128)S(1)}, f32[2,24,16,128]{3,2,1,0:T(8,128)S(1)}, f32[...) custom-call(s32[16,128]{1,0:T(8,128)} %mask_in.1, s32[16,128]{1,0:T(8,128)} %levels_in.1, ...), custom_call_target="tpu_custom_call" | custom-call | tf_op jit(solution)/shard_map/pack_columns/pallas_call | solution.py:484
  2.4 0.6 %collective-permute-start = (f32[7,16,128]{2,1,0:T(8,128)S(1)}, f32[7,16,128]{2,1,0:T(8,128)S(1)}, u32[]{:S(2)}, u32[]{:S(2)}) collective-permute-start(f32[7,16,128]{2,1,0:T(8,128)S(1)} %get-tuple-element.23.own_ref), channel_id=1, source_target_pairs={{0,4},{4,0},{8,12},{12,8},{16,20},{20,16},{24,28},{28,24},{1,5},{5... | collective-permute-start | bytes 172040 | tf_op jit(solution)/shard_map/ppermute | solution.py:505
  2.9 3.5 %collective-permute-start.1 = (f32[7,16,128]{2,1,0:T(8,128)S(1)}, f32[7,16,128]{2,1,0:T(8,128)S(1)}, u32[]{:S(2)}, u32[]{:S(2)}) collective-permute-start(f32[7,16,128]{2,1,0:T(8,128)S(1)} %get-tuple-element.23.own_ref), channel_id=1, source_target_pairs={{4,8},{8,4},{12,16},{16,12},{20,24},{24,20},{28,0},{0,28},{5,9},{9... | collective-permute-start | bytes 172040 | tf_op jit(solution)/shard_map/ppermute | solution.py:505
  6.5 0.1 pack_rows.1
  6.6 0.0 collective-permute-done.first_ref.refs_2_
  6.6 1.7 %collective-permute-done.1.second_ref.refs_3_ = f32[7,16,128]{2,1,0:T(8,128)S(1)} collective-permute-done((f32[7,16,128]{2,1,0:T(8,128)S(1)}, f32[7,16,128]{2,1,0:T(8,128)S(1)}, u32[]{:S(2)}, u32[]{:S(2)}) %collective-permute-start.1) | collective-permute-done | bytes 57376 | tf_op jit(solution)/shard_map/ppermute | solution.py:505
  8.3 0.3 %join_rows.1 = (f32[192,128]{1,0:T(8,128)S(1)}, f32[192,128]{1,0:T(8,128)S(1)}) custom-call(f32[16,128]{1,0:T(8,128)S(1)} %get-tuple-element.21.level_ref.refs_0_, f32[16,128]{1,0:T(8,128)S(1)} %get-tuple-element.22.eta_ref.refs_1_, f32[7,16,128]{2,1,0:T(8,128)S(1)} %get-tuple-element.23.own_ref, f32[7,16,128]{2,1,0:T(8,128)S(1)} %collective-permute-done.first_ref.refs_2_, ...), custom_call_target="tpu_custom_call" | custom-call | tf_op jit(solution)/shard_map/join_rows/pallas_call | solution.py:484
  8.7 0.7 %collective-permute-start.2 = (f32[192,128]{1,0:T(8,128)S(1)}, f32[192,128]{1,0:T(8,128)S(1)}, u32[]{:S(2)}, u32[]{:S(2)}) collective-permute-start(f32[192,128]{1,0:T(8,128)S(1)} %get-tuple-element.33), channel_id=1, source_target_pairs={{1,2},{2,1},{5,6},{6,5},{9,10},{10,9},{13,14},{14,13},{17,18},{18,... | collective-permute-start | bytes 294920 | tf_op jit(solution)/shard_map/ppermute | solution.py:505
  9.3 4.6 %collective-permute-start.3 = (f32[192,128]{1,0:T(8,128)S(1)}, f32[192,128]{1,0:T(8,128)S(1)}, u32[]{:S(2)}, u32[]{:S(2)}) collective-permute-start(f32[192,128]{1,0:T(8,128)S(1)} %get-tuple-element.34), channel_id=1, source_target_pairs={{0,1},{1,0},{2,3},{3,2},{4,5},{5,4},{6,7},{7,6},{8,9},{9,8},{10,11... | collective-permute-start | bytes 294920 | tf_op jit(solution)/shard_map/ppermute | solution.py:505
  13.9 0.0 collective-permute-done.2.refs_4_.first_row
  14.0 2.8 %collective-permute-done.3.refs_5_.second_row = f32[192,128]{1,0:T(8,128)S(1)} collective-permute-done((f32[192,128]{1,0:T(8,128)S(1)}, f32[192,128]{1,0:T(8,128)S(1)}, u32[]{:S(2)}, u32[]{:S(2)}) %collective-permute-start.3) | collective-permute-done | bytes 98336 | tf_op jit(solution)/shard_map/ppermute | solution.py:505
  16.7 1.1 %surface.1 = (f32[3,24,256]{2,1,0:T(8,128)S(1)}, f32[24,256]{1,0:T(8,128)S(1)}, f32[32,128]{1,0:T(8,128)}) custom-call(f32[16,128]{1,0:T(8,128)S(1)} %get-tuple-element.21.level_ref.refs_0_, f32[16,128]{1,0:T(8,128)S(1)} %get-tuple-element.22.eta_ref.refs_1_, f32[7,16,128]{2,1,0:T(8,128)S(1)} %collective-permute-done.first_ref.refs_2_, ...), custom_call_target="tpu_custom_call" | custom-call | tf_op jit(solution)/shard_map/surface/pallas_call | solution.py:484
  17.8 4.3 %all-to-all-start = ((f32[32,1,128]{2,1,0:T(1,128)}), f32[32,1,128]{2,1,0:T(1,128)S(1)}, u32[]{:S(2)}, u32[]{:S(2)}) async-start(f32[32,1,128]{2,1,0:T(1,128)} %bitcast.1), calls=%async_computation | async-start | bytes 32768 | tf_op jit(solution)/shard_map/all_to_all | solution.py:540
  22.1 4.0 %columns.1 = (f32[2,24,16,128]{3,2,1,0:T(8,128)S(1)}, f32[3,24,16,128]{3,2,1,0:T(8,128)S(1)}) custom-call(f32[2,24,16,128]{3,2,1,0:T(8,128)S(1)} %get-tuple-element.24.tracer_ref, f32[24,16,128]{2,1,0:T(8,128)S(1)} %get-tuple-element.25.u_ref, f32[24,16,128]{2,1,0:T(8,128)S(1)} %get-tuple-element.26.v_ref, f32[2,24,16,128]{3,2,1,0:T(8,128)S(1)} %get-tuple-element.27.bar_ref, ...), custom_call_target="tpu_custom_call" | custom-call | flops 19660800 | bytes 4194304 | tf_op jit(solution)/shard_map/columns/pallas_call | solution.py:484
  26.1 3.1 %all-to-all-done = f32[32,1,128]{2,1,0:T(1,128)S(1)} async-done(((f32[32,1,128]{2,1,0:T(1,128)}), f32[32,1,128]{2,1,0:T(1,128)S(1)}, u32[]{:S(2)}, u32[]{:S(2)}) %all-to-all-start) | async-done | bytes 16416 | tf_op jit(solution)/shard_map/all_to_all | solution.py:540
  29.2 1.6 %finish.1 = (f32[2,24,16,128]{3,2,1,0:T(8,128)}, f32[16,128]{1,0:T(8,128)}) custom-call(f32[32,128]{1,0:T(8,128)S(1)} %bitcast.4, f32[3,24,256]{2,1,0:T(8,128)S(1)} %get-tuple-element.36.basis_ref, f32[2,24,16,128]{3,2,1,0:T(8,128)S(1)} %get-tuple-element.38.base_ref, f32[3,24,16,128]{3,2,1,0:T(8,128)S(1)} %get-tuple-element.39.share_ref), custom_call_target="tpu_custom_call" | custom-call | tf_op jit(solution)/shard_map/finish/pallas_call | solution.py:484
Async XLA Ops:
  2.4 4.2 %collective-permute-start = (f32[7,16,128]{2,1,0:T(8,128)S(1)}, f32[7,16,128]{2,1,0:T(8,128)S(1)}, u32[]{:S(2)}, u32[]{:S(2)}) collective-permute-start(f32[7,16,128]{2,1,0:T(8,128)S(1)} %get-tuple-element.23.own_ref), channel_id=1, source_target_pairs={{0,4},{4,0},{8,12},{12,8},{16,20},{20,16},{24,28},{28,24},{1,5},{5... | collective-permute-start | bytes 172040 | tf_op jit(solution)/shard_map/ppermute | solution.py:505
  2.9 5.4 %collective-permute-start.1 = (f32[7,16,128]{2,1,0:T(8,128)S(1)}, f32[7,16,128]{2,1,0:T(8,128)S(1)}, u32[]{:S(2)}, u32[]{:S(2)}) collective-permute-start(f32[7,16,128]{2,1,0:T(8,128)S(1)} %get-tuple-element.23.own_ref), channel_id=1, source_target_pairs={{4,8},{8,4},{12,16},{16,12},{20,24},{24,20},{28,0},{0,28},{5,9},{9... | collective-permute-start | bytes 172040 | tf_op jit(solution)/shard_map/ppermute | solution.py:505
  8.7 5.3 %collective-permute-start.2 = (f32[192,128]{1,0:T(8,128)S(1)}, f32[192,128]{1,0:T(8,128)S(1)}, u32[]{:S(2)}, u32[]{:S(2)}) collective-permute-start(f32[192,128]{1,0:T(8,128)S(1)} %get-tuple-element.33), channel_id=1, source_target_pairs={{1,2},{2,1},{5,6},{6,5},{9,10},{10,9},{13,14},{14,13},{17,18},{18,... | collective-permute-start | bytes 294920 | tf_op jit(solution)/shard_map/ppermute | solution.py:505
  9.3 7.4 %collective-permute-start.3 = (f32[192,128]{1,0:T(8,128)S(1)}, f32[192,128]{1,0:T(8,128)S(1)}, u32[]{:S(2)}, u32[]{:S(2)}) collective-permute-start(f32[192,128]{1,0:T(8,128)S(1)} %get-tuple-element.34), channel_id=1, source_target_pairs={{0,1},{1,0},{2,3},{3,2},{4,5},{5,4},{6,7},{7,6},{8,9},{9,8},{10,11... | collective-permute-start | bytes 294920 | tf_op jit(solution)/shard_map/ppermute | solution.py:505
  17.8 11.4 %all-to-all-start = ((f32[32,1,128]{2,1,0:T(1,128)}), f32[32,1,128]{2,1,0:T(1,128)S(1)}, u32[]{:S(2)}, u32[]{:S(2)}) async-start(f32[32,1,128]{2,1,0:T(1,128)} %bitcast.1), calls=%async_computation | async-start | bytes 32768 | tf_op jit(solution)/shard_map/all_to_all | solution.py:540

commit v7 on v6

--- a/solution.py
+++ b/solution.py
@@ -20,7 +20,8 @@
 HBM = pl.BlockSpec(memory_space=pltpu.HBM)
 vmem_grant = 8 << 20
 chunk = 6
-U_TILE, V_TILE, BAR_TILE, SURFACE_TILE = 2, 3, 4, 6
+U_TILE, V_TILE, LAST_TILE = 2, 3, 4
+surface_turn = 18
 
 
 def lanes_of(shape):
@@ -56,23 +57,33 @@
     count, height, width = u_ref.shape
     lane = lanes_of((height, width))
     group = lane // 4
-    fields = (
-        (copies[0], tracer_ref.at[0]), (None, tracer_ref.at[1]), (copies[1], u_ref), (copies[2], v_ref),
-        (copies[3], bar_ref.at[0]), (None, bar_ref.at[1]),
-    )
-    for index, (copy, field) in enumerate(fields):
-        if copy is not None:
-            copy.wait()
-        tile = jnp.zeros((height, width), F32)
+    middle = jnp.where((lane % 4 == 1) | (lane % 4 == 2), group, -1)
+    beside = jnp.where((lane + 1) % 4 < 2, (lane + 1) // 4 - 1, -1)
+
+    def gathered(field, place, turn, tile):
         for k in range(count):
-            tile = jnp.where(group == k, roll(field[k], 4 * k + 2, 1), tile)
-        out_ref[index] = tile
+            tile = jnp.where(place == k, roll(field[k], 4 * k + turn, 1), tile)
+        return tile
+
+    empty = jnp.zeros((height, width), F32)
+    copies[0].wait()
+    for f in range(2):
+        out_ref[f] = gathered(tracer_ref.at[f], group, 2, empty)
+    copies[1].wait()
+    out_ref[U_TILE] = gathered(u_ref, group, 2, empty)
+    copies[2].wait()
+    v_tile = gathered(v_ref, middle, 2, empty)
+    copies[3].wait()
+    out_ref[V_TILE] = gathered(bar_ref.at[0], beside, 4, v_tile)
+    last = gathered(bar_ref.at[1], middle, 2, empty)
     for copy in copies[4:]:
         copy.wait()
     level = (mask_ref[...] * levels_ref[...]).astype(F32)
     level_ref[...] = level
     depth = jnp.where(lane < width // 2, roll(level, 3, 1), roll(level, -3, 1))
-    out_ref[SURFACE_TILE] = jnp.where((lane < 3) | (lane >= width - 3), eta_ref[...], depth)
+    surface = roll(jnp.where((lane < 3) | (lane >= width - 3), eta_ref[...], depth), -surface_turn, 1)
+    start = width - 6 - surface_turn
+    out_ref[LAST_TILE] = jnp.where((lane >= start) & (lane < start + 12), surface, last)
 
 
 class Sides:
@@ -84,7 +95,7 @@
         self.lane = lane
         self.layer = (lane // 4).astype(F32)
         self.eastern = lane % 4 == 1
-        east, west = self.pick(SURFACE_TILE)
+        east, west = (roll(tile, surface_turn, 1) for tile in self.pick(LAST_TILE))
         half = lane < self.shape[1] // 2
         self.eta = jnp.where(half, east, west)
         self.depth = jnp.where(half, roll(self.eta, -3, 1), roll(self.eta, 3, 1))
@@ -97,6 +108,10 @@
     def inner(self, tile):
         east, west = self.pick(tile)
         return jnp.where(self.eastern, roll(east, -1, 1), roll(west, 1, 1))
+
+    def bars(self):
+        east, west = self.pick(V_TILE)
+        return [jnp.where(self.eastern, roll(east, -3, 1), roll(west, -1, 1)), self.inner(LAST_TILE)]
 
     def outer(self, tile):
         east, west = self.pick(tile)
@@ -265,11 +280,12 @@
     s22 = k22 - k02 * k02 * i00
     g1 = spread * (d01 * d01 - d00 * d11) * i00
     g2 = spread * (d02 * d01 - d00 * d12) * i00
-    i11 = 1.0 / s11
-    c12 = s12 * i11
-    last = s22 - s12 * c12
-    y2 = jnp.where(last > 4e-7 * s22, (g2 - g1 * c12) / last, 0.0)
-    y1 = (g1 - s12 * y2) * i11
+    product = s11 * s22
+    det = product - s12 * s12
+    full = det > 4e-7 * product
+    inverse = 1.0 / det
+    y2 = jnp.where(full, (s11 * g2 - s12 * g1) * inverse, 0.0)
+    y1 = jnp.where(full, (s22 * g1 - s12 * g2) * inverse, g1 / s11)
     y0 = (d00 - k01 * y1 - k02 * y2) * i00
     return y0, y1, y2
 
@@ -327,7 +343,7 @@
         low_flux = 0.5 * low_flow * (corner_south[f : f + 1, :] + c[:1])
         flux_s = jnp.where(row == 0, low_flux, roll(flux_n, 1, 0))
         beyond.append(c - rate * (outward * (far_flux - edge_flux[f]) + (flux_n - flux_s)))
-    beyond += [sides.inner(BAR_TILE), sides.inner(BAR_TILE + 1), depth_in]
+    beyond += sides.bars() + [depth_in]
     filler = jnp.zeros((width - height * len(beyond), width), F32)
     turned = jnp.transpose(jnp.concatenate(beyond + [filler], axis=0))
 
@@ -514,7 +530,7 @@
     inputs = (sea_mask, levels, eta_bar, tracers, uvel, vvel, tracer_bar)
     own, level, eta, tracers, uvel, vvel, tracer_bar = call(
         pack_columns,
-        [(SURFACE_TILE + 1,) + tile, tile, tile, (2,) + field, field, field, (2,) + field],
+        [(LAST_TILE + 1,) + tile, tile, tile, (2,) + field, field, field, (2,) + field],
         "pack_columns",
         [HBM] * 7,
         [pltpu.VMEM(tile, jnp.int32), pltpu.VMEM(tile, jnp.int32), pltpu.SemaphoreType.DMA((7,))],

time: 30.9 us -> 30.7 us (level)
  Pallas kernels: 8.77 us -> 8.19 us
    all_to_all x1, waiting for transfers between devices: 3.15 us -> 3.78 us  [per_device(): lax.all_to_all(sums.reshape(devices, 1, width), ('gx', 'gy'), 0, 0)]
    pallas_call x6, Pallas kernels: 8.77 us -> 8.19 us  [run(): pl.pallas_call(kernel, out_shape=[jax.ShapeDtypeStruct(shape, F32) for sh...]
    ppermute x4, waiting for transfers between devices: 4.5 us -> 4.14 us  [swap(): return lax.ppermute(cells, axis, pairs)]
  transfers between devices with their start and end apart: 5 -> 5, of which waited for: 3 -> 3; matrix products, arithmetic and copies ran while one was open for 0% -> 0% of each run, Pallas kernels for 13% -> 11%
where the time goes in v7:
time: 30.7 us; the launch traced here: 30.5 us
  starting transfers between devices  13.7 us (45%)
  Pallas kernels  8.19 us (27%)
  waiting for transfers between devices  7.93 us (26%)
  between operations  0.68 us (2%)
    ppermute x4, starting transfers between devices, swap(): return lax.ppermute(cells, axis, pairs)  9.39 us
    pallas_call x6, Pallas kernels, run(): pl.pallas_call(kernel, out_shape=[jax.ShapeDtypeStruct(shape, F32) for sh...  8.19 us
    all_to_all x1, starting transfers between devices, per_device(): lax.all_to_all(sums.reshape(devices, 1, width), ('gx', 'gy'), 0, 0)  4.34 us
    ppermute x4, waiting for transfers between devices, swap(): return lax.ppermute(cells, axis, pairs)  4.14 us
    all_to_all x1, waiting for transfers between devices, per_device(): lax.all_to_all(sums.reshape(devices, 1, width), ('gx', 'gy'), 0, 0)  3.78 us
  transfers between devices with their start and end apart: 5, of which 3 were waited for; matrix products, arithmetic and copies ran while one was open for 0% of the time, Pallas kernels for 11%

profile of v7, /device:TPU:0, one launch (start us, length us, event | category | flops | bytes accessed | tf_op | source)
XLA Modules:
  0.0 30.5 jit_solution(7314726989882708364)
XLA Ops:
  0.6 1.8 %pack_columns.1 = (f32[5,16,128]{2,1,0:T(8,128)S(1)}, f32[16,128]{1,0:T(8,128)S(1)}, f32[16,128]{1,0:T(8,128)S(1)}, f32[2,24,16,128]{3,2,1,0:T(8,128)S(1)}, f32[...) custom-call(s32[16,128]{1,0:T(8,128)} %mask_in.1, s32[16,128]{1,0:T(8,128)} %levels_in.1, ...), custom_call_target="tpu_custom_call" | custom-call | tf_op jit(solution)/shard_map/pack_columns/pallas_call | solution.py:500
  2.4 0.6 %collective-permute-start = (f32[5,16,128]{2,1,0:T(8,128)S(1)}, f32[5,16,128]{2,1,0:T(8,128)S(1)}, u32[]{:S(2)}, u32[]{:S(2)}) collective-permute-start(f32[5,16,128]{2,1,0:T(8,128)S(1)} %get-tuple-element.23.own_ref), channel_id=1, source_target_pairs={{0,4},{4,0},{8,12},{12,8},{16,20},{20,16},{24,28},{28,24},{1,5},{5... | collective-permute-start | bytes 122888 | tf_op jit(solution)/shard_map/ppermute | solution.py:521
  3.0 3.5 %collective-permute-start.1 = (f32[5,16,128]{2,1,0:T(8,128)S(1)}, f32[5,16,128]{2,1,0:T(8,128)S(1)}, u32[]{:S(2)}, u32[]{:S(2)}) collective-permute-start(f32[5,16,128]{2,1,0:T(8,128)S(1)} %get-tuple-element.23.own_ref), channel_id=1, source_target_pairs={{4,8},{8,4},{12,16},{16,12},{20,24},{24,20},{28,0},{0,28},{5,9},{9... | collective-permute-start | bytes 122888 | tf_op jit(solution)/shard_map/ppermute | solution.py:521
  6.5 0.1 pack_rows.1
  6.7 0.0 collective-permute-done.first_ref.refs_2_
  6.7 1.5 %collective-permute-done.1.second_ref.refs_3_ = f32[5,16,128]{2,1,0:T(8,128)S(1)} collective-permute-done((f32[5,16,128]{2,1,0:T(8,128)S(1)}, f32[5,16,128]{2,1,0:T(8,128)S(1)}, u32[]{:S(2)}, u32[]{:S(2)}) %collective-permute-start.1) | collective-permute-done | bytes 40992 | tf_op jit(solution)/shard_map/ppermute | solution.py:521
  8.2 0.4 %join_rows.1 = (f32[192,128]{1,0:T(8,128)S(1)}, f32[192,128]{1,0:T(8,128)S(1)}) custom-call(f32[16,128]{1,0:T(8,128)S(1)} %get-tuple-element.21.level_ref.refs_0_, f32[16,128]{1,0:T(8,128)S(1)} %get-tuple-element.22.eta_ref.refs_1_, f32[5,16,128]{2,1,0:T(8,128)S(1)} %get-tuple-element.23.own_ref, f32[5,16,128]{2,1,0:T(8,128)S(1)} %collective-permute-done.first_ref.refs_2_, ...), custom_call_target="tpu_custom_call" | custom-call | tf_op jit(solution)/shard_map/join_rows/pallas_call | solution.py:500
  8.6 0.7 %collective-permute-start.2 = (f32[192,128]{1,0:T(8,128)S(1)}, f32[192,128]{1,0:T(8,128)S(1)}, u32[]{:S(2)}, u32[]{:S(2)}) collective-permute-start(f32[192,128]{1,0:T(8,128)S(1)} %get-tuple-element.33), channel_id=1, source_target_pairs={{1,2},{2,1},{5,6},{6,5},{9,10},{10,9},{13,14},{14,13},{17,18},{18,... | collective-permute-start | bytes 294920 | tf_op jit(solution)/shard_map/ppermute | solution.py:521
  9.3 4.6 %collective-permute-start.3 = (f32[192,128]{1,0:T(8,128)S(1)}, f32[192,128]{1,0:T(8,128)S(1)}, u32[]{:S(2)}, u32[]{:S(2)}) collective-permute-start(f32[192,128]{1,0:T(8,128)S(1)} %get-tuple-element.34), channel_id=1, source_target_pairs={{0,1},{1,0},{2,3},{3,2},{4,5},{5,4},{6,7},{7,6},{8,9},{9,8},{10,11... | collective-permute-start | bytes 294920 | tf_op jit(solution)/shard_map/ppermute | solution.py:521
  13.9 0.0 collective-permute-done.2.refs_4_.first_row
  13.9 2.6 %collective-permute-done.3.refs_5_.second_row = f32[192,128]{1,0:T(8,128)S(1)} collective-permute-done((f32[192,128]{1,0:T(8,128)S(1)}, f32[192,128]{1,0:T(8,128)S(1)}, u32[]{:S(2)}, u32[]{:S(2)}) %collective-permute-start.3) | collective-permute-done | bytes 98336 | tf_op jit(solution)/shard_map/ppermute | solution.py:521
  16.5 1.1 %surface.1 = (f32[3,24,256]{2,1,0:T(8,128)S(1)}, f32[24,256]{1,0:T(8,128)S(1)}, f32[32,128]{1,0:T(8,128)}) custom-call(f32[16,128]{1,0:T(8,128)S(1)} %get-tuple-element.21.level_ref.refs_0_, f32[16,128]{1,0:T(8,128)S(1)} %get-tuple-element.22.eta_ref.refs_1_, f32[5,16,128]{2,1,0:T(8,128)S(1)} %collective-permute-done.first_ref.refs_2_, ...), custom_call_target="tpu_custom_call" | custom-call | tf_op jit(solution)/shard_map/surface/pallas_call | solution.py:500
  17.6 4.3 %all-to-all-start = ((f32[32,1,128]{2,1,0:T(1,128)}), f32[32,1,128]{2,1,0:T(1,128)S(1)}, u32[]{:S(2)}, u32[]{:S(2)}) async-start(f32[32,1,128]{2,1,0:T(1,128)} %bitcast.1), calls=%async_computation | async-start | bytes 32768 | tf_op jit(solution)/shard_map/all_to_all | solution.py:556
  22.0 3.3 %columns.1 = (f32[2,24,16,128]{3,2,1,0:T(8,128)S(1)}, f32[3,24,16,128]{3,2,1,0:T(8,128)S(1)}) custom-call(f32[2,24,16,128]{3,2,1,0:T(8,128)S(1)} %get-tuple-element.24.tracer_ref, f32[24,16,128]{2,1,0:T(8,128)S(1)} %get-tuple-element.25.u_ref, f32[24,16,128]{2,1,0:T(8,128)S(1)} %get-tuple-element.26.v_ref, f32[2,24,16,128]{3,2,1,0:T(8,128)S(1)} %get-tuple-element.27.bar_ref, ...), custom_call_target="tpu_custom_call" | custom-call | flops 19660800 | bytes 4194304 | tf_op jit(solution)/shard_map/columns/pallas_call | solution.py:500
  25.3 3.8 %all-to-all-done = f32[32,1,128]{2,1,0:T(1,128)S(1)} async-done(((f32[32,1,128]{2,1,0:T(1,128)}), f32[32,1,128]{2,1,0:T(1,128)S(1)}, u32[]{:S(2)}, u32[]{:S(2)}) %all-to-all-start) | async-done | bytes 16416 | tf_op jit(solution)/shard_map/all_to_all | solution.py:556
  29.1 1.4 %finish.1 = (f32[2,24,16,128]{3,2,1,0:T(8,128)}, f32[16,128]{1,0:T(8,128)}) custom-call(f32[32,128]{1,0:T(8,128)S(1)} %bitcast.4, f32[3,24,256]{2,1,0:T(8,128)S(1)} %get-tuple-element.36.basis_ref, f32[2,24,16,128]{3,2,1,0:T(8,128)S(1)} %get-tuple-element.38.base_ref, f32[3,24,16,128]{3,2,1,0:T(8,128)S(1)} %get-tuple-element.39.share_ref), custom_call_target="tpu_custom_call" | custom-call | tf_op jit(solution)/shard_map/finish/pallas_call | solution.py:500
Async XLA Ops:
  2.4 4.2 %collective-permute-start = (f32[5,16,128]{2,1,0:T(8,128)S(1)}, f32[5,16,128]{2,1,0:T(8,128)S(1)}, u32[]{:S(2)}, u32[]{:S(2)}) collective-permute-start(f32[5,16,128]{2,1,0:T(8,128)S(1)} %get-tuple-element.23.own_ref), channel_id=1, source_target_pairs={{0,4},{4,0},{8,12},{12,8},{16,20},{20,16},{24,28},{28,24},{1,5},{5... | collective-permute-start | bytes 122888 | tf_op jit(solution)/shard_map/ppermute | solution.py:521
  3.0 5.2 %collective-permute-start.1 = (f32[5,16,128]{2,1,0:T(8,128)S(1)}, f32[5,16,128]{2,1,0:T(8,128)S(1)}, u32[]{:S(2)}, u32[]{:S(2)}) collective-permute-start(f32[5,16,128]{2,1,0:T(8,128)S(1)} %get-tuple-element.23.own_ref), channel_id=1, source_target_pairs={{4,8},{8,4},{12,16},{16,12},{20,24},{24,20},{28,0},{0,28},{5,9},{9... | collective-permute-start | bytes 122888 | tf_op jit(solution)/shard_map/ppermute | solution.py:521
  8.6 5.3 %collective-permute-start.2 = (f32[192,128]{1,0:T(8,128)S(1)}, f32[192,128]{1,0:T(8,128)S(1)}, u32[]{:S(2)}, u32[]{:S(2)}) collective-permute-start(f32[192,128]{1,0:T(8,128)S(1)} %get-tuple-element.33), channel_id=1, source_target_pairs={{1,2},{2,1},{5,6},{6,5},{9,10},{10,9},{13,14},{14,13},{17,18},{18,... | collective-permute-start | bytes 294920 | tf_op jit(solution)/shard_map/ppermute | solution.py:521
  9.3 7.2 %collective-permute-start.3 = (f32[192,128]{1,0:T(8,128)S(1)}, f32[192,128]{1,0:T(8,128)S(1)}, u32[]{:S(2)}, u32[]{:S(2)}) collective-permute-start(f32[192,128]{1,0:T(8,128)S(1)} %get-tuple-element.34), channel_id=1, source_target_pairs={{0,1},{1,0},{2,3},{3,2},{4,5},{5,4},{6,7},{7,6},{8,9},{9,8},{10,11... | collective-permute-start | bytes 294920 | tf_op jit(solution)/shard_map/ppermute | solution.py:521
  17.6 11.5 %all-to-all-start = ((f32[32,1,128]{2,1,0:T(1,128)}), f32[32,1,128]{2,1,0:T(1,128)S(1)}, u32[]{:S(2)}, u32[]{:S(2)}) async-start(f32[32,1,128]{2,1,0:T(1,128)} %bitcast.1), calls=%async_computation | async-start | bytes 32768 | tf_op jit(solution)/shard_map/all_to_all | solution.py:556

commit v8 on v7

--- a/solution.py
+++ b/solution.py
@@ -223,6 +223,10 @@
     return jnp.concatenate(parts, axis=1)
 
 
+pairs = ((0, 0), (0, 1), (0, 2), (1, 1), (1, 2), (2, 2), (2, 3))
+centers = ((0.0, 0.25), (1.0, 0.25), (2.0, -0.25))
+
+
 def surface_kernel(
     level_ref, eta_ref, first_ref, second_ref, first_row, second_row,
     basis_out, level_out, sums_out, *, count,
@@ -249,45 +253,66 @@
         along_y = north_weight * (field - roll(field, -1, 0)) + south_weight * (field - roll(field, 1, 0))
         return along_x + along_y
 
-    first = scaled(eta_ext)
-    second = scaled(first) - first
-    third = scaled(second)
-    basis_out[0] = eta_ext
-    basis_out[1] = first
-    basis_out[2] = second
-    vectors = [x[:height, :width] for x in (eta_ext, first, second, third)]
-    pairs = ((0, 0), (0, 1), (0, 2), (1, 1), (1, 2), (2, 2), (2, 3))
+    powers = [eta_ext]
+    for _ in range(3):
+        powers.append(scaled(powers[-1]))
+    for index in range(3):
+        basis_out[index] = powers[index]
+    powers = [x[:height, :width] for x in powers]
+    table = []
     row = rows_of((8, width))
-    table = jnp.zeros((8, width), F32)
-    for index, (a, b) in enumerate(pairs):
-        table = jnp.where(row == index, jnp.sum(vectors[a] * vectors[b], axis=0, keepdims=True), table)
+    for center, tilt in centers:
+        one, two, three = powers[1:]
+        if center:
+            moved = [x - center * y for x, y in zip(powers[1:], powers)]
+            twice = [x - center * y for x, y in zip(moved[1:], moved)]
+            one, two, three = moved[0], twice[0], twice[1] - center * twice[0]
+        vectors = (powers[0], one, two - tilt * one, three - tilt * two)
+        part = jnp.zeros((8, width), F32)
+        for index, (i, j) in enumerate(pairs):
+            part = jnp.where(row == index, jnp.sum(vectors[i] * vectors[j], axis=0, keepdims=True), part)
+        table.append(part)
+    table = jnp.concatenate(table, axis=0)
     totals = jnp.sum(table, axis=1, keepdims=True)
-    line = jnp.sum(jnp.where(lanes_of((8, width)) == row, totals, 0.0), axis=0, keepdims=True)
+    place = lanes_of(table.shape) == rows_of(table.shape)
+    line = jnp.sum(jnp.where(place, totals, 0.0), axis=0, keepdims=True)
     sums_out[...] = jnp.broadcast_to(line, sums_out.shape)
 
 
 def galerkin(sums):
-    d00, d01, d02, d11, d12, d22, d2q = [sums[:, i : i + 1] for i in range(7)]
-    k00 = d00 + spread * d01
-    k01 = d01 + spread * d11
-    k02 = d02 + spread * d12
-    k11 = d11 + spread * (d11 + d12)
-    k12 = d12 + spread * (d12 + d22)
-    k22 = d22 + spread * d2q
+    mean, square = sums[:, 1:2], sums[:, 0:1]
+    center = jnp.zeros_like(mean)
+    tilt = jnp.full_like(mean, centers[0][1])
+    chosen = sums
+    for index in range(1, len(centers)):
+        here = mean > 0.5 * (centers[index - 1][0] + centers[index][0]) * square
+        center = jnp.where(here, centers[index][0], center)
+        tilt = jnp.where(here, centers[index][1], tilt)
+        chosen = jnp.where(here, roll(sums, -8 * index, 1), chosen)
+    d00, d01, d02, d11, d12, d22, d2q = [chosen[:, i : i + 1] for i in range(7)]
+    base = 1.0 + spread * center
+    k00 = base * d00 + spread * d01
+    k01 = base * d01 + spread * d11
+    k02 = base * d02 + spread * d12
+    k11 = base * d11 + spread * (tilt * d11 + d12)
+    k12 = base * d12 + spread * (tilt * d12 + d22)
+    k22 = base * d22 + spread * d2q
     i00 = 1.0 / k00
     s11 = k11 - k01 * k01 * i00
     s12 = k12 - k01 * k02 * i00
     s22 = k22 - k02 * k02 * i00
     g1 = spread * (d01 * d01 - d00 * d11) * i00
     g2 = spread * (d02 * d01 - d00 * d12) * i00
-    product = s11 * s22
-    det = product - s12 * s12
-    full = det > 4e-7 * product
-    inverse = 1.0 / det
-    y2 = jnp.where(full, (s11 * g2 - s12 * g1) * inverse, 0.0)
-    y1 = jnp.where(full, (s22 * g1 - s12 * g2) * inverse, g1 / s11)
+    second = s11 > 1e-7 * k11
+    i11 = jnp.where(second, 1.0 / s11, 0.0)
+    c12 = s12 * i11
+    last = s22 - s12 * c12
+    third = second & (last > 4e-7 * s22)
+    y2 = jnp.where(third, (g2 - g1 * c12) / last, 0.0)
+    y1 = (g1 - s12 * y2) * i11
     y0 = (d00 - k01 * y1 - k02 * y2) * i00
-    return y0, y1, y2
+    inner = center + tilt
+    return y0 - center * y1 + center * inner * y2, y1 - (center + inner) * y2, y2
 
 
 def column_kernel(

time: 30.7 us -> 30.6 us (level)
  no operation moved by 1% of the time
where the time goes in v8:
time: 30.6 us; the launch traced here: 30.5 us
  starting transfers between devices  13.7 us (45%)
  Pallas kernels  8.13 us (27%)
  waiting for transfers between devices  7.93 us (26%)
  between operations  0.68 us (2%)
    ppermute x4, starting transfers between devices, swap(): return lax.ppermute(cells, axis, pairs)  9.39 us
    pallas_call x6, Pallas kernels, run(): pl.pallas_call(kernel, out_shape=[jax.ShapeDtypeStruct(shape, F32) for sh...  8.13 us
    all_to_all x1, starting transfers between devices, per_device(): lax.all_to_all(sums.reshape(devices, 1, width), ('gx', 'gy'), 0, 0)  4.34 us
    ppermute x4, waiting for transfers between devices, swap(): return lax.ppermute(cells, axis, pairs)  4.14 us
    all_to_all x1, waiting for transfers between devices, per_device(): lax.all_to_all(sums.reshape(devices, 1, width), ('gx', 'gy'), 0, 0)  3.78 us
  transfers between devices with their start and end apart: 5, of which 3 were waited for; matrix products, arithmetic and copies ran while one was open for 0% of the time, Pallas kernels for 11%

profile of v8, /device:TPU:0, one launch (start us, length us, event | category | flops | bytes accessed | tf_op | source)
XLA Modules:
  0.0 30.5 jit_solution(11984438558807251043)
XLA Ops:
  0.6 1.8 %pack_columns.1 = (f32[5,16,128]{2,1,0:T(8,128)S(1)}, f32[16,128]{1,0:T(8,128)S(1)}, f32[16,128]{1,0:T(8,128)S(1)}, f32[2,24,16,128]{3,2,1,0:T(8,128)S(1)}, f32[...) custom-call(s32[16,128]{1,0:T(8,128)} %mask_in.1, s32[16,128]{1,0:T(8,128)} %levels_in.1, ...), custom_call_target="tpu_custom_call" | custom-call | tf_op jit(solution)/shard_map/pack_columns/pallas_call | solution.py:525
  2.4 0.6 %collective-permute-start = (f32[5,16,128]{2,1,0:T(8,128)S(1)}, f32[5,16,128]{2,1,0:T(8,128)S(1)}, u32[]{:S(2)}, u32[]{:S(2)}) collective-permute-start(f32[5,16,128]{2,1,0:T(8,128)S(1)} %get-tuple-element.23.own_ref), channel_id=1, source_target_pairs={{0,4},{4,0},{8,12},{12,8},{16,20},{20,16},{24,28},{28,24},{1,5},{5... | collective-permute-start | bytes 122888 | tf_op jit(solution)/shard_map/ppermute | solution.py:546
  3.0 3.5 %collective-permute-start.1 = (f32[5,16,128]{2,1,0:T(8,128)S(1)}, f32[5,16,128]{2,1,0:T(8,128)S(1)}, u32[]{:S(2)}, u32[]{:S(2)}) collective-permute-start(f32[5,16,128]{2,1,0:T(8,128)S(1)} %get-tuple-element.23.own_ref), channel_id=1, source_target_pairs={{4,8},{8,4},{12,16},{16,12},{20,24},{24,20},{28,0},{0,28},{5,9},{9... | collective-permute-start | bytes 122888 | tf_op jit(solution)/shard_map/ppermute | solution.py:546
  6.5 0.1 pack_rows.1
  6.7 0.0 collective-permute-done.first_ref.refs_2_
  6.7 1.5 %collective-permute-done.1.second_ref.refs_3_ = f32[5,16,128]{2,1,0:T(8,128)S(1)} collective-permute-done((f32[5,16,128]{2,1,0:T(8,128)S(1)}, f32[5,16,128]{2,1,0:T(8,128)S(1)}, u32[]{:S(2)}, u32[]{:S(2)}) %collective-permute-start.1) | collective-permute-done | bytes 40992 | tf_op jit(solution)/shard_map/ppermute | solution.py:546
  8.2 0.4 %join_rows.1 = (f32[192,128]{1,0:T(8,128)S(1)}, f32[192,128]{1,0:T(8,128)S(1)}) custom-call(f32[16,128]{1,0:T(8,128)S(1)} %get-tuple-element.21.level_ref.refs_0_, f32[16,128]{1,0:T(8,128)S(1)} %get-tuple-element.22.eta_ref.refs_1_, f32[5,16,128]{2,1,0:T(8,128)S(1)} %get-tuple-element.23.own_ref, f32[5,16,128]{2,1,0:T(8,128)S(1)} %collective-permute-done.first_ref.refs_2_, ...), custom_call_target="tpu_custom_call" | custom-call | tf_op jit(solution)/shard_map/join_rows/pallas_call | solution.py:525
  8.6 0.7 %collective-permute-start.2 = (f32[192,128]{1,0:T(8,128)S(1)}, f32[192,128]{1,0:T(8,128)S(1)}, u32[]{:S(2)}, u32[]{:S(2)}) collective-permute-start(f32[192,128]{1,0:T(8,128)S(1)} %get-tuple-element.33), channel_id=1, source_target_pairs={{1,2},{2,1},{5,6},{6,5},{9,10},{10,9},{13,14},{14,13},{17,18},{18,... | collective-permute-start | bytes 294920 | tf_op jit(solution)/shard_map/ppermute | solution.py:546
  9.3 4.6 %collective-permute-start.3 = (f32[192,128]{1,0:T(8,128)S(1)}, f32[192,128]{1,0:T(8,128)S(1)}, u32[]{:S(2)}, u32[]{:S(2)}) collective-permute-start(f32[192,128]{1,0:T(8,128)S(1)} %get-tuple-element.34), channel_id=1, source_target_pairs={{0,1},{1,0},{2,3},{3,2},{4,5},{5,4},{6,7},{7,6},{8,9},{9,8},{10,11... | collective-permute-start | bytes 294920 | tf_op jit(solution)/shard_map/ppermute | solution.py:546
  13.9 0.0 collective-permute-done.2.refs_4_.first_row
  13.9 2.6 %collective-permute-done.3.refs_5_.second_row = f32[192,128]{1,0:T(8,128)S(1)} collective-permute-done((f32[192,128]{1,0:T(8,128)S(1)}, f32[192,128]{1,0:T(8,128)S(1)}, u32[]{:S(2)}, u32[]{:S(2)}) %collective-permute-start.3) | collective-permute-done | bytes 98336 | tf_op jit(solution)/shard_map/ppermute | solution.py:546
  16.5 1.2 %surface.1 = (f32[3,24,256]{2,1,0:T(8,128)S(1)}, f32[24,256]{1,0:T(8,128)S(1)}, f32[32,128]{1,0:T(8,128)}) custom-call(f32[16,128]{1,0:T(8,128)S(1)} %get-tuple-element.21.level_ref.refs_0_, f32[16,128]{1,0:T(8,128)S(1)} %get-tuple-element.22.eta_ref.refs_1_, f32[5,16,128]{2,1,0:T(8,128)S(1)} %collective-permute-done.first_ref.refs_2_, ...), custom_call_target="tpu_custom_call" | custom-call | tf_op jit(solution)/shard_map/surface/pallas_call | solution.py:525
  17.6 4.3 %all-to-all-start = ((f32[32,1,128]{2,1,0:T(1,128)}), f32[32,1,128]{2,1,0:T(1,128)S(1)}, u32[]{:S(2)}, u32[]{:S(2)}) async-start(f32[32,1,128]{2,1,0:T(1,128)} %bitcast.1), calls=%async_computation | async-start | bytes 32768 | tf_op jit(solution)/shard_map/all_to_all | solution.py:581
  22.0 3.3 %columns.1 = (f32[2,24,16,128]{3,2,1,0:T(8,128)S(1)}, f32[3,24,16,128]{3,2,1,0:T(8,128)S(1)}) custom-call(f32[2,24,16,128]{3,2,1,0:T(8,128)S(1)} %get-tuple-element.24.tracer_ref, f32[24,16,128]{2,1,0:T(8,128)S(1)} %get-tuple-element.25.u_ref, f32[24,16,128]{2,1,0:T(8,128)S(1)} %get-tuple-element.26.v_ref, f32[2,24,16,128]{3,2,1,0:T(8,128)S(1)} %get-tuple-element.27.bar_ref, ...), custom_call_target="tpu_custom_call" | custom-call | flops 19660800 | bytes 4194304 | tf_op jit(solution)/shard_map/columns/pallas_call | solution.py:525
  25.3 3.8 %all-to-all-done = f32[32,1,128]{2,1,0:T(1,128)S(1)} async-done(((f32[32,1,128]{2,1,0:T(1,128)}), f32[32,1,128]{2,1,0:T(1,128)S(1)}, u32[]{:S(2)}, u32[]{:S(2)}) %all-to-all-start) | async-done | bytes 16416 | tf_op jit(solution)/shard_map/all_to_all | solution.py:581
  29.1 1.3 %finish.1 = (f32[2,24,16,128]{3,2,1,0:T(8,128)}, f32[16,128]{1,0:T(8,128)}) custom-call(f32[32,128]{1,0:T(8,128)S(1)} %bitcast.4, f32[3,24,256]{2,1,0:T(8,128)S(1)} %get-tuple-element.36.basis_ref, f32[2,24,16,128]{3,2,1,0:T(8,128)S(1)} %get-tuple-element.38.base_ref, f32[3,24,16,128]{3,2,1,0:T(8,128)S(1)} %get-tuple-element.39.share_ref), custom_call_target="tpu_custom_call" | custom-call | tf_op jit(solution)/shard_map/finish/pallas_call | solution.py:525
Async XLA Ops:
  2.4 4.2 %collective-permute-start = (f32[5,16,128]{2,1,0:T(8,128)S(1)}, f32[5,16,128]{2,1,0:T(8,128)S(1)}, u32[]{:S(2)}, u32[]{:S(2)}) collective-permute-start(f32[5,16,128]{2,1,0:T(8,128)S(1)} %get-tuple-element.23.own_ref), channel_id=1, source_target_pairs={{0,4},{4,0},{8,12},{12,8},{16,20},{20,16},{24,28},{28,24},{1,5},{5... | collective-permute-start | bytes 122888 | tf_op jit(solution)/shard_map/ppermute | solution.py:546
  3.0 5.2 %collective-permute-start.1 = (f32[5,16,128]{2,1,0:T(8,128)S(1)}, f32[5,16,128]{2,1,0:T(8,128)S(1)}, u32[]{:S(2)}, u32[]{:S(2)}) collective-permute-start(f32[5,16,128]{2,1,0:T(8,128)S(1)} %get-tuple-element.23.own_ref), channel_id=1, source_target_pairs={{4,8},{8,4},{12,16},{16,12},{20,24},{24,20},{28,0},{0,28},{5,9},{9... | collective-permute-start | bytes 122888 | tf_op jit(solution)/shard_map/ppermute | solution.py:546
  8.6 5.3 %collective-permute-start.2 = (f32[192,128]{1,0:T(8,128)S(1)}, f32[192,128]{1,0:T(8,128)S(1)}, u32[]{:S(2)}, u32[]{:S(2)}) collective-permute-start(f32[192,128]{1,0:T(8,128)S(1)} %get-tuple-element.33), channel_id=1, source_target_pairs={{1,2},{2,1},{5,6},{6,5},{9,10},{10,9},{13,14},{14,13},{17,18},{18,... | collective-permute-start | bytes 294920 | tf_op jit(solution)/shard_map/ppermute | solution.py:546
  9.3 7.2 %collective-permute-start.3 = (f32[192,128]{1,0:T(8,128)S(1)}, f32[192,128]{1,0:T(8,128)S(1)}, u32[]{:S(2)}, u32[]{:S(2)}) collective-permute-start(f32[192,128]{1,0:T(8,128)S(1)} %get-tuple-element.34), channel_id=1, source_target_pairs={{0,1},{1,0},{2,3},{3,2},{4,5},{5,4},{6,7},{7,6},{8,9},{9,8},{10,11... | collective-permute-start | bytes 294920 | tf_op jit(solution)/shard_map/ppermute | solution.py:546
  17.6 11.5 %all-to-all-start = ((f32[32,1,128]{2,1,0:T(1,128)}), f32[32,1,128]{2,1,0:T(1,128)S(1)}, u32[]{:S(2)}, u32[]{:S(2)}) async-start(f32[32,1,128]{2,1,0:T(1,128)} %bitcast.1), calls=%async_computation | async-start | bytes 32768 | tf_op jit(solution)/shard_map/all_to_all | solution.py:581

commit v9 on v8

--- a/solution.py
+++ b/solution.py
@@ -280,16 +280,16 @@
 
 
 def galerkin(sums):
-    mean, square = sums[:, 1:2], sums[:, 0:1]
-    center = jnp.zeros_like(mean)
-    tilt = jnp.full_like(mean, centers[0][1])
-    chosen = sums
+    lane = lanes_of(sums.shape)
+    d00, d01, d02, d11, d12, d22, d2q = [roll(sums, -i, 1) for i in range(7)]
+    mean, square = d01[:, :1], d00[:, :1]
+    place = jnp.zeros(mean.shape, jnp.int32)
+    center = jnp.full(sums.shape, centers[0][0], F32)
+    tilt = jnp.full(sums.shape, centers[0][1], F32)
     for index in range(1, len(centers)):
-        here = mean > 0.5 * (centers[index - 1][0] + centers[index][0]) * square
-        center = jnp.where(here, centers[index][0], center)
-        tilt = jnp.where(here, centers[index][1], tilt)
-        chosen = jnp.where(here, roll(sums, -8 * index, 1), chosen)
-    d00, d01, d02, d11, d12, d22, d2q = [chosen[:, i : i + 1] for i in range(7)]
+        place = jnp.where(mean > 0.5 * (centers[index - 1][0] + centers[index][0]) * square, 8 * index, place)
+        center = jnp.where(lane == 8 * index, centers[index][0], center)
+        tilt = jnp.where(lane == 8 * index, centers[index][1], tilt)
     base = 1.0 + spread * center
     k00 = base * d00 + spread * d01
     k01 = base * d01 + spread * d11
@@ -312,7 +312,8 @@
     y1 = (g1 - s12 * y2) * i11
     y0 = (d00 - k01 * y1 - k02 * y2) * i00
     inner = center + tilt
-    return y0 - center * y1 + center * inner * y2, y1 - (center + inner) * y2, y2
+    results = (y0 - center * y1 + center * inner * y2, y1 - (center + inner) * y2, y2)
+    return [jnp.sum(jnp.where(lane == place, y, 0.0), axis=1, keepdims=True) for y in results]
 
 
 def column_kernel(

time: 30.6 us -> 30.3 us (level)
  Pallas kernels: 8.13 us -> 7.82 us
    pallas_call x6, Pallas kernels: 8.13 us -> 7.82 us  [run(): pl.pallas_call(kernel, out_shape=[jax.ShapeDtypeStruct(shape, F32) for sh...]
  transfers between devices with their start and end apart: 5 -> 5, of which waited for: 3 -> 3; matrix products, arithmetic and copies ran while one was open for 0% -> 0% of each run, Pallas kernels for 11% -> 12%
where the time goes in v9:
time: 30.3 us; the launch traced here: 30.1 us
  starting transfers between devices  13.7 us (45%)
  waiting for transfers between devices  7.93 us (26%)
  Pallas kernels  7.82 us (26%)
  between operations  0.68 us (2%)
    ppermute x4, starting transfers between devices, swap(): return lax.ppermute(cells, axis, pairs)  9.39 us
    pallas_call x6, Pallas kernels, run(): pl.pallas_call(kernel, out_shape=[jax.ShapeDtypeStruct(shape, F32) for sh...  7.82 us
    all_to_all x1, starting transfers between devices, per_device(): lax.all_to_all(sums.reshape(devices, 1, width), ('gx', 'gy'), 0, 0)  4.34 us
    ppermute x4, waiting for transfers between devices, swap(): return lax.ppermute(cells, axis, pairs)  4.14 us
    all_to_all x1, waiting for transfers between devices, per_device(): lax.all_to_all(sums.reshape(devices, 1, width), ('gx', 'gy'), 0, 0)  3.78 us
  transfers between devices with their start and end apart: 5, of which 3 were waited for; matrix products, arithmetic and copies ran while one was open for 0% of the time, Pallas kernels for 12%

profile of v9, /device:TPU:0, one launch (start us, length us, event | category | flops | bytes accessed | tf_op | source)
XLA Modules:
  0.0 30.1 jit_solution(6653765097108569799)
XLA Ops:
  0.6 1.8 %pack_columns.1 = (f32[5,16,128]{2,1,0:T(8,128)S(1)}, f32[16,128]{1,0:T(8,128)S(1)}, f32[16,128]{1,0:T(8,128)S(1)}, f32[2,24,16,128]{3,2,1,0:T(8,128)S(1)}, f32[...) custom-call(s32[16,128]{1,0:T(8,128)} %mask_in.1, s32[16,128]{1,0:T(8,128)} %levels_in.1, ...), custom_call_target="tpu_custom_call" | custom-call | tf_op jit(solution)/shard_map/pack_columns/pallas_call | solution.py:526
  2.4 0.6 %collective-permute-start = (f32[5,16,128]{2,1,0:T(8,128)S(1)}, f32[5,16,128]{2,1,0:T(8,128)S(1)}, u32[]{:S(2)}, u32[]{:S(2)}) collective-permute-start(f32[5,16,128]{2,1,0:T(8,128)S(1)} %get-tuple-element.23.own_ref), channel_id=1, source_target_pairs={{0,4},{4,0},{8,12},{12,8},{16,20},{20,16},{24,28},{28,24},{1,5},{5... | collective-permute-start | bytes 122888 | tf_op jit(solution)/shard_map/ppermute | solution.py:547
  3.0 3.5 %collective-permute-start.1 = (f32[5,16,128]{2,1,0:T(8,128)S(1)}, f32[5,16,128]{2,1,0:T(8,128)S(1)}, u32[]{:S(2)}, u32[]{:S(2)}) collective-permute-start(f32[5,16,128]{2,1,0:T(8,128)S(1)} %get-tuple-element.23.own_ref), channel_id=1, source_target_pairs={{4,8},{8,4},{12,16},{16,12},{20,24},{24,20},{28,0},{0,28},{5,9},{9... | collective-permute-start | bytes 122888 | tf_op jit(solution)/shard_map/ppermute | solution.py:547
  6.5 0.1 pack_rows.1
  6.7 0.0 collective-permute-done.first_ref.refs_2_
  6.7 1.5 %collective-permute-done.1.second_ref.refs_3_ = f32[5,16,128]{2,1,0:T(8,128)S(1)} collective-permute-done((f32[5,16,128]{2,1,0:T(8,128)S(1)}, f32[5,16,128]{2,1,0:T(8,128)S(1)}, u32[]{:S(2)}, u32[]{:S(2)}) %collective-permute-start.1) | collective-permute-done | bytes 40992 | tf_op jit(solution)/shard_map/ppermute | solution.py:547
  8.2 0.4 %join_rows.1 = (f32[192,128]{1,0:T(8,128)S(1)}, f32[192,128]{1,0:T(8,128)S(1)}) custom-call(f32[16,128]{1,0:T(8,128)S(1)} %get-tuple-element.21.level_ref.refs_0_, f32[16,128]{1,0:T(8,128)S(1)} %get-tuple-element.22.eta_ref.refs_1_, f32[5,16,128]{2,1,0:T(8,128)S(1)} %get-tuple-element.23.own_ref, f32[5,16,128]{2,1,0:T(8,128)S(1)} %collective-permute-done.first_ref.refs_2_, ...), custom_call_target="tpu_custom_call" | custom-call | tf_op jit(solution)/shard_map/join_rows/pallas_call | solution.py:526
  8.6 0.7 %collective-permute-start.2 = (f32[192,128]{1,0:T(8,128)S(1)}, f32[192,128]{1,0:T(8,128)S(1)}, u32[]{:S(2)}, u32[]{:S(2)}) collective-permute-start(f32[192,128]{1,0:T(8,128)S(1)} %get-tuple-element.33), channel_id=1, source_target_pairs={{1,2},{2,1},{5,6},{6,5},{9,10},{10,9},{13,14},{14,13},{17,18},{18,... | collective-permute-start | bytes 294920 | tf_op jit(solution)/shard_map/ppermute | solution.py:547
  9.3 4.6 %collective-permute-start.3 = (f32[192,128]{1,0:T(8,128)S(1)}, f32[192,128]{1,0:T(8,128)S(1)}, u32[]{:S(2)}, u32[]{:S(2)}) collective-permute-start(f32[192,128]{1,0:T(8,128)S(1)} %get-tuple-element.34), channel_id=1, source_target_pairs={{0,1},{1,0},{2,3},{3,2},{4,5},{5,4},{6,7},{7,6},{8,9},{9,8},{10,11... | collective-permute-start | bytes 294920 | tf_op jit(solution)/shard_map/ppermute | solution.py:547
  13.9 0.0 collective-permute-done.2.refs_4_.first_row
  13.9 2.6 %collective-permute-done.3.refs_5_.second_row = f32[192,128]{1,0:T(8,128)S(1)} collective-permute-done((f32[192,128]{1,0:T(8,128)S(1)}, f32[192,128]{1,0:T(8,128)S(1)}, u32[]{:S(2)}, u32[]{:S(2)}) %collective-permute-start.3) | collective-permute-done | bytes 98336 | tf_op jit(solution)/shard_map/ppermute | solution.py:547
  16.5 1.2 %surface.1 = (f32[3,24,256]{2,1,0:T(8,128)S(1)}, f32[24,256]{1,0:T(8,128)S(1)}, f32[32,128]{1,0:T(8,128)}) custom-call(f32[16,128]{1,0:T(8,128)S(1)} %get-tuple-element.21.level_ref.refs_0_, f32[16,128]{1,0:T(8,128)S(1)} %get-tuple-element.22.eta_ref.refs_1_, f32[5,16,128]{2,1,0:T(8,128)S(1)} %collective-permute-done.first_ref.refs_2_, ...), custom_call_target="tpu_custom_call" | custom-call | tf_op jit(solution)/shard_map/surface/pallas_call | solution.py:526
  17.6 4.3 %all-to-all-start = ((f32[32,1,128]{2,1,0:T(1,128)}), f32[32,1,128]{2,1,0:T(1,128)S(1)}, u32[]{:S(2)}, u32[]{:S(2)}) async-start(f32[32,1,128]{2,1,0:T(1,128)} %bitcast.1), calls=%async_computation | async-start | bytes 32768 | tf_op jit(solution)/shard_map/all_to_all | solution.py:582
  22.0 3.3 %columns.1 = (f32[2,24,16,128]{3,2,1,0:T(8,128)S(1)}, f32[3,24,16,128]{3,2,1,0:T(8,128)S(1)}) custom-call(f32[2,24,16,128]{3,2,1,0:T(8,128)S(1)} %get-tuple-element.24.tracer_ref, f32[24,16,128]{2,1,0:T(8,128)S(1)} %get-tuple-element.25.u_ref, f32[24,16,128]{2,1,0:T(8,128)S(1)} %get-tuple-element.26.v_ref, f32[2,24,16,128]{3,2,1,0:T(8,128)S(1)} %get-tuple-element.27.bar_ref, ...), custom_call_target="tpu_custom_call" | custom-call | flops 19660800 | bytes 4194304 | tf_op jit(solution)/shard_map/columns/pallas_call | solution.py:526
  25.3 3.8 %all-to-all-done = f32[32,1,128]{2,1,0:T(1,128)S(1)} async-done(((f32[32,1,128]{2,1,0:T(1,128)}), f32[32,1,128]{2,1,0:T(1,128)S(1)}, u32[]{:S(2)}, u32[]{:S(2)}) %all-to-all-start) | async-done | bytes 16416 | tf_op jit(solution)/shard_map/all_to_all | solution.py:582
  29.1 1.0 %finish.1 = (f32[2,24,16,128]{3,2,1,0:T(8,128)}, f32[16,128]{1,0:T(8,128)}) custom-call(f32[32,128]{1,0:T(8,128)S(1)} %bitcast.4, f32[3,24,256]{2,1,0:T(8,128)S(1)} %get-tuple-element.36.basis_ref, f32[2,24,16,128]{3,2,1,0:T(8,128)S(1)} %get-tuple-element.38.base_ref, f32[3,24,16,128]{3,2,1,0:T(8,128)S(1)} %get-tuple-element.39.share_ref), custom_call_target="tpu_custom_call" | custom-call | tf_op jit(solution)/shard_map/finish/pallas_call | solution.py:526
Async XLA Ops:
  2.4 4.2 %collective-permute-start = (f32[5,16,128]{2,1,0:T(8,128)S(1)}, f32[5,16,128]{2,1,0:T(8,128)S(1)}, u32[]{:S(2)}, u32[]{:S(2)}) collective-permute-start(f32[5,16,128]{2,1,0:T(8,128)S(1)} %get-tuple-element.23.own_ref), channel_id=1, source_target_pairs={{0,4},{4,0},{8,12},{12,8},{16,20},{20,16},{24,28},{28,24},{1,5},{5... | collective-permute-start | bytes 122888 | tf_op jit(solution)/shard_map/ppermute | solution.py:547
  3.0 5.2 %collective-permute-start.1 = (f32[5,16,128]{2,1,0:T(8,128)S(1)}, f32[5,16,128]{2,1,0:T(8,128)S(1)}, u32[]{:S(2)}, u32[]{:S(2)}) collective-permute-start(f32[5,16,128]{2,1,0:T(8,128)S(1)} %get-tuple-element.23.own_ref), channel_id=1, source_target_pairs={{4,8},{8,4},{12,16},{16,12},{20,24},{24,20},{28,0},{0,28},{5,9},{9... | collective-permute-start | bytes 122888 | tf_op jit(solution)/shard_map/ppermute | solution.py:547
  8.6 5.3 %collective-permute-start.2 = (f32[192,128]{1,0:T(8,128)S(1)}, f32[192,128]{1,0:T(8,128)S(1)}, u32[]{:S(2)}, u32[]{:S(2)}) collective-permute-start(f32[192,128]{1,0:T(8,128)S(1)} %get-tuple-element.33), channel_id=1, source_target_pairs={{1,2},{2,1},{5,6},{6,5},{9,10},{10,9},{13,14},{14,13},{17,18},{18,... | collective-permute-start | bytes 294920 | tf_op jit(solution)/shard_map/ppermute | solution.py:547
  9.3 7.2 %collective-permute-start.3 = (f32[192,128]{1,0:T(8,128)S(1)}, f32[192,128]{1,0:T(8,128)S(1)}, u32[]{:S(2)}, u32[]{:S(2)}) collective-permute-start(f32[192,128]{1,0:T(8,128)S(1)} %get-tuple-element.34), channel_id=1, source_target_pairs={{0,1},{1,0},{2,3},{3,2},{4,5},{5,4},{6,7},{7,6},{8,9},{9,8},{10,11... | collective-permute-start | bytes 294920 | tf_op jit(solution)/shard_map/ppermute | solution.py:547
  17.6 11.5 %all-to-all-start = ((f32[32,1,128]{2,1,0:T(1,128)}), f32[32,1,128]{2,1,0:T(1,128)S(1)}, u32[]{:S(2)}, u32[]{:S(2)}) async-start(f32[32,1,128]{2,1,0:T(1,128)} %bitcast.1), calls=%async_computation | async-start | bytes 32768 | tf_op jit(solution)/shard_map/all_to_all | solution.py:582

commit v10 on v9

--- a/solution.py
+++ b/solution.py
@@ -242,11 +242,9 @@
     eta_ext = extended(eta_ref[...], sides.eta, north, south, 0)
     level_ext = extended(level, sides.depth, north, south, 4)
     level_out[...] = level_ext
-    depth = level_ext / count
-    east_weight = (surface_stiffness / spread) * jnp.minimum(depth, roll(depth, -1, 1))
-    north_weight = (surface_stiffness / spread) * jnp.minimum(depth, roll(depth, -1, 0))
-
-    west_weight, south_weight = roll(east_weight, 1, 1), roll(north_weight, 1, 0)
+    rate = surface_stiffness / (spread * count)
+    east_weight, west_weight = (rate * jnp.minimum(level_ext, roll(level_ext, step, 1)) for step in (-1, 1))
+    north_weight, south_weight = (rate * jnp.minimum(level_ext, roll(level_ext, step, 0)) for step in (-1, 1))
 
     def scaled(field):
         along_x = east_weight * (field - roll(field, -1, 1)) + west_weight * (field - roll(field, 1, 1))

time: 30.3 us -> 30.3 us (level)
  no operation moved by 1% of the time
where the time goes in v10:
time: 30.3 us; the launch traced here: 30.1 us
  starting transfers between devices  13.7 us (45%)
  waiting for transfers between devices  7.93 us (26%)
  Pallas kernels  7.75 us (26%)
  between operations  0.68 us (2%)
    ppermute x4, starting transfers between devices, swap(): return lax.ppermute(cells, axis, pairs)  9.39 us
    pallas_call x6, Pallas kernels, run(): pl.pallas_call(kernel, out_shape=[jax.ShapeDtypeStruct(shape, F32) for sh...  7.75 us
    all_to_all x1, starting transfers between devices, per_device(): lax.all_to_all(sums.reshape(devices, 1, width), ('gx', 'gy'), 0, 0)  4.34 us
    ppermute x4, waiting for transfers between devices, swap(): return lax.ppermute(cells, axis, pairs)  4.14 us
    all_to_all x1, waiting for transfers between devices, per_device(): lax.all_to_all(sums.reshape(devices, 1, width), ('gx', 'gy'), 0, 0)  3.78 us
  transfers between devices with their start and end apart: 5, of which 3 were waited for; matrix products, arithmetic and copies ran while one was open for 0% of the time, Pallas kernels for 12%

profile of v10, /device:TPU:0, one launch (start us, length us, event | category | flops | bytes accessed | tf_op | source)
XLA Modules:
  0.0 30.1 jit_solution(14989959496766481268)
XLA Ops:
  0.6 1.8 %pack_columns.1 = (f32[5,16,128]{2,1,0:T(8,128)S(1)}, f32[16,128]{1,0:T(8,128)S(1)}, f32[16,128]{1,0:T(8,128)S(1)}, f32[2,24,16,128]{3,2,1,0:T(8,128)S(1)}, f32[...) custom-call(s32[16,128]{1,0:T(8,128)} %mask_in.1, s32[16,128]{1,0:T(8,128)} %levels_in.1, ...), custom_call_target="tpu_custom_call" | custom-call | tf_op jit(solution)/shard_map/pack_columns/pallas_call | solution.py:524
  2.4 0.6 %collective-permute-start = (f32[5,16,128]{2,1,0:T(8,128)S(1)}, f32[5,16,128]{2,1,0:T(8,128)S(1)}, u32[]{:S(2)}, u32[]{:S(2)}) collective-permute-start(f32[5,16,128]{2,1,0:T(8,128)S(1)} %get-tuple-element.23.own_ref), channel_id=1, source_target_pairs={{0,4},{4,0},{8,12},{12,8},{16,20},{20,16},{24,28},{28,24},{1,5},{5... | collective-permute-start | bytes 122888 | tf_op jit(solution)/shard_map/ppermute | solution.py:545
  3.0 3.5 %collective-permute-start.1 = (f32[5,16,128]{2,1,0:T(8,128)S(1)}, f32[5,16,128]{2,1,0:T(8,128)S(1)}, u32[]{:S(2)}, u32[]{:S(2)}) collective-permute-start(f32[5,16,128]{2,1,0:T(8,128)S(1)} %get-tuple-element.23.own_ref), channel_id=1, source_target_pairs={{4,8},{8,4},{12,16},{16,12},{20,24},{24,20},{28,0},{0,28},{5,9},{9... | collective-permute-start | bytes 122888 | tf_op jit(solution)/shard_map/ppermute | solution.py:545
  6.5 0.1 pack_rows.1
  6.7 0.0 collective-permute-done.first_ref.refs_2_
  6.7 1.5 %collective-permute-done.1.second_ref.refs_3_ = f32[5,16,128]{2,1,0:T(8,128)S(1)} collective-permute-done((f32[5,16,128]{2,1,0:T(8,128)S(1)}, f32[5,16,128]{2,1,0:T(8,128)S(1)}, u32[]{:S(2)}, u32[]{:S(2)}) %collective-permute-start.1) | collective-permute-done | bytes 40992 | tf_op jit(solution)/shard_map/ppermute | solution.py:545
  8.2 0.4 %join_rows.1 = (f32[192,128]{1,0:T(8,128)S(1)}, f32[192,128]{1,0:T(8,128)S(1)}) custom-call(f32[16,128]{1,0:T(8,128)S(1)} %get-tuple-element.21.level_ref.refs_0_, f32[16,128]{1,0:T(8,128)S(1)} %get-tuple-element.22.eta_ref.refs_1_, f32[5,16,128]{2,1,0:T(8,128)S(1)} %get-tuple-element.23.own_ref, f32[5,16,128]{2,1,0:T(8,128)S(1)} %collective-permute-done.first_ref.refs_2_, ...), custom_call_target="tpu_custom_call" | custom-call | tf_op jit(solution)/shard_map/join_rows/pallas_call | solution.py:524
  8.6 0.7 %collective-permute-start.2 = (f32[192,128]{1,0:T(8,128)S(1)}, f32[192,128]{1,0:T(8,128)S(1)}, u32[]{:S(2)}, u32[]{:S(2)}) collective-permute-start(f32[192,128]{1,0:T(8,128)S(1)} %get-tuple-element.33), channel_id=1, source_target_pairs={{1,2},{2,1},{5,6},{6,5},{9,10},{10,9},{13,14},{14,13},{17,18},{18,... | collective-permute-start | bytes 294920 | tf_op jit(solution)/shard_map/ppermute | solution.py:545
  9.3 4.6 %collective-permute-start.3 = (f32[192,128]{1,0:T(8,128)S(1)}, f32[192,128]{1,0:T(8,128)S(1)}, u32[]{:S(2)}, u32[]{:S(2)}) collective-permute-start(f32[192,128]{1,0:T(8,128)S(1)} %get-tuple-element.34), channel_id=1, source_target_pairs={{0,1},{1,0},{2,3},{3,2},{4,5},{5,4},{6,7},{7,6},{8,9},{9,8},{10,11... | collective-permute-start | bytes 294920 | tf_op jit(solution)/shard_map/ppermute | solution.py:545
  13.9 0.0 collective-permute-done.2.refs_4_.first_row
  13.9 2.6 %collective-permute-done.3.refs_5_.second_row = f32[192,128]{1,0:T(8,128)S(1)} collective-permute-done((f32[192,128]{1,0:T(8,128)S(1)}, f32[192,128]{1,0:T(8,128)S(1)}, u32[]{:S(2)}, u32[]{:S(2)}) %collective-permute-start.3) | collective-permute-done | bytes 98336 | tf_op jit(solution)/shard_map/ppermute | solution.py:545
  16.5 1.1 %surface.1 = (f32[3,24,256]{2,1,0:T(8,128)S(1)}, f32[24,256]{1,0:T(8,128)S(1)}, f32[32,128]{1,0:T(8,128)}) custom-call(f32[16,128]{1,0:T(8,128)S(1)} %get-tuple-element.21.level_ref.refs_0_, f32[16,128]{1,0:T(8,128)S(1)} %get-tuple-element.22.eta_ref.refs_1_, f32[5,16,128]{2,1,0:T(8,128)S(1)} %collective-permute-done.first_ref.refs_2_, ...), custom_call_target="tpu_custom_call" | custom-call | tf_op jit(solution)/shard_map/surface/pallas_call | solution.py:524
  17.6 4.3 %all-to-all-start = ((f32[32,1,128]{2,1,0:T(1,128)}), f32[32,1,128]{2,1,0:T(1,128)S(1)}, u32[]{:S(2)}, u32[]{:S(2)}) async-start(f32[32,1,128]{2,1,0:T(1,128)} %bitcast.1), calls=%async_computation | async-start | bytes 32768 | tf_op jit(solution)/shard_map/all_to_all | solution.py:580
  21.9 3.3 %columns.1 = (f32[2,24,16,128]{3,2,1,0:T(8,128)S(1)}, f32[3,24,16,128]{3,2,1,0:T(8,128)S(1)}) custom-call(f32[2,24,16,128]{3,2,1,0:T(8,128)S(1)} %get-tuple-element.24.tracer_ref, f32[24,16,128]{2,1,0:T(8,128)S(1)} %get-tuple-element.25.u_ref, f32[24,16,128]{2,1,0:T(8,128)S(1)} %get-tuple-element.26.v_ref, f32[2,24,16,128]{3,2,1,0:T(8,128)S(1)} %get-tuple-element.27.bar_ref, ...), custom_call_target="tpu_custom_call" | custom-call | flops 19660800 | bytes 4194304 | tf_op jit(solution)/shard_map/columns/pallas_call | solution.py:524
  25.3 3.8 %all-to-all-done = f32[32,1,128]{2,1,0:T(1,128)S(1)} async-done(((f32[32,1,128]{2,1,0:T(1,128)}), f32[32,1,128]{2,1,0:T(1,128)S(1)}, u32[]{:S(2)}, u32[]{:S(2)}) %all-to-all-start) | async-done | bytes 16416 | tf_op jit(solution)/shard_map/all_to_all | solution.py:580
  29.1 1.0 %finish.1 = (f32[2,24,16,128]{3,2,1,0:T(8,128)}, f32[16,128]{1,0:T(8,128)}) custom-call(f32[32,128]{1,0:T(8,128)S(1)} %bitcast.4, f32[3,24,256]{2,1,0:T(8,128)S(1)} %get-tuple-element.36.basis_ref, f32[2,24,16,128]{3,2,1,0:T(8,128)S(1)} %get-tuple-element.38.base_ref, f32[3,24,16,128]{3,2,1,0:T(8,128)S(1)} %get-tuple-element.39.share_ref), custom_call_target="tpu_custom_call" | custom-call | tf_op jit(solution)/shard_map/finish/pallas_call | solution.py:524
Async XLA Ops:
  2.4 4.2 %collective-permute-start = (f32[5,16,128]{2,1,0:T(8,128)S(1)}, f32[5,16,128]{2,1,0:T(8,128)S(1)}, u32[]{:S(2)}, u32[]{:S(2)}) collective-permute-start(f32[5,16,128]{2,1,0:T(8,128)S(1)} %get-tuple-element.23.own_ref), channel_id=1, source_target_pairs={{0,4},{4,0},{8,12},{12,8},{16,20},{20,16},{24,28},{28,24},{1,5},{5... | collective-permute-start | bytes 122888 | tf_op jit(solution)/shard_map/ppermute | solution.py:545
  3.0 5.2 %collective-permute-start.1 = (f32[5,16,128]{2,1,0:T(8,128)S(1)}, f32[5,16,128]{2,1,0:T(8,128)S(1)}, u32[]{:S(2)}, u32[]{:S(2)}) collective-permute-start(f32[5,16,128]{2,1,0:T(8,128)S(1)} %get-tuple-element.23.own_ref), channel_id=1, source_target_pairs={{4,8},{8,4},{12,16},{16,12},{20,24},{24,20},{28,0},{0,28},{5,9},{9... | collective-permute-start | bytes 122888 | tf_op jit(solution)/shard_map/ppermute | solution.py:545
  8.6 5.3 %collective-permute-start.2 = (f32[192,128]{1,0:T(8,128)S(1)}, f32[192,128]{1,0:T(8,128)S(1)}, u32[]{:S(2)}, u32[]{:S(2)}) collective-permute-start(f32[192,128]{1,0:T(8,128)S(1)} %get-tuple-element.33), channel_id=1, source_target_pairs={{1,2},{2,1},{5,6},{6,5},{9,10},{10,9},{13,14},{14,13},{17,18},{18,... | collective-permute-start | bytes 294920 | tf_op jit(solution)/shard_map/ppermute | solution.py:545
  9.3 7.2 %collective-permute-start.3 = (f32[192,128]{1,0:T(8,128)S(1)}, f32[192,128]{1,0:T(8,128)S(1)}, u32[]{:S(2)}, u32[]{:S(2)}) collective-permute-start(f32[192,128]{1,0:T(8,128)S(1)} %get-tuple-element.34), channel_id=1, source_target_pairs={{0,1},{1,0},{2,3},{3,2},{4,5},{5,4},{6,7},{7,6},{8,9},{9,8},{10,11... | collective-permute-start | bytes 294920 | tf_op jit(solution)/shard_map/ppermute | solution.py:545
  17.6 11.5 %all-to-all-start = ((f32[32,1,128]{2,1,0:T(1,128)}), f32[32,1,128]{2,1,0:T(1,128)S(1)}, u32[]{:S(2)}, u32[]{:S(2)}) async-start(f32[32,1,128]{2,1,0:T(1,128)} %bitcast.1), calls=%async_computation | async-start | bytes 32768 | tf_op jit(solution)/shard_map/all_to_all | solution.py:580

commit v11 on v10

--- a/solution.py
+++ b/solution.py
@@ -152,8 +152,8 @@
         self.bars = [slice(f * count, (f + 1) * count) for f in range(4, 6)]
         self.v = slice(6 * count, 7 * count)
         self.surface = [slice(7 * count + 8 * i, 7 * count + 8 * i + 8) for i in range(2)]
-        self.corner = slice(7 * count + 16, 7 * count + 24)
-        self.rows = 7 * count + 24
+        self.corner = self.surface[1]
+        self.rows = 7 * count + 16
 
 
 def is_even(axis, shape):
@@ -203,22 +203,28 @@
         put(plan.summed[f], summed(0, f, height - 1, -1.0), summed(1, f, 0, 1.0))
         put(plan.bars[f], b_ref[0, part, :], b_ref[1, part, :])
     put(plan.v, v_ref[...], no_flow)
-    for part, eta, depth in zip(plan.surface, (eta_ref[...], sides.eta), (level, sides.depth)):
+    def ends(eta, depth):
         north = jnp.where(row8 < 4, roll(depth[height - 8 :, :], 4, 0), eta[height - 8 :, :])
-        put(part, north, jnp.where(row8 < 4, eta[:8, :], roll(depth[:8, :], 4, 0)))
+        return north, jnp.where(row8 < 4, eta[:8, :], roll(depth[:8, :], 4, 0))
+
+    put(plan.surface[0], *ends(eta_ref[...], level))
     lines = [inner[0], inner[1], v_inner]
     north = south = pad
     for index, cells in enumerate(lines):
         north = jnp.where(row8 == index, cells[height - 1 :, :], north)
         south = jnp.where(row8 == index, cells[:1, :], south)
-    put(plan.corner, north, south)
+    start = width - 6 - surface_turn
+    lane8 = lanes_of((8, width))
+    beyond = (lane8 >= start) & (lane8 < start + 12)
+    moved = [roll(cells, -surface_turn, 1) for cells in ends(sides.eta, sides.depth)]
+    put(plan.corner, jnp.where(beyond, moved[0], north), jnp.where(beyond, moved[1], south))
 
 
 def extended(own, side, north, south, turn):
     row8 = rows_of((8, own.shape[1]))
     parts = []
     for index, tile in enumerate((own, side)):
-        up, down = (roll(msg[index], turn, 0) for msg in (north, south))
+        up, down = (roll(roll(msg[index], index * surface_turn, 1), turn, 0) for msg in (north, south))
         parts.append(jnp.concatenate([tile, jnp.where(row8 < 4, up, down)], axis=0))
     return jnp.concatenate(parts, axis=1)
 

time: 30.3 us -> 30.2 us (level)
  no operation moved by 1% of the time
where the time goes in v11:
time: 30.2 us; the launch traced here: 30 us
  starting transfers between devices  13.7 us (45%)
  waiting for transfers between devices  7.88 us (26%)
  Pallas kernels  7.75 us (26%)
  between operations  0.68 us (2%)
    ppermute x4, starting transfers between devices, swap(): return lax.ppermute(cells, axis, pairs)  9.39 us
    pallas_call x6, Pallas kernels, run(): pl.pallas_call(kernel, out_shape=[jax.ShapeDtypeStruct(shape, F32) for sh...  7.75 us
    all_to_all x1, starting transfers between devices, per_device(): lax.all_to_all(sums.reshape(devices, 1, width), ('gx', 'gy'), 0, 0)  4.3 us
    ppermute x4, waiting for transfers between devices, swap(): return lax.ppermute(cells, axis, pairs)  4.1 us
    all_to_all x1, waiting for transfers between devices, per_device(): lax.all_to_all(sums.reshape(devices, 1, width), ('gx', 'gy'), 0, 0)  3.78 us
  transfers between devices with their start and end apart: 5, of which 3 were waited for; matrix products, arithmetic and copies ran while one was open for 0% of the time, Pallas kernels for 12%

profile of v11, /device:TPU:0, one launch (start us, length us, event | category | flops | bytes accessed | tf_op | source)
XLA Modules:
  0.0 30.0 jit_solution(16423091675844397947)
XLA Ops:
  0.6 1.8 %pack_columns.1 = (f32[5,16,128]{2,1,0:T(8,128)S(1)}, f32[16,128]{1,0:T(8,128)S(1)}, f32[16,128]{1,0:T(8,128)S(1)}, f32[2,24,16,128]{3,2,1,0:T(8,128)S(1)}, f32[...) custom-call(s32[16,128]{1,0:T(8,128)} %mask_in.1, s32[16,128]{1,0:T(8,128)} %levels_in.1, ...), custom_call_target="tpu_custom_call" | custom-call | tf_op jit(solution)/shard_map/pack_columns/pallas_call | solution.py:530
  2.4 0.6 %collective-permute-start = (f32[5,16,128]{2,1,0:T(8,128)S(1)}, f32[5,16,128]{2,1,0:T(8,128)S(1)}, u32[]{:S(2)}, u32[]{:S(2)}) collective-permute-start(f32[5,16,128]{2,1,0:T(8,128)S(1)} %get-tuple-element.23.own_ref), channel_id=1, source_target_pairs={{0,4},{4,0},{8,12},{12,8},{16,20},{20,16},{24,28},{28,24},{1,5},{5... | collective-permute-start | bytes 122888 | tf_op jit(solution)/shard_map/ppermute | solution.py:551
  3.0 3.5 %collective-permute-start.1 = (f32[5,16,128]{2,1,0:T(8,128)S(1)}, f32[5,16,128]{2,1,0:T(8,128)S(1)}, u32[]{:S(2)}, u32[]{:S(2)}) collective-permute-start(f32[5,16,128]{2,1,0:T(8,128)S(1)} %get-tuple-element.23.own_ref), channel_id=1, source_target_pairs={{4,8},{8,4},{12,16},{16,12},{20,24},{24,20},{28,0},{0,28},{5,9},{9... | collective-permute-start | bytes 122888 | tf_op jit(solution)/shard_map/ppermute | solution.py:551
  6.5 0.1 pack_rows.1
  6.7 0.0 collective-permute-done.first_ref.refs_2_
  6.7 1.5 %collective-permute-done.1.second_ref.refs_3_ = f32[5,16,128]{2,1,0:T(8,128)S(1)} collective-permute-done((f32[5,16,128]{2,1,0:T(8,128)S(1)}, f32[5,16,128]{2,1,0:T(8,128)S(1)}, u32[]{:S(2)}, u32[]{:S(2)}) %collective-permute-start.1) | collective-permute-done | bytes 40992 | tf_op jit(solution)/shard_map/ppermute | solution.py:551
  8.2 0.4 %join_rows.1 = (f32[184,128]{1,0:T(8,128)S(1)}, f32[184,128]{1,0:T(8,128)S(1)}) custom-call(f32[16,128]{1,0:T(8,128)S(1)} %get-tuple-element.21.level_ref.refs_0_, f32[16,128]{1,0:T(8,128)S(1)} %get-tuple-element.22.eta_ref.refs_1_, f32[5,16,128]{2,1,0:T(8,128)S(1)} %get-tuple-element.23.own_ref, f32[5,16,128]{2,1,0:T(8,128)S(1)} %collective-permute-done.first_ref.refs_2_, ...), custom_call_target="tpu_custom_call" | custom-call | tf_op jit(solution)/shard_map/join_rows/pallas_call | solution.py:530
  8.6 0.7 %collective-permute-start.2 = (f32[184,128]{1,0:T(8,128)S(1)}, f32[184,128]{1,0:T(8,128)S(1)}, u32[]{:S(2)}, u32[]{:S(2)}) collective-permute-start(f32[184,128]{1,0:T(8,128)S(1)} %get-tuple-element.33), channel_id=1, source_target_pairs={{1,2},{2,1},{5,6},{6,5},{9,10},{10,9},{13,14},{14,13},{17,18},{18,... | collective-permute-start | bytes 282632 | tf_op jit(solution)/shard_map/ppermute | solution.py:551
  9.3 4.6 %collective-permute-start.3 = (f32[184,128]{1,0:T(8,128)S(1)}, f32[184,128]{1,0:T(8,128)S(1)}, u32[]{:S(2)}, u32[]{:S(2)}) collective-permute-start(f32[184,128]{1,0:T(8,128)S(1)} %get-tuple-element.34), channel_id=1, source_target_pairs={{0,1},{1,0},{2,3},{3,2},{4,5},{5,4},{6,7},{7,6},{8,9},{9,8},{10,11... | collective-permute-start | bytes 282632 | tf_op jit(solution)/shard_map/ppermute | solution.py:551
  13.9 0.0 collective-permute-done.2.refs_4_.first_row
  13.9 2.5 %collective-permute-done.3.refs_5_.second_row = f32[184,128]{1,0:T(8,128)S(1)} collective-permute-done((f32[184,128]{1,0:T(8,128)S(1)}, f32[184,128]{1,0:T(8,128)S(1)}, u32[]{:S(2)}, u32[]{:S(2)}) %collective-permute-start.3) | collective-permute-done | bytes 94240 | tf_op jit(solution)/shard_map/ppermute | solution.py:551
  16.4 1.1 %surface.1 = (f32[3,24,256]{2,1,0:T(8,128)S(1)}, f32[24,256]{1,0:T(8,128)S(1)}, f32[32,128]{1,0:T(8,128)}) custom-call(f32[16,128]{1,0:T(8,128)S(1)} %get-tuple-element.21.level_ref.refs_0_, f32[16,128]{1,0:T(8,128)S(1)} %get-tuple-element.22.eta_ref.refs_1_, f32[5,16,128]{2,1,0:T(8,128)S(1)} %collective-permute-done.first_ref.refs_2_, ...), custom_call_target="tpu_custom_call" | custom-call | tf_op jit(solution)/shard_map/surface/pallas_call | solution.py:530
  17.5 4.3 %all-to-all-start = ((f32[32,1,128]{2,1,0:T(1,128)}), f32[32,1,128]{2,1,0:T(1,128)S(1)}, u32[]{:S(2)}, u32[]{:S(2)}) async-start(f32[32,1,128]{2,1,0:T(1,128)} %bitcast.1), calls=%async_computation | async-start | bytes 32768 | tf_op jit(solution)/shard_map/all_to_all | solution.py:586
  21.8 3.3 %columns.1 = (f32[2,24,16,128]{3,2,1,0:T(8,128)S(1)}, f32[3,24,16,128]{3,2,1,0:T(8,128)S(1)}) custom-call(f32[2,24,16,128]{3,2,1,0:T(8,128)S(1)} %get-tuple-element.24.tracer_ref, f32[24,16,128]{2,1,0:T(8,128)S(1)} %get-tuple-element.25.u_ref, f32[24,16,128]{2,1,0:T(8,128)S(1)} %get-tuple-element.26.v_ref, f32[2,24,16,128]{3,2,1,0:T(8,128)S(1)} %get-tuple-element.27.bar_ref, ...), custom_call_target="tpu_custom_call" | custom-call | flops 19660800 | bytes 4194304 | tf_op jit(solution)/shard_map/columns/pallas_call | solution.py:530
  25.2 3.8 %all-to-all-done = f32[32,1,128]{2,1,0:T(1,128)S(1)} async-done(((f32[32,1,128]{2,1,0:T(1,128)}), f32[32,1,128]{2,1,0:T(1,128)S(1)}, u32[]{:S(2)}, u32[]{:S(2)}) %all-to-all-start) | async-done | bytes 16416 | tf_op jit(solution)/shard_map/all_to_all | solution.py:586
  29.0 1.0 %finish.1 = (f32[2,24,16,128]{3,2,1,0:T(8,128)}, f32[16,128]{1,0:T(8,128)}) custom-call(f32[32,128]{1,0:T(8,128)S(1)} %bitcast.4, f32[3,24,256]{2,1,0:T(8,128)S(1)} %get-tuple-element.36.basis_ref, f32[2,24,16,128]{3,2,1,0:T(8,128)S(1)} %get-tuple-element.38.base_ref, f32[3,24,16,128]{3,2,1,0:T(8,128)S(1)} %get-tuple-element.39.share_ref), custom_call_target="tpu_custom_call" | custom-call | tf_op jit(solution)/shard_map/finish/pallas_call | solution.py:530
Async XLA Ops:
  2.4 4.2 %collective-permute-start = (f32[5,16,128]{2,1,0:T(8,128)S(1)}, f32[5,16,128]{2,1,0:T(8,128)S(1)}, u32[]{:S(2)}, u32[]{:S(2)}) collective-permute-start(f32[5,16,128]{2,1,0:T(8,128)S(1)} %get-tuple-element.23.own_ref), channel_id=1, source_target_pairs={{0,4},{4,0},{8,12},{12,8},{16,20},{20,16},{24,28},{28,24},{1,5},{5... | collective-permute-start | bytes 122888 | tf_op jit(solution)/shard_map/ppermute | solution.py:551
  3.0 5.2 %collective-permute-start.1 = (f32[5,16,128]{2,1,0:T(8,128)S(1)}, f32[5,16,128]{2,1,0:T(8,128)S(1)}, u32[]{:S(2)}, u32[]{:S(2)}) collective-permute-start(f32[5,16,128]{2,1,0:T(8,128)S(1)} %get-tuple-element.23.own_ref), channel_id=1, source_target_pairs={{4,8},{8,4},{12,16},{16,12},{20,24},{24,20},{28,0},{0,28},{5,9},{9... | collective-permute-start | bytes 122888 | tf_op jit(solution)/shard_map/ppermute | solution.py:551
  8.6 5.3 %collective-permute-start.2 = (f32[184,128]{1,0:T(8,128)S(1)}, f32[184,128]{1,0:T(8,128)S(1)}, u32[]{:S(2)}, u32[]{:S(2)}) collective-permute-start(f32[184,128]{1,0:T(8,128)S(1)} %get-tuple-element.33), channel_id=1, source_target_pairs={{1,2},{2,1},{5,6},{6,5},{9,10},{10,9},{13,14},{14,13},{17,18},{18,... | collective-permute-start | bytes 282632 | tf_op jit(solution)/shard_map/ppermute | solution.py:551
  9.3 7.2 %collective-permute-start.3 = (f32[184,128]{1,0:T(8,128)S(1)}, f32[184,128]{1,0:T(8,128)S(1)}, u32[]{:S(2)}, u32[]{:S(2)}) collective-permute-start(f32[184,128]{1,0:T(8,128)S(1)} %get-tuple-element.34), channel_id=1, source_target_pairs={{0,1},{1,0},{2,3},{3,2},{4,5},{5,4},{6,7},{7,6},{8,9},{9,8},{10,11... | collective-permute-start | bytes 282632 | tf_op jit(solution)/shard_map/ppermute | solution.py:551
  17.5 11.4 %all-to-all-start = ((f32[32,1,128]{2,1,0:T(1,128)}), f32[32,1,128]{2,1,0:T(1,128)S(1)}, u32[]{:S(2)}, u32[]{:S(2)}) async-start(f32[32,1,128]{2,1,0:T(1,128)} %bitcast.1), calls=%async_computation | async-start | bytes 32768 | tf_op jit(solution)/shard_map/all_to_all | solution.py:586

commit v12 on v11

--- a/solution.py
+++ b/solution.py
@@ -52,7 +52,7 @@
         (mask_in, mask_ref), (levels_in, levels_ref), (eta_in, eta_ref),
     )
     copies = [pltpu.make_async_copy(source, target, sems.at[i]) for i, (source, target) in enumerate(pairs)]
-    for copy in copies:
+    for copy in copies[4:] + copies[:4]:
         copy.start()
     count, height, width = u_ref.shape
     lane = lanes_of((height, width))

time: 30.2 us -> 30.2 us (level)
  no operation moved by 1% of the time
where the time goes in v12:
time: 30.2 us; the launch traced here: 30 us
  starting transfers between devices  13.7 us (45%)
  waiting for transfers between devices  7.88 us (26%)
  Pallas kernels  7.8 us (26%)
  between operations  0.68 us (2%)
    ppermute x4, starting transfers between devices, swap(): return lax.ppermute(cells, axis, pairs)  9.39 us
    pallas_call x6, Pallas kernels, run(): pl.pallas_call(kernel, out_shape=[jax.ShapeDtypeStruct(shape, F32) for sh...  7.8 us
    all_to_all x1, starting transfers between devices, per_device(): lax.all_to_all(sums.reshape(devices, 1, width), ('gx', 'gy'), 0, 0)  4.3 us
    ppermute x4, waiting for transfers between devices, swap(): return lax.ppermute(cells, axis, pairs)  4.1 us
    all_to_all x1, waiting for transfers between devices, per_device(): lax.all_to_all(sums.reshape(devices, 1, width), ('gx', 'gy'), 0, 0)  3.78 us
  transfers between devices with their start and end apart: 5, of which 3 were waited for; matrix products, arithmetic and copies ran while one was open for 0% of the time, Pallas kernels for 12%

profile of v12, /device:TPU:0, one launch (start us, length us, event | category | flops | bytes accessed | tf_op | source)
XLA Modules:
  0.0 30.0 jit_solution(17605904208369954630)
XLA Ops:
  0.6 1.8 %pack_columns.1 = (f32[5,16,128]{2,1,0:T(8,128)S(1)}, f32[16,128]{1,0:T(8,128)S(1)}, f32[16,128]{1,0:T(8,128)S(1)}, f32[2,24,16,128]{3,2,1,0:T(8,128)S(1)}, f32[...) custom-call(s32[16,128]{1,0:T(8,128)} %mask_in.1, s32[16,128]{1,0:T(8,128)} %levels_in.1, ...), custom_call_target="tpu_custom_call" | custom-call | tf_op jit(solution)/shard_map/pack_columns/pallas_call | solution.py:530
  2.5 0.6 %collective-permute-start = (f32[5,16,128]{2,1,0:T(8,128)S(1)}, f32[5,16,128]{2,1,0:T(8,128)S(1)}, u32[]{:S(2)}, u32[]{:S(2)}) collective-permute-start(f32[5,16,128]{2,1,0:T(8,128)S(1)} %get-tuple-element.23.own_ref), channel_id=1, source_target_pairs={{0,4},{4,0},{8,12},{12,8},{16,20},{20,16},{24,28},{28,24},{1,5},{5... | collective-permute-start | bytes 122888 | tf_op jit(solution)/shard_map/ppermute | solution.py:551
  3.0 3.5 %collective-permute-start.1 = (f32[5,16,128]{2,1,0:T(8,128)S(1)}, f32[5,16,128]{2,1,0:T(8,128)S(1)}, u32[]{:S(2)}, u32[]{:S(2)}) collective-permute-start(f32[5,16,128]{2,1,0:T(8,128)S(1)} %get-tuple-element.23.own_ref), channel_id=1, source_target_pairs={{4,8},{8,4},{12,16},{16,12},{20,24},{24,20},{28,0},{0,28},{5,9},{9... | collective-permute-start | bytes 122888 | tf_op jit(solution)/shard_map/ppermute | solution.py:551
  6.6 0.1 pack_rows.1
  6.7 0.0 collective-permute-done.first_ref.refs_2_
  6.7 1.5 %collective-permute-done.1.second_ref.refs_3_ = f32[5,16,128]{2,1,0:T(8,128)S(1)} collective-permute-done((f32[5,16,128]{2,1,0:T(8,128)S(1)}, f32[5,16,128]{2,1,0:T(8,128)S(1)}, u32[]{:S(2)}, u32[]{:S(2)}) %collective-permute-start.1) | collective-permute-done | bytes 40992 | tf_op jit(solution)/shard_map/ppermute | solution.py:551
  8.3 0.4 %join_rows.1 = (f32[184,128]{1,0:T(8,128)S(1)}, f32[184,128]{1,0:T(8,128)S(1)}) custom-call(f32[16,128]{1,0:T(8,128)S(1)} %get-tuple-element.21.level_ref.refs_0_, f32[16,128]{1,0:T(8,128)S(1)} %get-tuple-element.22.eta_ref.refs_1_, f32[5,16,128]{2,1,0:T(8,128)S(1)} %get-tuple-element.23.own_ref, f32[5,16,128]{2,1,0:T(8,128)S(1)} %collective-permute-done.first_ref.refs_2_, ...), custom_call_target="tpu_custom_call" | custom-call | tf_op jit(solution)/shard_map/join_rows/pallas_call | solution.py:530
  8.7 0.7 %collective-permute-start.2 = (f32[184,128]{1,0:T(8,128)S(1)}, f32[184,128]{1,0:T(8,128)S(1)}, u32[]{:S(2)}, u32[]{:S(2)}) collective-permute-start(f32[184,128]{1,0:T(8,128)S(1)} %get-tuple-element.33), channel_id=1, source_target_pairs={{1,2},{2,1},{5,6},{6,5},{9,10},{10,9},{13,14},{14,13},{17,18},{18,... | collective-permute-start | bytes 282632 | tf_op jit(solution)/shard_map/ppermute | solution.py:551
  9.3 4.6 %collective-permute-start.3 = (f32[184,128]{1,0:T(8,128)S(1)}, f32[184,128]{1,0:T(8,128)S(1)}, u32[]{:S(2)}, u32[]{:S(2)}) collective-permute-start(f32[184,128]{1,0:T(8,128)S(1)} %get-tuple-element.34), channel_id=1, source_target_pairs={{0,1},{1,0},{2,3},{3,2},{4,5},{5,4},{6,7},{7,6},{8,9},{9,8},{10,11... | collective-permute-start | bytes 282632 | tf_op jit(solution)/shard_map/ppermute | solution.py:551
  13.9 0.0 collective-permute-done.2.refs_4_.first_row
  13.9 2.5 %collective-permute-done.3.refs_5_.second_row = f32[184,128]{1,0:T(8,128)S(1)} collective-permute-done((f32[184,128]{1,0:T(8,128)S(1)}, f32[184,128]{1,0:T(8,128)S(1)}, u32[]{:S(2)}, u32[]{:S(2)}) %collective-permute-start.3) | collective-permute-done | bytes 94240 | tf_op jit(solution)/shard_map/ppermute | solution.py:551
  16.5 1.1 %surface.1 = (f32[3,24,256]{2,1,0:T(8,128)S(1)}, f32[24,256]{1,0:T(8,128)S(1)}, f32[32,128]{1,0:T(8,128)}) custom-call(f32[16,128]{1,0:T(8,128)S(1)} %get-tuple-element.21.level_ref.refs_0_, f32[16,128]{1,0:T(8,128)S(1)} %get-tuple-element.22.eta_ref.refs_1_, f32[5,16,128]{2,1,0:T(8,128)S(1)} %collective-permute-done.first_ref.refs_2_, ...), custom_call_target="tpu_custom_call" | custom-call | tf_op jit(solution)/shard_map/surface/pallas_call | solution.py:530
  17.6 4.3 %all-to-all-start = ((f32[32,1,128]{2,1,0:T(1,128)}), f32[32,1,128]{2,1,0:T(1,128)S(1)}, u32[]{:S(2)}, u32[]{:S(2)}) async-start(f32[32,1,128]{2,1,0:T(1,128)} %bitcast.1), calls=%async_computation | async-start | bytes 32768 | tf_op jit(solution)/shard_map/all_to_all | solution.py:586
  21.9 3.3 %columns.1 = (f32[2,24,16,128]{3,2,1,0:T(8,128)S(1)}, f32[3,24,16,128]{3,2,1,0:T(8,128)S(1)}) custom-call(f32[2,24,16,128]{3,2,1,0:T(8,128)S(1)} %get-tuple-element.24.tracer_ref, f32[24,16,128]{2,1,0:T(8,128)S(1)} %get-tuple-element.25.u_ref, f32[24,16,128]{2,1,0:T(8,128)S(1)} %get-tuple-element.26.v_ref, f32[2,24,16,128]{3,2,1,0:T(8,128)S(1)} %get-tuple-element.27.bar_ref, ...), custom_call_target="tpu_custom_call" | custom-call | flops 19660800 | bytes 4194304 | tf_op jit(solution)/shard_map/columns/pallas_call | solution.py:530
  25.2 3.8 %all-to-all-done = f32[32,1,128]{2,1,0:T(1,128)S(1)} async-done(((f32[32,1,128]{2,1,0:T(1,128)}), f32[32,1,128]{2,1,0:T(1,128)S(1)}, u32[]{:S(2)}, u32[]{:S(2)}) %all-to-all-start) | async-done | bytes 16416 | tf_op jit(solution)/shard_map/all_to_all | solution.py:586
  29.0 1.0 %finish.1 = (f32[2,24,16,128]{3,2,1,0:T(8,128)}, f32[16,128]{1,0:T(8,128)}) custom-call(f32[32,128]{1,0:T(8,128)S(1)} %bitcast.4, f32[3,24,256]{2,1,0:T(8,128)S(1)} %get-tuple-element.36.basis_ref, f32[2,24,16,128]{3,2,1,0:T(8,128)S(1)} %get-tuple-element.38.base_ref, f32[3,24,16,128]{3,2,1,0:T(8,128)S(1)} %get-tuple-element.39.share_ref), custom_call_target="tpu_custom_call" | custom-call | tf_op jit(solution)/shard_map/finish/pallas_call | solution.py:530
Async XLA Ops:
  2.5 4.2 %collective-permute-start = (f32[5,16,128]{2,1,0:T(8,128)S(1)}, f32[5,16,128]{2,1,0:T(8,128)S(1)}, u32[]{:S(2)}, u32[]{:S(2)}) collective-permute-start(f32[5,16,128]{2,1,0:T(8,128)S(1)} %get-tuple-element.23.own_ref), channel_id=1, source_target_pairs={{0,4},{4,0},{8,12},{12,8},{16,20},{20,16},{24,28},{28,24},{1,5},{5... | collective-permute-start | bytes 122888 | tf_op jit(solution)/shard_map/ppermute | solution.py:551
  3.0 5.2 %collective-permute-start.1 = (f32[5,16,128]{2,1,0:T(8,128)S(1)}, f32[5,16,128]{2,1,0:T(8,128)S(1)}, u32[]{:S(2)}, u32[]{:S(2)}) collective-permute-start(f32[5,16,128]{2,1,0:T(8,128)S(1)} %get-tuple-element.23.own_ref), channel_id=1, source_target_pairs={{4,8},{8,4},{12,16},{16,12},{20,24},{24,20},{28,0},{0,28},{5,9},{9... | collective-permute-start | bytes 122888 | tf_op jit(solution)/shard_map/ppermute | solution.py:551
  8.7 5.3 %collective-permute-start.2 = (f32[184,128]{1,0:T(8,128)S(1)}, f32[184,128]{1,0:T(8,128)S(1)}, u32[]{:S(2)}, u32[]{:S(2)}) collective-permute-start(f32[184,128]{1,0:T(8,128)S(1)} %get-tuple-element.33), channel_id=1, source_target_pairs={{1,2},{2,1},{5,6},{6,5},{9,10},{10,9},{13,14},{14,13},{17,18},{18,... | collective-permute-start | bytes 282632 | tf_op jit(solution)/shard_map/ppermute | solution.py:551
  9.3 7.2 %collective-permute-start.3 = (f32[184,128]{1,0:T(8,128)S(1)}, f32[184,128]{1,0:T(8,128)S(1)}, u32[]{:S(2)}, u32[]{:S(2)}) collective-permute-start(f32[184,128]{1,0:T(8,128)S(1)} %get-tuple-element.34), channel_id=1, source_target_pairs={{0,1},{1,0},{2,3},{3,2},{4,5},{5,4},{6,7},{7,6},{8,9},{9,8},{10,11... | collective-permute-start | bytes 282632 | tf_op jit(solution)/shard_map/ppermute | solution.py:551
  17.6 11.4 %all-to-all-start = ((f32[32,1,128]{2,1,0:T(1,128)}), f32[32,1,128]{2,1,0:T(1,128)S(1)}, u32[]{:S(2)}, u32[]{:S(2)}) async-start(f32[32,1,128]{2,1,0:T(1,128)} %bitcast.1), calls=%async_computation | async-start | bytes 32768 | tf_op jit(solution)/shard_map/all_to_all | solution.py:586
